TPU v7x, 128 devices: a whole 4x4x4 slice. The times are simulated.
128 devices in a mesh: smp: 32 (over x, z, y_lo), col: 2 (over core), slab: 2 (over y_hi).
Axes of the slice: x: 4, y: 4 (y_hi: 2, y_lo: 2; y = y_hi * 2 + y_lo), z: 4, core: 2. Of those that a mesh axis runs over, the one named last changes fastest.
Arguments:
- jacobian: bfloat16 [1024, 32, 16384], P('smp', 'slab', 'col'), may hold values from -0.005722046 to 0.005722046
- local_energy: float32 [1024], P('smp'), may hold values from -6 to 6
Outputs:
- update: float32 [32, 16384], P('slab', ('col', 'smp'))
All inputs are finite; a program needn't handle non-finite values.
Results may differ from a plain program's by a relative error of at most 0.0085.
Values may be sent and summed in bfloat16 or wider, within the bound.
A program may use at most 192 MiB of HBM per device.

v0:
```python
import jax
import jax.numpy as jnp
from jax import lax
from jax.sharding import PartitionSpec as P

SLABS = 32
SLAB_COLS = 16384


def shards(jacobian, local_energy):
    energies = lax.all_gather(local_energy, "smp", axis=0, tiled=True)
    samples = energies.shape[0]
    root_count = jnp.sqrt(jnp.float32(samples))
    eps = (energies - jnp.mean(energies)) / root_count
    columns = lax.all_to_all(jacobian, "smp", split_axis=2, concat_axis=0, tiled=True)
    slab_count = columns.shape[1]
    width = columns.shape[2]
    values = columns.astype(jnp.float32)
    mean_row = jnp.mean(values, axis=0, keepdims=True)
    centered = (
        ((values - mean_row) / root_count).astype(jnp.bfloat16).reshape(samples, slab_count * width)
    )
    partial_gram = jnp.dot(centered, centered.T, preferred_element_type=jnp.float32)
    gram = lax.psum(partial_gram, ("smp", "col", "slab"))
    shift = 0.01 * jnp.trace(gram) / samples
    factor = jnp.linalg.cholesky(gram + shift * jnp.eye(samples, dtype=jnp.float32))
    middle = lax.linalg.triangular_solve(factor, eps[:, None], left_side=True, lower=True)
    coeffs = lax.linalg.triangular_solve(
        factor, middle, left_side=True, lower=True, transpose_a=True
    )[:, 0]
    delta = jnp.dot(coeffs, centered.astype(jnp.float32), precision=lax.Precision.HIGHEST)
    squared = lax.psum(jnp.sum(delta * delta), ("smp", "col", "slab"))
    limit = 0.3 * jnp.sqrt(jnp.float32(SLABS * SLAB_COLS))
    scaled = -jnp.minimum(1.0, limit / jnp.sqrt(squared)) * delta
    return scaled.reshape(slab_count, width)


def solution(mesh):
    in_specs = (P("smp", "slab", "col"), P("smp"))
    out_specs = P("slab", ("col", "smp"))
    return jax.shard_map(shards, mesh=mesh, in_specs=in_specs, out_specs=out_specs, check_vma=False)
```

profile of v0, /device:TPU:8, one launch (start us, length us, event | category | flops | bytes accessed | tf_op | source)
XLA Modules:
  0.0 895.7 jit_solution(18186082243385075913)
XLA Ops:
  6.5 45.6 %copy.65 = bf16[32,16,8192]{0,1,2:T(8,128)(2,1)} copy(bf16[32,16,8192]{2,1,0:T(8,128)(2,1)} %param.2) | data formatting | bytes 16777216 | tf_op args[0]
  52.1 39.8 %reshape.341 = bf16[32,2,65536]{2,1,0:T(2,128)(2,1)} reshape(bf16[8192,16,32]{2,1,0:T(8,128)(2,1)} %bitcast.340) | data formatting | bytes 16777216
  91.9 105.2 %all_to_all.4 = bf16[32,2,65536]{2,1,0:T(2,128)(2,1)} all-to-all(bf16[32,2,65536]{2,1,0:T(2,128)(2,1)} %reshape.341), channel_id=1, replica_groups=mesh['smp'=32,'col'=2,'slab'=2] {'smp'}, dimensions={0} | all-to-all | bytes 16777216 | tf_op jit(solution)/shard_map/all_to_all | solution.py:15
  197.1 30.6 %reshape.342 = bf16[8192,16,32]{2,1,0:T(8,128)(2,1)} reshape(bf16[32,2,65536]{2,1,0:T(2,128)(2,1)} %all_to_all.4) | data formatting | bytes 16777216
  227.7 44.0 %copy.66 = f32[32,16,32,256]{3,1,0,2:T(8,128)} copy(bf16[32,16,32,256]{0,1,3,2:T(8,128)(2,1)} %bitcast.339) | data formatting | bytes 25165824 | tf_op jit(solution)/shard_map/convert_element_type | solution.py:18
  271.7 6.9 bitcast_reduce_fusion
  278.6 7.2 fusion.1
  289.0 16.6 %fusion.5 = f32[1024,1024]{0,1:T(8,128)} fusion(bf16[1024,16,256]{2,1,0:T(8,128)(2,1)S(1)} %bitcast.342), kind=kOutput, calls=%fused_computation.15 | convolution fusion | flops 8589934592 | bytes 12582912 | tf_op jit(solution)/shard_map/dot_general | solution.py:23
  307.9 78.4 %all-reduce.1 = f32[1024]{0:T(1024)S(1)} all-reduce(f32[1024]{0:T(1024)S(1)} %dynamic-update-slice.47), channel_id=1, replica_groups=mesh['smp'=32,'col'=2,'slab'=2] {'smp'}, use_global_device_ids=true, to_apply=%add.1 | all-reduce | flops 1024 | bytes 8192
  387.7 12.3 %copy.96 = bf16[128,8,16,256]{3,1,2,0:T(8,128)(2,1)} copy(bf16[128,8,16,256]{3,2,1,0:T(8,128)(2,1)} %bitcast.343) | data formatting | bytes 16777216
  400.0 59.6 %all-reduce.4.cloned.1.call-done = f32[1024,1024]{0,1:T(8,128)} async-done(((f32[1024,1024]{0,1:T(8,128)}), f32[1024,1024]{0,1:T(8,128)}) %all-reduce.4.cloned.1.call-update) | async-done | bytes 4194320 | tf_op jit(solution)/shard_map/psum | solution.py:24
  467.9 5.5 copy.70
  479.9 11.7 %cholesky.222 = f32[128,128]{1,0:T(8,128)S(1)} custom-call(f32[128,128]{1,0:T(8,128)S(1)} %cholesky.577), custom_call_target="Cholesky" | custom-call | tf_op jit(solution)/shard_map/jit(cholesky)/cholesky | solution.py:26
  491.7 9.8 %custom-call.64 = f32[1,128,128]{1,2,0:T(8,128)S(1)} custom-call(f32[1,128,128]{2,1,0:T(8,128)S(1)} %get-tuple-element.52), custom_call_target="InvertDiagBlocksLowerTriangular" | custom-call | tf_op jit(solution)/shard_map/jit(cholesky)/cholesky | solution.py:26
  504.6 11.7 %cholesky.243 = f32[128,128]{1,0:T(8,128)S(1)} custom-call(f32[128,128]{1,0:T(8,128)S(1)} %cholesky.581), custom_call_target="Cholesky" | custom-call | tf_op jit(solution)/shard_map/jit(cholesky)/cholesky | solution.py:26
  519.6 9.8 %custom-call.65 = f32[1,128,128]{1,2,0:T(8,128)S(1)} custom-call(f32[1,128,128]{2,1,0:T(8,128)S(1)} %get-tuple-element.50), custom_call_target="InvertDiagBlocksLowerTriangular" | custom-call | tf_op jit(solution)/shard_map/jit(cholesky)/cholesky | solution.py:26
  535.0 11.7 %cholesky.466 = f32[128,128]{1,0:T(8,128)S(1)} custom-call(f32[128,128]{1,0:T(8,128)S(1)} %cholesky.586), custom_call_target="Cholesky" | custom-call | tf_op jit(solution)/shard_map/jit(cholesky)/cholesky | solution.py:26
  547.5 9.8 %custom-call.66 = f32[1,128,128]{1,2,0:T(8,128)S(1)} custom-call(f32[1,128,128]{2,1,0:T(8,128)S(1)} %get-tuple-element.48), custom_call_target="InvertDiagBlocksLowerTriangular" | custom-call | tf_op jit(solution)/shard_map/jit(cholesky)/cholesky | solution.py:26
  561.8 11.7 %cholesky.485 = f32[128,128]{1,0:T(8,128)S(1)} custom-call(f32[128,128]{1,0:T(8,128)S(1)} %cholesky.591), custom_call_target="Cholesky" | custom-call | tf_op jit(solution)/shard_map/jit(cholesky)/cholesky | solution.py:26
  574.3 9.8 %custom-call.67 = f32[1,128,128]{1,2,0:T(8,128)S(1)} custom-call(f32[1,128,128]{2,1,0:T(8,128)S(1)} %get-tuple-element.46), custom_call_target="InvertDiagBlocksLowerTriangular" | custom-call | tf_op jit(solution)/shard_map/jit(cholesky)/cholesky | solution.py:26
  588.4 11.9 %cholesky.504 = f32[128,128]{1,0:T(8,128)S(1)} custom-call(f32[128,128]{1,0:T(8,128)S(1)} %cholesky.596), custom_call_target="Cholesky" | custom-call | tf_op jit(solution)/shard_map/jit(cholesky)/cholesky | solution.py:26
  601.1 9.8 %custom-call.68 = f32[1,128,128]{1,2,0:T(8,128)S(1)} custom-call(f32[1,128,128]{2,1,0:T(8,128)S(1)} %get-tuple-element.44), custom_call_target="InvertDiagBlocksLowerTriangular" | custom-call | tf_op jit(solution)/shard_map/jit(cholesky)/cholesky | solution.py:26
  615.1 11.7 %cholesky.524 = f32[128,128]{1,0:T(8,128)S(1)} custom-call(f32[128,128]{1,0:T(8,128)S(1)} %cholesky.601), custom_call_target="Cholesky" | custom-call | tf_op jit(solution)/shard_map/jit(cholesky)/cholesky | solution.py:26
  627.6 9.8 %custom-call.69 = f32[1,128,128]{1,2,0:T(8,128)S(1)} custom-call(f32[1,128,128]{2,1,0:T(8,128)S(1)} %get-tuple-element.42), custom_call_target="InvertDiagBlocksLowerTriangular" | custom-call | tf_op jit(solution)/shard_map/jit(cholesky)/cholesky | solution.py:26
  641.5 11.7 %cholesky.544 = f32[128,128]{1,0:T(8,128)S(1)} custom-call(f32[128,128]{1,0:T(8,128)S(1)} %cholesky.606), custom_call_target="Cholesky" | custom-call | tf_op jit(solution)/shard_map/jit(cholesky)/cholesky | solution.py:26
  654.0 9.8 %custom-call.70 = f32[1,128,128]{1,2,0:T(8,128)S(1)} custom-call(f32[1,128,128]{2,1,0:T(8,128)S(1)} %get-tuple-element.40), custom_call_target="InvertDiagBlocksLowerTriangular" | custom-call | tf_op jit(solution)/shard_map/jit(cholesky)/cholesky | solution.py:26
  666.8 11.7 %cholesky.562 = f32[128,128]{1,0:T(8,128)S(1)} custom-call(f32[128,128]{1,0:T(8,128)S(1)} %convolution_subtract_fusion.6), custom_call_target="Cholesky" | custom-call | tf_op jit(solution)/shard_map/jit(cholesky)/cholesky | solution.py:26
  688.7 4.9 select_select_fusion
  693.6 24.5 %while.1 = (s32[]{:T(128)}, f32[1024,1024]{0,1:T(8,128)}, s32[8,2]{0,1:T(2,128)S(1)}, f32[8,128,128]{2,1,0:T(8,128)S(1)}, s32[]{:T(128)}) while((s32[]{:T(128)}, f32[1024,1024]{0,1:T(8,128)}, s32[8,2]{0,1:T(2,128)S(1)}, f32[8,128,128]{2,1,0:T(8,128)S(1)}, s32[]{:T(128)}) %tuple.52), condition=%wide.while_cond, body=%wide.while_body.sunk | while | flops 2 | bytes 393321 | solution.py:28
  718.1 78.8 %custom-call.71 = f32[8,128,128]{1,2,0:T(8,128)S(1)} custom-call(f32[8,128,128]{2,1,0:T(8,128)S(1)} %get-tuple-element.12), custom_call_target="InvertDiagBlocksLowerTriangular" | custom-call | tf_op jit(solution)/shard_map/triangular_solve | solution.py:28
  817.8 5.7 fusion.125
  824.1 63.3 %psum.15 = f32[]{:T(128)} all-reduce(f32[]{:T(128)} %multiply_reduce_fusion), channel_id=1, replica_groups=mesh['smp'=32,'col'=2,'slab'=2] {'smp','col','slab'}, use_global_device_ids=true, to_apply=%region_21.22 | all-reduce | flops 1 | bytes 8 | tf_op jit(solution)/shard_map/psum | solution.py:32
  (171 shorter events, 107.1 us)
Async XLA Ops:
  6.5 453.1 %all-reduce.4.cloned.1.call-start = ((), (), s32[]{:S(2)}) async-start(), calls=%async_computation.1 | async-start | bytes 8388608 | tf_op jit(solution)/shard_map/psum | solution.py:24
  285.8 3.2 copy-start
  305.6 0.7 copy-start.3
  305.6 2.0 copy-start.2
  477.9 2.0 copy-start.1
Sparse Core Ops, SparseCore 0:
  305.8 153.8 all-reduce.3
where the time goes:
time: 904 us; the launch traced here: 896 us
  other arithmetic  279 us (31%)
  blocking collectives  247 us (27%)
  local copies, waits for them, and re-layouts  219 us (24%)
  matrix products  70 us (8%)
  waiting for transfers between devices  59.6 us (7%)
  between operations  21.6 us (2%)
    another operation x30, other arithmetic, shards(): jnp.linalg.cholesky(gram + shift * jnp.eye(samples, dtype=jnp.float32))  167 us
    unnamed x33, local copies, waits for them, and re-layouts  135 us
    all_to_all x1, blocking collectives, shards(): lax.all_to_all(jacobian, 'smp', split_axis=2, concat_axis=0, tiled=True)  105 us
    another operation x3, other arithmetic, shards(): lax.linalg.triangular_solve(factor, middle, left_side=True, lower=True, t...  83.6 us
    unnamed x1, blocking collectives  78.4 us
    psum x1, blocking collectives, shards(): squared = lax.psum(jnp.sum(delta * delta), ('smp', 'col', 'slab'))  63.3 us
    psum x1, waiting for transfers between devices, shards(): gram = lax.psum(partial_gram, ('smp', 'col', 'slab'))  59.6 us
    convert_element_type x1, local copies, waits for them, and re-layouts, shards(): values = columns.astype(jnp.float32)  44 us
  transfers between devices with their start and end apart: 1, of which 1 were waited for; matrix products, arithmetic and copies ran while one was open for 2% of the time, Pallas kernels for 0%

commit v1 on v0

--- a/solution.py
+++ b/solution.py
@@ -9,6 +9,7 @@
 
 def shards(jacobian, local_energy):
     energies = lax.all_gather(local_energy, "smp", axis=0, tiled=True)
+    jacobian, energies = lax.optimization_barrier((jacobian, energies))
     samples = energies.shape[0]
     root_count = jnp.sqrt(jnp.float32(samples))
     eps = (energies - jnp.mean(energies)) / root_count
@@ -29,7 +30,8 @@
         factor, middle, left_side=True, lower=True, transpose_a=True
     )[:, 0]
     delta = jnp.dot(coeffs, centered.astype(jnp.float32), precision=lax.Precision.HIGHEST)
-    squared = lax.psum(jnp.sum(delta * delta), ("smp", "col", "slab"))
+    squared = jnp.dot(coeffs, jnp.dot(gram, coeffs, precision=lax.Precision.HIGHEST),
+                      precision=lax.Precision.HIGHEST)
     limit = 0.3 * jnp.sqrt(jnp.float32(SLABS * SLAB_COLS))
     scaled = -jnp.minimum(1.0, limit / jnp.sqrt(squared)) * delta
     return scaled.reshape(slab_count, width)

time: 904 us -> 912 us (level)
  waiting for transfers between devices: 59.6 us -> 140 us
  blocking collectives: 247 us -> 171 us
    psum x1, waiting for transfers between devices: 59.6 us -> 140 us  [shards(): gram = lax.psum(partial_gram, ('smp', 'col', 'slab'))]
    optimization_barrier x0 -> x1, blocking collectives: none -> 78.7 us  [shards(): jacobian, energies = lax.optimization_barrier((jacobian, energies))]
    unnamed x1 -> x0, blocking collectives: 78.4 us -> none
    psum x1 -> x0, blocking collectives: 63.3 us -> none  [shards(): squared = lax.psum(jnp.sum(delta * delta), ('smp', 'col', 'slab'))]
    optimization_barrier x0 -> x1, local copies, waits for them, and re-layouts: none -> 45.6 us  [shards(): jacobian, energies = lax.optimization_barrier((jacobian, energies))]
    unnamed x33 -> x30, local copies, waits for them, and re-layouts: 135 us -> 90.2 us
    all_to_all x1, blocking collectives: 105 us -> 92.8 us  [shards(): lax.all_to_all(jacobian, 'smp', split_axis=2, concat_axis=0, tiled=True)]
  transfers between devices with their start and end apart: 1 -> 1, of which waited for: 1 -> 1; matrix products, arithmetic and copies ran while one was open for 2% -> 1% of each run, Pallas kernels for 0% -> 0%
where the time goes in v1:
time: 912 us; the launch traced here: 904 us
  other arithmetic  279 us (31%)
  local copies, waits for them, and re-layouts  219 us (24%)
  blocking collectives  171 us (19%)
  waiting for transfers between devices  140 us (15%)
  matrix products  72.4 us (8%)
  between operations  21.5 us (2%)
    another operation x30, other arithmetic, shards(): jnp.linalg.cholesky(gram + shift * jnp.eye(samples, dtype=jnp.float32))  168 us
    psum x1, waiting for transfers between devices, shards(): gram = lax.psum(partial_gram, ('smp', 'col', 'slab'))  140 us
    all_to_all x1, blocking collectives, shards(): lax.all_to_all(jacobian, 'smp', split_axis=2, concat_axis=0, tiled=True)  92.8 us
    unnamed x30, local copies, waits for them, and re-layouts  90.2 us
    another operation x3, other arithmetic, shards(): lax.linalg.triangular_solve(factor, middle, left_side=True, lower=True, t...  83.7 us
    optimization_barrier x1, blocking collectives, shards(): jacobian, energies = lax.optimization_barrier((jacobian, energies))  78.7 us
    optimization_barrier x1, local copies, waits for them, and re-layouts, shards(): jacobian, energies = lax.optimization_barrier((jacobian, energies))  45.6 us
    convert_element_type x1, local copies, waits for them, and re-layouts, shards(): values = columns.astype(jnp.float32)  44 us
  transfers between devices with their start and end apart: 1, of which 1 were waited for; matrix products, arithmetic and copies ran while one was open for 1% of the time, Pallas kernels for 0%

profile of v1, /device:TPU:8, one launch (start us, length us, event | category | flops | bytes accessed | tf_op | source)
XLA Modules:
  0.0 904.4 jit_solution(12480278940735346125)
XLA Ops:
  9.3 78.7 %all-reduce.1 = f32[1024]{0:T(1024)S(1)} all-reduce(f32[1024]{0:T(1024)S(1)} %dynamic-update-slice.47), channel_id=1, replica_groups=mesh['smp'=32,'col'=2,'slab'=2] {'smp'}, use_global_device_ids=true, to_apply=%add.1 | all-reduce | flops 1024 | bytes 8192 | tf_op jit(solution)/shard_map/optimization_barrier | solution.py:12
  88.0 45.6 %copy.65 = bf16[32,16,8192]{0,1,2:T(8,128)(2,1)} copy(bf16[32,16,8192]{2,1,0:T(8,128)(2,1)} %param.2) | data formatting | bytes 16777216 | tf_op jit(solution)/shard_map/optimization_barrier | solution.py:12
  133.6 39.8 %reshape.346 = bf16[32,2,65536]{2,1,0:T(2,128)(2,1)} reshape(bf16[8192,16,32]{2,1,0:T(8,128)(2,1)} %bitcast.343) | data formatting | bytes 16777216
  173.4 92.8 %all_to_all.4 = bf16[32,2,65536]{2,1,0:T(2,128)(2,1)} all-to-all(bf16[32,2,65536]{2,1,0:T(2,128)(2,1)} %reshape.346), channel_id=1, replica_groups=mesh['smp'=32,'col'=2,'slab'=2] {'smp'}, dimensions={0} | all-to-all | bytes 16777216 | tf_op jit(solution)/shard_map/all_to_all | solution.py:16
  266.1 30.6 %reshape.347 = bf16[8192,16,32]{2,1,0:T(8,128)(2,1)} reshape(bf16[32,2,65536]{2,1,0:T(2,128)(2,1)} %all_to_all.4) | data formatting | bytes 16777216
  296.8 44.0 %copy.66 = f32[32,16,32,256]{3,1,0,2:T(8,128)} copy(bf16[32,16,32,256]{0,1,3,2:T(8,128)(2,1)} %bitcast.342) | data formatting | bytes 25165824 | tf_op jit(solution)/shard_map/convert_element_type | solution.py:19
  340.8 6.9 bitcast_reduce_fusion
  347.7 7.2 fusion.1
  358.1 16.8 %fusion.5 = f32[1024,1024]{0,1:T(8,128)} fusion(bf16[1024,16,256]{2,1,0:T(8,128)(2,1)S(1)} %bitcast.345), kind=kOutput, calls=%fused_computation.15 | convolution fusion | flops 8589934592 | bytes 12582912 | tf_op jit(solution)/shard_map/dot_general | solution.py:24
  376.3 12.2 %copy.98 = bf16[128,8,16,256]{3,1,2,0:T(8,128)(2,1)} copy(bf16[128,8,16,256]{3,2,1,0:T(8,128)(2,1)} %bitcast.346) | data formatting | bytes 16777216
  388.6 140.5 %all-reduce.4.cloned.1.call-done = f32[1024,1024]{0,1:T(8,128)} async-done(((f32[1024,1024]{0,1:T(8,128)}), f32[1024,1024]{0,1:T(8,128)}) %all-reduce.4.cloned.1.call-update) | async-done | bytes 4194320 | tf_op jit(solution)/shard_map/psum | solution.py:25
  532.5 4.8 select_add_fusion
  537.4 5.7 copy.70
  549.6 11.7 %cholesky.222 = f32[128,128]{1,0:T(8,128)S(1)} custom-call(f32[128,128]{1,0:T(8,128)S(1)} %cholesky.577), custom_call_target="Cholesky" | custom-call | tf_op jit(solution)/shard_map/jit(cholesky)/cholesky | solution.py:27
  561.3 9.8 %custom-call.64 = f32[1,128,128]{1,2,0:T(8,128)S(1)} custom-call(f32[1,128,128]{2,1,0:T(8,128)S(1)} %get-tuple-element.56), custom_call_target="InvertDiagBlocksLowerTriangular" | custom-call | tf_op jit(solution)/shard_map/jit(cholesky)/cholesky | solution.py:27
  574.3 11.7 %cholesky.243 = f32[128,128]{1,0:T(8,128)S(1)} custom-call(f32[128,128]{1,0:T(8,128)S(1)} %cholesky.581), custom_call_target="Cholesky" | custom-call | tf_op jit(solution)/shard_map/jit(cholesky)/cholesky | solution.py:27
  589.1 9.8 %custom-call.65 = f32[1,128,128]{1,2,0:T(8,128)S(1)} custom-call(f32[1,128,128]{2,1,0:T(8,128)S(1)} %get-tuple-element.54), custom_call_target="InvertDiagBlocksLowerTriangular" | custom-call | tf_op jit(solution)/shard_map/jit(cholesky)/cholesky | solution.py:27
  604.4 11.7 %cholesky.466 = f32[128,128]{1,0:T(8,128)S(1)} custom-call(f32[128,128]{1,0:T(8,128)S(1)} %cholesky.586), custom_call_target="Cholesky" | custom-call | tf_op jit(solution)/shard_map/jit(cholesky)/cholesky | solution.py:27
  616.9 9.8 %custom-call.66 = f32[1,128,128]{1,2,0:T(8,128)S(1)} custom-call(f32[1,128,128]{2,1,0:T(8,128)S(1)} %get-tuple-element.52), custom_call_target="InvertDiagBlocksLowerTriangular" | custom-call | tf_op jit(solution)/shard_map/jit(cholesky)/cholesky | solution.py:27
  631.3 11.7 %cholesky.485 = f32[128,128]{1,0:T(8,128)S(1)} custom-call(f32[128,128]{1,0:T(8,128)S(1)} %cholesky.591), custom_call_target="Cholesky" | custom-call | tf_op jit(solution)/shard_map/jit(cholesky)/cholesky | solution.py:27
  643.8 9.8 %custom-call.67 = f32[1,128,128]{1,2,0:T(8,128)S(1)} custom-call(f32[1,128,128]{2,1,0:T(8,128)S(1)} %get-tuple-element.50), custom_call_target="InvertDiagBlocksLowerTriangular" | custom-call | tf_op jit(solution)/shard_map/jit(cholesky)/cholesky | solution.py:27
  657.9 12.1 %cholesky.504 = f32[128,128]{1,0:T(8,128)S(1)} custom-call(f32[128,128]{1,0:T(8,128)S(1)} %cholesky.596), custom_call_target="Cholesky" | custom-call | tf_op jit(solution)/shard_map/jit(cholesky)/cholesky | solution.py:27
  670.8 9.8 %custom-call.68 = f32[1,128,128]{1,2,0:T(8,128)S(1)} custom-call(f32[1,128,128]{2,1,0:T(8,128)S(1)} %get-tuple-element.48), custom_call_target="InvertDiagBlocksLowerTriangular" | custom-call | tf_op jit(solution)/shard_map/jit(cholesky)/cholesky | solution.py:27
  684.8 11.7 %cholesky.524 = f32[128,128]{1,0:T(8,128)S(1)} custom-call(f32[128,128]{1,0:T(8,128)S(1)} %cholesky.601), custom_call_target="Cholesky" | custom-call | tf_op jit(solution)/shard_map/jit(cholesky)/cholesky | solution.py:27
  697.3 9.8 %custom-call.69 = f32[1,128,128]{1,2,0:T(8,128)S(1)} custom-call(f32[1,128,128]{2,1,0:T(8,128)S(1)} %get-tuple-element.46), custom_call_target="InvertDiagBlocksLowerTriangular" | custom-call | tf_op jit(solution)/shard_map/jit(cholesky)/cholesky | solution.py:27
  710.9 11.7 %cholesky.544 = f32[128,128]{1,0:T(8,128)S(1)} custom-call(f32[128,128]{1,0:T(8,128)S(1)} %cholesky.606), custom_call_target="Cholesky" | custom-call | tf_op jit(solution)/shard_map/jit(cholesky)/cholesky | solution.py:27
  723.4 9.8 %custom-call.70 = f32[1,128,128]{1,2,0:T(8,128)S(1)} custom-call(f32[1,128,128]{2,1,0:T(8,128)S(1)} %get-tuple-element.44), custom_call_target="InvertDiagBlocksLowerTriangular" | custom-call | tf_op jit(solution)/shard_map/jit(cholesky)/cholesky | solution.py:27
  736.3 11.7 %cholesky.562 = f32[128,128]{1,0:T(8,128)S(1)} custom-call(f32[128,128]{1,0:T(8,128)S(1)} %convolution_subtract_fusion.6), custom_call_target="Cholesky" | custom-call | tf_op jit(solution)/shard_map/jit(cholesky)/cholesky | solution.py:27
  758.1 4.9 select_select_fusion
  763.0 24.5 %while.1 = (s32[]{:T(128)}, f32[1024,1024]{0,1:T(8,128)}, s32[8,2]{0,1:T(2,128)S(1)}, f32[8,128,128]{2,1,0:T(8,128)S(1)}, s32[]{:T(128)}) while((s32[]{:T(128)}, f32[1024,1024]{0,1:T(8,128)}, s32[8,2]{0,1:T(2,128)S(1)}, f32[8,128,128]{2,1,0:T(8,128)S(1)}, s32[]{:T(128)}) %tuple.54), condition=%wide.while_cond, body=%wide.while_body.sunk | while | flops 2 | bytes 393321 | solution.py:29
  787.5 78.8 %custom-call.71 = f32[8,128,128]{1,2,0:T(8,128)S(1)} custom-call(f32[8,128,128]{2,1,0:T(8,128)S(1)} %get-tuple-element.16), custom_call_target="InvertDiagBlocksLowerTriangular" | custom-call | tf_op jit(solution)/shard_map/triangular_solve | solution.py:29
  891.0 5.7 fusion.126
  (169 shorter events, 104.9 us)
Async XLA Ops:
  6.5 522.5 %all-reduce.4.cloned.1.call-start = ((), (), s32[]{:S(2)}) async-start(), calls=%async_computation.1 | async-start | bytes 8388608 | tf_op jit(solution)/shard_map/psum | solution.py:25
  354.9 3.2 copy-start.1
  547.6 2.0 copy-start.2
  866.3 21.1 %copy-start = (f32[1024,1024]{0,1:T(8,128)S(1)}, f32[1024,1024]{0,1:T(8,128)}, u32[]{:S(2)}) copy-start(f32[1024,1024]{0,1:T(8,128)} %all-reduce.4.cloned.1.call-done) | copy-start | bytes 12582916
Sparse Core Ops, SparseCore 0:
  375.1 153.9 all-reduce.3

commit v2 on v1

--- a/solution.py
+++ b/solution.py
@@ -1,19 +1,92 @@
+import functools
+
 import jax
 import jax.numpy as jnp
 from jax import lax
+from jax.experimental import pallas as pl
+from jax.experimental.pallas import tpu as pltpu
 from jax.sharding import PartitionSpec as P
 
 SLABS = 32
 SLAB_COLS = 16384
 
 
-def shards(jacobian, local_energy):
-    energies = lax.all_gather(local_energy, "smp", axis=0, tiled=True)
-    jacobian, energies = lax.optimization_barrier((jacobian, energies))
+def exchange_kernel(n, width, jac_ref, en_ref, cols_ref, en_all_ref,
+                    send_sems, recv_sems, en_send, en_recv, local_sems):
+    me = lax.axis_index("smp")
+    col = lax.axis_index("col")
+    slab = lax.axis_index("slab")
+
+    def piece(t):
+        return jac_ref.at[:, :, pl.ds(pl.multiple_of(t * width, width), width)]
+
+    local = pltpu.make_async_copy(piece(me), cols_ref.at[me], local_sems.at[0])
+    local.start()
+    local_en = pltpu.make_async_copy(en_ref, en_all_ref.at[me], local_sems.at[1])
+    local_en.start()
+    sends = []
+    for k in range(1, n):
+        t = lax.rem(me + k, n)
+        dev = (t, col, slab)
+        c = pltpu.make_async_remote_copy(
+            src_ref=piece(t), dst_ref=cols_ref.at[me],
+            send_sem=send_sems.at[t], recv_sem=recv_sems.at[me],
+            device_id=dev, device_id_type=pl.DeviceIdType.MESH)
+        c.start()
+        e = pltpu.make_async_remote_copy(
+            src_ref=en_ref, dst_ref=en_all_ref.at[me],
+            send_sem=en_send.at[t], recv_sem=en_recv.at[me],
+            device_id=dev, device_id_type=pl.DeviceIdType.MESH)
+        e.start()
+        sends.append((c, e))
+    for k in range(1, n):
+        s = lax.rem(me + n - k, n)
+        dev = (s, col, slab)
+        pltpu.make_async_remote_copy(
+            src_ref=piece(me), dst_ref=cols_ref.at[s],
+            send_sem=send_sems.at[s], recv_sem=recv_sems.at[s],
+            device_id=dev, device_id_type=pl.DeviceIdType.MESH).wait_recv()
+        pltpu.make_async_remote_copy(
+            src_ref=en_ref, dst_ref=en_all_ref.at[s],
+            send_sem=en_send.at[s], recv_sem=en_recv.at[s],
+            device_id=dev, device_id_type=pl.DeviceIdType.MESH).wait_recv()
+    for c, e in sends:
+        c.wait_send()
+        e.wait_send()
+    local.wait()
+    local_en.wait()
+
+
+def exchange(jacobian, local_energy, n):
+    rows, slabs, cols = jacobian.shape
+    width = cols // n
+    en = local_energy.reshape(1, rows)
+    return pl.pallas_call(
+        functools.partial(exchange_kernel, n, width),
+        out_shape=(
+            jax.ShapeDtypeStruct((n, rows, slabs, width), jacobian.dtype),
+            jax.ShapeDtypeStruct((n, 1, rows), local_energy.dtype),
+        ),
+        in_specs=[pl.BlockSpec(memory_space=pl.ANY)] * 2,
+        out_specs=(pl.BlockSpec(memory_space=pl.ANY), pl.BlockSpec(memory_space=pl.ANY)),
+        scratch_shapes=[
+            pltpu.SemaphoreType.DMA((n,)),
+            pltpu.SemaphoreType.DMA((n,)),
+            pltpu.SemaphoreType.DMA((n,)),
+            pltpu.SemaphoreType.DMA((n,)),
+            pltpu.SemaphoreType.DMA((2,)),
+        ],
+        compiler_params=pltpu.CompilerParams(has_side_effects=True),
+    )(jacobian, en)
+
+
+def shards(n, jacobian, local_energy):
+    gathered, energies = exchange(jacobian, local_energy, n)
+    energies = energies.reshape(-1)
     samples = energies.shape[0]
     root_count = jnp.sqrt(jnp.float32(samples))
     eps = (energies - jnp.mean(energies)) / root_count
-    columns = lax.all_to_all(jacobian, "smp", split_axis=2, concat_axis=0, tiled=True)
+    columns = gathered.reshape(samples, gathered.shape[2], gathered.shape[3])
     slab_count = columns.shape[1]
     width = columns.shape[2]
     values = columns.astype(jnp.float32)
@@ -40,4 +113,5 @@
 def solution(mesh):
     in_specs = (P("smp", "slab", "col"), P("smp"))
     out_specs = P("slab", ("col", "smp"))
-    return jax.shard_map(shards, mesh=mesh, in_specs=in_specs, out_specs=out_specs, check_vma=False)
+    return jax.shard_map(functools.partial(shards, mesh.shape["smp"]), mesh=mesh,
+                         in_specs=in_specs, out_specs=out_specs, check_vma=False)

time: 912 us -> 802 us (0.88)
  Pallas kernels: 0 us -> 186 us
  blocking collectives: 171 us -> 0 us
  local copies, waits for them, and re-layouts: 219 us -> 55.5 us
  waiting for transfers between devices: 140 us -> 176 us
    pallas_call x0 -> x1, Pallas kernels: none -> 186 us  [exchange(): pl.pallas_call(functools.partial(exchange_kernel, n, width), out_shape=(j...]
    all_to_all x1 -> x0, blocking collectives: 92.8 us -> none  [shards(): lax.all_to_all(jacobian, 'smp', split_axis=2, concat_axis=0, tiled=True)]
    optimization_barrier x1 -> x0, blocking collectives: 78.7 us -> none  [shards(): jacobian, energies = lax.optimization_barrier((jacobian, energies))]
    unnamed x30 -> x25, local copies, waits for them, and re-layouts: 90.2 us -> 15.2 us
    optimization_barrier x1 -> x0, local copies, waits for them, and re-layouts: 45.6 us -> none  [shards(): jacobian, energies = lax.optimization_barrier((jacobian, energies))]
    convert_element_type x1 -> x0, local copies, waits for them, and re-layouts: 44 us -> none  [shards(): values = columns.astype(jnp.float32)]
    psum x1, waiting for transfers between devices: 140 us -> 176 us  [shards(): gram = lax.psum(partial_gram, ('smp', 'col', 'slab'))]
    another operation x40 -> x49, local copies, waits for them, and re-layouts: 24.2 us -> 24.9 us
  transfers between devices with their start and end apart: 1 -> 1, of which waited for: 1 -> 1; matrix products, arithmetic and copies ran while one was open for 1% -> 2% of each run, Pallas kernels for 0% -> 0%
where the time goes in v2:
time: 802 us; the launch traced here: 796 us
  other arithmetic  278 us (35%)
  Pallas kernels  186 us (23%)
  waiting for transfers between devices  176 us (22%)
  matrix products  79.9 us (10%)
  local copies, waits for them, and re-layouts  55.5 us (7%)
  between operations  20.8 us (3%)
    pallas_call x1, Pallas kernels, exchange(): pl.pallas_call(functools.partial(exchange_kernel, n, width), out_shape=(j...  186 us
    psum x1, waiting for transfers between devices, shards(): gram = lax.psum(partial_gram, ('smp', 'col', 'slab'))  176 us
    another operation x30, other arithmetic, shards(): jnp.linalg.cholesky(gram + shift * jnp.eye(samples, dtype=jnp.float32))  167 us
    another operation x3, other arithmetic, shards(): lax.linalg.triangular_solve(factor, middle, left_side=True, lower=True, t...  83.6 us
    another operation x14, matrix products, shards(): jnp.linalg.cholesky(gram + shift * jnp.eye(samples, dtype=jnp.float32))  27.2 us
    another operation x40, local copies, waits for them, and re-layouts  24.2 us
    dot_general x1, matrix products, shards(): jnp.dot(centered, centered.T, preferred_element_type=jnp.float32)  24.1 us
  transfers between devices with their start and end apart: 1, of which 1 were waited for; matrix products, arithmetic and copies ran while one was open for 2% of the time, Pallas kernels for 0%

profile of v2, /device:TPU:8, one launch (start us, length us, event | category | flops | bytes accessed | tf_op | source)
XLA Modules:
  0.0 796.0 jit_solution(17737281996057158115)
XLA Ops:
  6.5 185.8 %shard_map.28 = (bf16[32,32,16,256]{3,2,1,0:T(8,128)(2,1)}, f32[32,1,32]{2,1,0:T(1,128)}) custom-call(bf16[32,16,8192]{2,1,0:T(8,128)(2,1)} %jac_ref.1, f32[1,32]{1,0:T(1,128)} %bitcast.342), custom_call_target="tpu_custom_call" | custom-call | tf_op jit(solution)/shard_map/pallas_call | solution.py:64
  192.4 4.5 convert_reduce_fusion
  196.9 8.9 %fusion.1 = bf16[32,32,16,256]{3,2,1,0:T(8,128)(2,1)} fusion(bf16[32,32,16,256]{3,2,1,0:T(8,128)(2,1)} %get-tuple-element.7, f32[16,256]{1,0:T(8,128)S(1)} %broadcast_multiply_fusion.1), kind=kLoop, calls=%fused_computation.5 | loop fusion | flops 16777216 | bytes 16793600 | tf_op jit(solution)/shard_map/convert_element_type | solution.py:95
  205.8 24.1 %fusion.5 = f32[1024,1024]{0,1:T(8,128)} fusion(bf16[1024,16,256]{2,1,0:T(8,128)(2,1)} %bitcast.328), kind=kOutput, calls=%fused_computation.15 | convolution fusion | flops 8589934592 | bytes 12582912 | tf_op jit(solution)/shard_map/dot_general | solution.py:97
  232.6 12.2 %copy.34 = bf16[128,8,16,256]{3,1,2,0:T(8,128)(2,1)} copy(bf16[128,8,16,256]{3,2,1,0:T(8,128)(2,1)} %bitcast.329) | data formatting | bytes 16777216
  244.8 175.8 %all-reduce.3.cloned.1.call-done = f32[1024,1024]{0,1:T(8,128)} async-done(((f32[1024,1024]{0,1:T(8,128)}), f32[1024,1024]{0,1:T(8,128)}) %all-reduce.3.cloned.1.call-update) | async-done | bytes 4194320 | tf_op jit(solution)/shard_map/psum | solution.py:98
  424.1 4.8 select_add_fusion
  429.0 5.6 copy.6
  434.5 4.5 fusion.4
  441.0 11.7 %cholesky.222 = f32[128,128]{1,0:T(8,128)S(1)} custom-call(f32[128,128]{1,0:T(8,128)S(1)} %cholesky.577), custom_call_target="Cholesky" | custom-call | tf_op jit(solution)/shard_map/jit(cholesky)/cholesky | solution.py:100
  452.8 9.8 %custom-call.64 = f32[1,128,128]{1,2,0:T(8,128)S(1)} custom-call(f32[1,128,128]{2,1,0:T(8,128)S(1)} %get-tuple-element.52), custom_call_target="InvertDiagBlocksLowerTriangular" | custom-call | tf_op jit(solution)/shard_map/jit(cholesky)/cholesky | solution.py:100
  466.0 11.7 %cholesky.243 = f32[128,128]{1,0:T(8,128)S(1)} custom-call(f32[128,128]{1,0:T(8,128)S(1)} %cholesky.581), custom_call_target="Cholesky" | custom-call | tf_op jit(solution)/shard_map/jit(cholesky)/cholesky | solution.py:100
  480.7 9.8 %custom-call.65 = f32[1,128,128]{1,2,0:T(8,128)S(1)} custom-call(f32[1,128,128]{2,1,0:T(8,128)S(1)} %get-tuple-element.50), custom_call_target="InvertDiagBlocksLowerTriangular" | custom-call | tf_op jit(solution)/shard_map/jit(cholesky)/cholesky | solution.py:100
  496.0 11.7 %cholesky.466 = f32[128,128]{1,0:T(8,128)S(1)} custom-call(f32[128,128]{1,0:T(8,128)S(1)} %cholesky.586), custom_call_target="Cholesky" | custom-call | tf_op jit(solution)/shard_map/jit(cholesky)/cholesky | solution.py:100
  508.5 9.8 %custom-call.66 = f32[1,128,128]{1,2,0:T(8,128)S(1)} custom-call(f32[1,128,128]{2,1,0:T(8,128)S(1)} %get-tuple-element.48), custom_call_target="InvertDiagBlocksLowerTriangular" | custom-call | tf_op jit(solution)/shard_map/jit(cholesky)/cholesky | solution.py:100
  519.6 3.3 convolution_subtract_fusion.2
  522.9 11.7 %cholesky.485 = f32[128,128]{1,0:T(8,128)S(1)} custom-call(f32[128,128]{1,0:T(8,128)S(1)} %cholesky.591), custom_call_target="Cholesky" | custom-call | tf_op jit(solution)/shard_map/jit(cholesky)/cholesky | solution.py:100
  535.4 9.8 %custom-call.67 = f32[1,128,128]{1,2,0:T(8,128)S(1)} custom-call(f32[1,128,128]{2,1,0:T(8,128)S(1)} %get-tuple-element.46), custom_call_target="InvertDiagBlocksLowerTriangular" | custom-call | tf_op jit(solution)/shard_map/jit(cholesky)/cholesky | solution.py:100
  546.3 3.1 convolution_subtract_fusion.3
  549.5 11.9 %cholesky.504 = f32[128,128]{1,0:T(8,128)S(1)} custom-call(f32[128,128]{1,0:T(8,128)S(1)} %cholesky.596), custom_call_target="Cholesky" | custom-call | tf_op jit(solution)/shard_map/jit(cholesky)/cholesky | solution.py:100
  562.2 9.8 %custom-call.68 = f32[1,128,128]{1,2,0:T(8,128)S(1)} custom-call(f32[1,128,128]{2,1,0:T(8,128)S(1)} %get-tuple-element.44), custom_call_target="InvertDiagBlocksLowerTriangular" | custom-call | tf_op jit(solution)/shard_map/jit(cholesky)/cholesky | solution.py:100
  573.1 3.1 convolution_subtract_fusion.4
  576.2 11.7 %cholesky.524 = f32[128,128]{1,0:T(8,128)S(1)} custom-call(f32[128,128]{1,0:T(8,128)S(1)} %cholesky.601), custom_call_target="Cholesky" | custom-call | tf_op jit(solution)/shard_map/jit(cholesky)/cholesky | solution.py:100
  588.7 9.8 %custom-call.69 = f32[1,128,128]{1,2,0:T(8,128)S(1)} custom-call(f32[1,128,128]{2,1,0:T(8,128)S(1)} %get-tuple-element.42), custom_call_target="InvertDiagBlocksLowerTriangular" | custom-call | tf_op jit(solution)/shard_map/jit(cholesky)/cholesky | solution.py:100
  599.5 3.1 convolution_subtract_fusion.5
  602.6 11.7 %cholesky.544 = f32[128,128]{1,0:T(8,128)S(1)} custom-call(f32[128,128]{1,0:T(8,128)S(1)} %cholesky.606), custom_call_target="Cholesky" | custom-call | tf_op jit(solution)/shard_map/jit(cholesky)/cholesky | solution.py:100
  615.1 9.8 %custom-call.70 = f32[1,128,128]{1,2,0:T(8,128)S(1)} custom-call(f32[1,128,128]{2,1,0:T(8,128)S(1)} %get-tuple-element.40), custom_call_target="InvertDiagBlocksLowerTriangular" | custom-call | tf_op jit(solution)/shard_map/jit(cholesky)/cholesky | solution.py:100
  627.9 11.7 %cholesky.562 = f32[128,128]{1,0:T(8,128)S(1)} custom-call(f32[128,128]{1,0:T(8,128)S(1)} %convolution_subtract_fusion.6), custom_call_target="Cholesky" | custom-call | tf_op jit(solution)/shard_map/jit(cholesky)/cholesky | solution.py:100
  649.8 4.9 select_select_fusion
  654.7 24.5 %while.1 = (s32[]{:T(128)}, f32[1024,1024]{0,1:T(8,128)}, s32[8,2]{0,1:T(2,128)S(1)}, f32[8,128,128]{2,1,0:T(8,128)S(1)}, s32[]{:T(128)}) while((s32[]{:T(128)}, f32[1024,1024]{0,1:T(8,128)}, s32[8,2]{0,1:T(2,128)S(1)}, f32[8,128,128]{2,1,0:T(8,128)S(1)}, s32[]{:T(128)}) %tuple.56), condition=%wide.while_cond, body=%wide.while_body.sunk | while | flops 2 | bytes 393329 | solution.py:102
  679.1 78.8 %custom-call.71 = f32[8,128,128]{1,2,0:T(8,128)S(1)} custom-call(f32[8,128,128]{2,1,0:T(8,128)S(1)} %get-tuple-element.16), custom_call_target="InvertDiagBlocksLowerTriangular" | custom-call | tf_op jit(solution)/shard_map/triangular_solve | solution.py:102
  778.9 5.8 fusion.124
  (170 shorter events, 84.2 us)
Async XLA Ops:
  6.5 414.1 %all-reduce.3.cloned.1.call-start = ((), (), s32[]{:S(2)}) async-start(), calls=%async_computation | async-start | bytes 8388608 | tf_op jit(solution)/shard_map/psum | solution.py:98
  229.8 0.7 copy-start.2
  439.0 2.0 copy-start.1
  778.9 5.8 copy-start
Sparse Core Ops, SparseCore 0:
  230.0 190.6 all-reduce.2

commit v3 on v2

--- a/solution.py
+++ b/solution.py
@@ -80,6 +80,21 @@
     )(jacobian, en)
 
 
+def symmetric_psum(partial, axes, block=128):
+    size = partial.shape[0]
+    nb = size // block
+    blocks = partial.reshape(nb, block, nb, block).transpose(0, 2, 1, 3)
+    pairs = [(i, j) for i in range(nb) for j in range(i + 1)]
+    lower = jnp.stack([blocks[i, j] for i, j in pairs])
+    lower = lax.psum(lower, axes)
+    where = {p: k for k, p in enumerate(pairs)}
+    rows = []
+    for i in range(nb):
+        row = [lower[where[(i, j)]] if j <= i else lower[where[(j, i)]].T for j in range(nb)]
+        rows.append(jnp.concatenate(row, axis=1))
+    return jnp.concatenate(rows, axis=0)
+
+
 def shards(n, jacobian, local_energy):
     gathered, energies = exchange(jacobian, local_energy, n)
     energies = energies.reshape(-1)
@@ -95,7 +110,7 @@
         ((values - mean_row) / root_count).astype(jnp.bfloat16).reshape(samples, slab_count * width)
     )
     partial_gram = jnp.dot(centered, centered.T, preferred_element_type=jnp.float32)
-    gram = lax.psum(partial_gram, ("smp", "col", "slab"))
+    gram = symmetric_psum(partial_gram, ("smp", "col", "slab"))
     shift = 0.01 * jnp.trace(gram) / samples
     factor = jnp.linalg.cholesky(gram + shift * jnp.eye(samples, dtype=jnp.float32))
     middle = lax.linalg.triangular_solve(factor, eps[:, None], left_side=True, lower=True)

time: 802 us -> 890 us (1.11)
  local copies, waits for them, and re-layouts: 55.5 us -> 154 us
  matrix products: 79.9 us -> 69.8 us
    unnamed x25 -> x145, local copies, waits for them, and re-layouts: 15.2 us -> 76.3 us
    convert_element_type x0 -> x1, local copies, waits for them, and re-layouts: none -> 13.6 us  [shards(): ((values - mean_row) / root_count).astype(jnp.bfloat16)]
    dot_general x1, matrix products: 24.1 us -> 12.1 us  [shards(): jnp.dot(centered, centered.T, preferred_element_type=jnp.float32)]
    another operation x40 -> x41, local copies, waits for them, and re-layouts: 24.2 us -> 29 us
    another operation x30 -> x31, other arithmetic: 167 us -> 168 us  [shards(): jnp.linalg.cholesky(gram + shift * jnp.eye(samples, dtype=jnp.float32))]
where the time goes in v3:
time: 890 us; the launch traced here: 882 us
  other arithmetic  280 us (31%)
  Pallas kernels  186 us (21%)
  waiting for transfers between devices  171 us (19%)
  local copies, waits for them, and re-layouts  154 us (17%)
  matrix products  69.8 us (8%)
  between operations  21.4 us (2%)
    pallas_call x1, Pallas kernels, exchange(): pl.pallas_call(functools.partial(exchange_kernel, n, width), out_shape=(j...  186 us
    psum x1, waiting for transfers between devices, symmetric_psum(): lower = lax.psum(lower, axes)  171 us
    another operation x31, other arithmetic, shards(): jnp.linalg.cholesky(gram + shift * jnp.eye(samples, dtype=jnp.float32))  168 us
    another operation x3, other arithmetic, shards(): lax.linalg.triangular_solve(factor, middle, left_side=True, lower=True, t...  85 us
    unnamed x145, local copies, waits for them, and re-layouts  76.3 us
    another operation x40, local copies, waits for them, and re-layouts  29 us
    another operation x14, matrix products, shards(): jnp.linalg.cholesky(gram + shift * jnp.eye(samples, dtype=jnp.float32))  27 us
  transfers between devices with their start and end apart: 1, of which 1 were waited for; matrix products, arithmetic and copies ran while one was open for 2% of the time, Pallas kernels for 0%

profile of v3, /device:TPU:8, one launch (start us, length us, event | category | flops | bytes accessed | tf_op | source)
XLA Modules:
  0.0 881.5 jit_solution(16730244765215376117)
XLA Ops:
  6.5 185.8 %shard_map.28 = (bf16[32,32,16,256]{3,2,1,0:T(8,128)(2,1)}, f32[32,1,32]{2,1,0:T(1,128)}) custom-call(bf16[32,16,8192]{2,1,0:T(8,128)(2,1)} %jac_ref.1, f32[1,32]{1,0:T(1,128)} %bitcast.662), custom_call_target="tpu_custom_call" | custom-call | tf_op jit(solution)/shard_map/pallas_call | solution.py:64
  192.4 4.5 convert_reduce_fusion
  196.9 8.9 %fusion.1 = bf16[32,32,16,256]{3,2,1,0:T(8,128)(2,1)} fusion(bf16[32,32,16,256]{3,2,1,0:T(8,128)(2,1)} %get-tuple-element.7, f32[16,256]{1,0:T(8,128)S(1)} %broadcast_multiply_fusion.1), kind=kLoop, calls=%fused_computation.5 | loop fusion | flops 16777216 | bytes 16793600 | tf_op jit(solution)/shard_map/convert_element_type | solution.py:110
  205.8 13.6 %reshape.299 = bf16[8,128,4096,1]{2,1,0,3:T(8,128)(2,1)} reshape(bf16[32,32,16,256]{3,2,1,0:T(8,128)(2,1)} %fusion.1) | data formatting | bytes 16777216 | tf_op jit(solution)/shard_map/convert_element_type | solution.py:110
  219.4 12.1 %fusion.5 = f32[8,8,128,128]{2,3,1,0:T(8,128)S(1)} fusion(bf16[8,128,4096,1]{2,1,0,3:T(8,128)(2,1)} %reshape.299), kind=kOutput, calls=%fused_computation.15 | convolution fusion | flops 8589934592 | bytes 12582912 | tf_op jit(solution)/shard_map/dot_general | solution.py:112
  237.7 12.2 %copy.86 = bf16[128,8,16,256]{3,1,2,0:T(8,128)(2,1)} copy(bf16[128,8,16,256]{3,2,1,0:T(8,128)(2,1)} %bitcast.648) | data formatting | bytes 16777216
  250.5 170.7 %all-reduce.3.cloned.1.call-done = f32[36,128,128]{1,2,0:T(8,128)} async-done(((f32[36,128,128]{1,2,0:T(8,128)}), f32[36,128,128]{1,2,0:T(8,128)}) %all-reduce.3.cloned.1.call-update) | async-done | bytes 2359312 | tf_op jit(solution)/shard_map/psum | solution.py:89
  501.5 4.8 select_add_fusion
  506.3 5.7 copy.36
  512.1 4.5 fusion.4
  518.5 11.7 %cholesky.222 = f32[128,128]{1,0:T(8,128)S(1)} custom-call(f32[128,128]{1,0:T(8,128)S(1)} %cholesky.577), custom_call_target="Cholesky" | custom-call | tf_op jit(solution)/shard_map/jit(cholesky)/cholesky | solution.py:115
  530.4 9.8 %custom-call.64 = f32[1,128,128]{1,2,0:T(8,128)S(1)} custom-call(f32[1,128,128]{2,1,0:T(8,128)S(1)} %get-tuple-element.83), custom_call_target="InvertDiagBlocksLowerTriangular" | custom-call | tf_op jit(solution)/shard_map/jit(cholesky)/cholesky | solution.py:115
  543.5 11.7 %cholesky.243 = f32[128,128]{1,0:T(8,128)S(1)} custom-call(f32[128,128]{1,0:T(8,128)S(1)} %cholesky.581), custom_call_target="Cholesky" | custom-call | tf_op jit(solution)/shard_map/jit(cholesky)/cholesky | solution.py:115
  558.0 9.8 %custom-call.65 = f32[1,128,128]{1,2,0:T(8,128)S(1)} custom-call(f32[1,128,128]{2,1,0:T(8,128)S(1)} %get-tuple-element.81), custom_call_target="InvertDiagBlocksLowerTriangular" | custom-call | tf_op jit(solution)/shard_map/jit(cholesky)/cholesky | solution.py:115
  573.2 11.7 %cholesky.466 = f32[128,128]{1,0:T(8,128)S(1)} custom-call(f32[128,128]{1,0:T(8,128)S(1)} %cholesky.586), custom_call_target="Cholesky" | custom-call | tf_op jit(solution)/shard_map/jit(cholesky)/cholesky | solution.py:115
  585.7 9.8 %custom-call.66 = f32[1,128,128]{1,2,0:T(8,128)S(1)} custom-call(f32[1,128,128]{2,1,0:T(8,128)S(1)} %get-tuple-element.79), custom_call_target="InvertDiagBlocksLowerTriangular" | custom-call | tf_op jit(solution)/shard_map/jit(cholesky)/cholesky | solution.py:115
  596.8 3.3 convolution_subtract_fusion.2
  600.1 11.7 %cholesky.485 = f32[128,128]{1,0:T(8,128)S(1)} custom-call(f32[128,128]{1,0:T(8,128)S(1)} %cholesky.591), custom_call_target="Cholesky" | custom-call | tf_op jit(solution)/shard_map/jit(cholesky)/cholesky | solution.py:115
  612.6 9.8 %custom-call.67 = f32[1,128,128]{1,2,0:T(8,128)S(1)} custom-call(f32[1,128,128]{2,1,0:T(8,128)S(1)} %get-tuple-element.77), custom_call_target="InvertDiagBlocksLowerTriangular" | custom-call | tf_op jit(solution)/shard_map/jit(cholesky)/cholesky | solution.py:115
  623.6 3.1 convolution_subtract_fusion.3
  626.7 12.1 %cholesky.504 = f32[128,128]{1,0:T(8,128)S(1)} custom-call(f32[128,128]{1,0:T(8,128)S(1)} %cholesky.596), custom_call_target="Cholesky" | custom-call | tf_op jit(solution)/shard_map/jit(cholesky)/cholesky | solution.py:115
  639.6 9.8 %custom-call.68 = f32[1,128,128]{1,2,0:T(8,128)S(1)} custom-call(f32[1,128,128]{2,1,0:T(8,128)S(1)} %get-tuple-element.75), custom_call_target="InvertDiagBlocksLowerTriangular" | custom-call | tf_op jit(solution)/shard_map/jit(cholesky)/cholesky | solution.py:115
  653.6 11.7 %cholesky.524 = f32[128,128]{1,0:T(8,128)S(1)} custom-call(f32[128,128]{1,0:T(8,128)S(1)} %cholesky.601), custom_call_target="Cholesky" | custom-call | tf_op jit(solution)/shard_map/jit(cholesky)/cholesky | solution.py:115
  666.1 9.8 %custom-call.69 = f32[1,128,128]{1,2,0:T(8,128)S(1)} custom-call(f32[1,128,128]{2,1,0:T(8,128)S(1)} %get-tuple-element.73), custom_call_target="InvertDiagBlocksLowerTriangular" | custom-call | tf_op jit(solution)/shard_map/jit(cholesky)/cholesky | solution.py:115
  679.7 11.7 %cholesky.544 = f32[128,128]{1,0:T(8,128)S(1)} custom-call(f32[128,128]{1,0:T(8,128)S(1)} %cholesky.606), custom_call_target="Cholesky" | custom-call | tf_op jit(solution)/shard_map/jit(cholesky)/cholesky | solution.py:115
  692.2 9.8 %custom-call.70 = f32[1,128,128]{1,2,0:T(8,128)S(1)} custom-call(f32[1,128,128]{2,1,0:T(8,128)S(1)} %get-tuple-element.71), custom_call_target="InvertDiagBlocksLowerTriangular" | custom-call | tf_op jit(solution)/shard_map/jit(cholesky)/cholesky | solution.py:115
  705.1 11.7 %cholesky.562 = f32[128,128]{1,0:T(8,128)S(1)} custom-call(f32[128,128]{1,0:T(8,128)S(1)} %convolution_subtract_fusion.6), custom_call_target="Cholesky" | custom-call | tf_op jit(solution)/shard_map/jit(cholesky)/cholesky | solution.py:115
  727.9 4.9 select_select_fusion
  732.8 29.1 %while.1 = (s32[]{:T(128)}, f32[1024,1024]{0,1:T(8,128)}, s32[8,2]{0,1:T(2,128)S(1)}, f32[8,128,128]{2,1,0:T(8,128)}, s32[]{:T(128)}) while((s32[]{:T(128)}, f32[1024,1024]{0,1:T(8,128)}, s32[8,2]{0,1:T(2,128)S(1)}, f32[8,128,128]{2,1,0:T(8,128)}, s32[]{:T(128)}) %tuple.83), condition=%wide.while_cond, body=%wide.while_body.sunk | while | flops 2 | bytes 393329 | solution.py:117
  761.8 79.6 %custom-call.71 = f32[8,128,128]{1,2,0:T(8,128)S(1)} custom-call(f32[8,128,128]{2,1,0:T(8,128)} %get-tuple-element.16), custom_call_target="InvertDiagBlocksLowerTriangular" | custom-call | tf_op jit(solution)/shard_map/triangular_solve | solution.py:117
  862.4 4.4 fusion.128
  866.8 5.7 fusion.129
  (310 shorter events, 173.4 us)
Async XLA Ops:
  6.5 414.6 %all-reduce.3.cloned.1.call-start = ((), (), s32[]{:S(2)}) async-start(), calls=%async_computation | async-start | bytes 4718592 | tf_op jit(solution)/shard_map/psum | solution.py:89
  231.5 2.0 copy-start.4
  232.1 1.4 copy-start.2
  421.2 32.5 %copy-start.1 = (f32[36,128,128]{1,2,0:T(8,128)S(1)}, f32[36,128,128]{1,2,0:T(8,128)}, u32[]{:S(2)}) copy-start(f32[36,128,128]{1,2,0:T(8,128)} %all-reduce.3.cloned.1.call-done) | copy-start | bytes 7077892
  454.3 4.7 copy-start.3
  516.6 2.0 copy-start
  727.8 4.9 copy-start.9
  727.9 113.6 %copy-start.5 = (f32[128,1]{0,1:T(1,128)S(1)}, f32[128,1]{0,1:T(1,128)}, u32[]{:S(2)}) copy-start(f32[128,1]{0,1:T(1,128)} %reshape.300) | copy-start | bytes 1540
  727.9 113.7 %copy-start.6 = (f32[128]{0:T(128)S(1)}, f32[128]{0:T(128)}, u32[]{:S(2)}) copy-start(f32[128]{0:T(128)} %triangular_solve.286) | copy-start | bytes 1540
  727.9 118.9 %copy-start.7 = (f32[128]{0:T(128)S(1)}, f32[128]{0:T(128)}, u32[]{:S(2)}) copy-start(f32[128]{0:T(128)} %triangular_solve.329) | copy-start | bytes 1540
  727.9 121.9 %copy-start.8 = (f32[128]{0:T(128)S(1)}, f32[128]{0:T(128)}, u32[]{:S(2)}) copy-start(f32[128]{0:T(128)} %triangular_solve.351) | copy-start | bytes 1540
Sparse Core Ops, SparseCore 0:
  233.6 187.4 all-reduce.2

commit v4 on v2

--- a/solution.py
+++ b/solution.py
@@ -95,7 +95,7 @@
         ((values - mean_row) / root_count).astype(jnp.bfloat16).reshape(samples, slab_count * width)
     )
     partial_gram = jnp.dot(centered, centered.T, preferred_element_type=jnp.float32)
-    gram = lax.psum(partial_gram, ("smp", "col", "slab"))
+    gram = lax.psum(lax.psum(lax.psum(partial_gram, "col"), "slab"), "smp")
     shift = 0.01 * jnp.trace(gram) / samples
     factor = jnp.linalg.cholesky(gram + shift * jnp.eye(samples, dtype=jnp.float32))
     middle = lax.linalg.triangular_solve(factor, eps[:, None], left_side=True, lower=True)

time: 802 us -> 1130 us (1.41)
  waiting for transfers between devices: 176 us -> 501 us
    psum x1 -> x3, waiting for transfers between devices: 176 us -> 500 us  [shards(): gram = lax.psum(lax.psum(lax.psum(partial_gram, 'col'), 'slab'), 'smp')]
  transfers between devices with their start and end apart: 1 -> 3, of which waited for: 1 -> 3; matrix products, arithmetic and copies ran while one was open for 2% -> 1% of each run, Pallas kernels for 0% -> 0%
where the time goes in v4:
time: 1130 us; the launch traced here: 1120 us
  waiting for transfers between devices  501 us (44%)
  other arithmetic  278 us (25%)
  Pallas kernels  186 us (16%)
  matrix products  79.7 us (7%)
  local copies, waits for them, and re-layouts  54.9 us (5%)
  between operations  20.5 us (2%)
    psum x3, waiting for transfers between devices, shards(): gram = lax.psum(lax.psum(lax.psum(partial_gram, 'col'), 'slab'), 'smp')  500 us
    pallas_call x1, Pallas kernels, exchange(): pl.pallas_call(functools.partial(exchange_kernel, n, width), out_shape=(j...  186 us
    another operation x30, other arithmetic, shards(): jnp.linalg.cholesky(gram + shift * jnp.eye(samples, dtype=jnp.float32))  167 us
    another operation x3, other arithmetic, shards(): lax.linalg.triangular_solve(factor, middle, left_side=True, lower=True, t...  83.6 us
    another operation x14, matrix products, shards(): jnp.linalg.cholesky(gram + shift * jnp.eye(samples, dtype=jnp.float32))  27.2 us
    another operation x40, local copies, waits for them, and re-layouts  24.2 us
    dot_general x1, matrix products, shards(): jnp.dot(centered, centered.T, preferred_element_type=jnp.float32)  23.9 us
  transfers between devices with their start and end apart: 3, of which 3 were waited for; matrix products, arithmetic and copies ran while one was open for 1% of the time, Pallas kernels for 0%

profile of v4, /device:TPU:8, one launch (start us, length us, event | category | flops | bytes accessed | tf_op | source)
XLA Modules:
  0.0 1119.7 jit_solution(13348377517986233069)
XLA Ops:
  6.5 185.8 %shard_map.28 = (bf16[32,32,16,256]{3,2,1,0:T(8,128)(2,1)}, f32[32,1,32]{2,1,0:T(1,128)}) custom-call(bf16[32,16,8192]{2,1,0:T(8,128)(2,1)} %jac_ref.1, f32[1,32]{1,0:T(1,128)} %bitcast.342), custom_call_target="tpu_custom_call" | custom-call | tf_op jit(solution)/shard_map/pallas_call | solution.py:64
  192.4 4.5 convert_reduce_fusion
  196.9 8.9 fusion.1
  205.8 23.9 %fusion.5 = f32[1024,1024]{0,1:T(8,128)} fusion(bf16[1024,16,256]{2,1,0:T(8,128)(2,1)} %bitcast.328), kind=kOutput, calls=%fused_computation.15 | convolution fusion | flops 8589934592 | bytes 12582912 | tf_op jit(solution)/shard_map/dot_general | solution.py:97
  229.7 70.4 %all-reduce.5.cloned.1.call-done = f32[1024,1024]{0,1:T(8,128)} async-done(((f32[1024,1024]{0,1:T(8,128)}), f32[1024,1024]{0,1:T(8,128)}) %all-reduce.5.cloned.1.call-update) | async-done | bytes 4194320 | tf_op jit(solution)/shard_map/psum | solution.py:98
  300.4 118.9 %all-reduce.7.cloned.1.call-done = f32[1024,1024]{0,1:T(8,128)} async-done(((f32[1024,1024]{0,1:T(8,128)}), f32[1024,1024]{0,1:T(8,128)}) %all-reduce.7.cloned.1.call-update) | async-done | bytes 4194320 | tf_op jit(solution)/shard_map/psum | solution.py:98
  421.4 12.2 %copy.34 = bf16[128,8,16,256]{3,1,2,0:T(8,128)(2,1)} copy(bf16[128,8,16,256]{3,2,1,0:T(8,128)(2,1)} %bitcast.329) | data formatting | bytes 16777216
  433.6 311.1 %all-reduce.9.cloned.1.call-done = f32[1024,1024]{0,1:T(8,128)} async-done(((f32[1024,1024]{0,1:T(8,128)}), f32[1024,1024]{0,1:T(8,128)}) %all-reduce.9.cloned.1.call-update) | async-done | bytes 4194320 | tf_op jit(solution)/shard_map/psum | solution.py:98
  748.2 4.8 select_add_fusion
  753.1 5.6 copy.6
  758.6 4.5 fusion.4
  765.1 11.7 %cholesky.222 = f32[128,128]{1,0:T(8,128)S(1)} custom-call(f32[128,128]{1,0:T(8,128)S(1)} %cholesky.577), custom_call_target="Cholesky" | custom-call | tf_op jit(solution)/shard_map/jit(cholesky)/cholesky | solution.py:100
  776.9 9.8 custom-call.64
  790.1 11.7 %cholesky.243 = f32[128,128]{1,0:T(8,128)S(1)} custom-call(f32[128,128]{1,0:T(8,128)S(1)} %cholesky.581), custom_call_target="Cholesky" | custom-call | tf_op jit(solution)/shard_map/jit(cholesky)/cholesky | solution.py:100
  804.8 9.8 custom-call.65
  820.1 11.7 %cholesky.466 = f32[128,128]{1,0:T(8,128)S(1)} custom-call(f32[128,128]{1,0:T(8,128)S(1)} %cholesky.586), custom_call_target="Cholesky" | custom-call | tf_op jit(solution)/shard_map/jit(cholesky)/cholesky | solution.py:100
  832.6 9.8 custom-call.66
  843.6 3.3 convolution_subtract_fusion.2
  847.0 11.7 %cholesky.485 = f32[128,128]{1,0:T(8,128)S(1)} custom-call(f32[128,128]{1,0:T(8,128)S(1)} %cholesky.591), custom_call_target="Cholesky" | custom-call | tf_op jit(solution)/shard_map/jit(cholesky)/cholesky | solution.py:100
  859.5 9.8 custom-call.67
  870.4 3.1 convolution_subtract_fusion.3
  873.6 11.9 %cholesky.504 = f32[128,128]{1,0:T(8,128)S(1)} custom-call(f32[128,128]{1,0:T(8,128)S(1)} %cholesky.596), custom_call_target="Cholesky" | custom-call | tf_op jit(solution)/shard_map/jit(cholesky)/cholesky | solution.py:100
  886.3 9.8 custom-call.68
  900.3 11.7 %cholesky.524 = f32[128,128]{1,0:T(8,128)S(1)} custom-call(f32[128,128]{1,0:T(8,128)S(1)} %cholesky.601), custom_call_target="Cholesky" | custom-call | tf_op jit(solution)/shard_map/jit(cholesky)/cholesky | solution.py:100
  912.8 9.8 custom-call.69
  926.7 11.7 %cholesky.544 = f32[128,128]{1,0:T(8,128)S(1)} custom-call(f32[128,128]{1,0:T(8,128)S(1)} %cholesky.606), custom_call_target="Cholesky" | custom-call | tf_op jit(solution)/shard_map/jit(cholesky)/cholesky | solution.py:100
  939.2 9.8 custom-call.70
  952.0 11.7 %cholesky.562 = f32[128,128]{1,0:T(8,128)S(1)} custom-call(f32[128,128]{1,0:T(8,128)S(1)} %convolution_subtract_fusion.6), custom_call_target="Cholesky" | custom-call | tf_op jit(solution)/shard_map/jit(cholesky)/cholesky | solution.py:100
  973.9 4.9 select_select_fusion
  978.8 24.5 %while.1 = (s32[]{:T(128)}, f32[1024,1024]{0,1:T(8,128)}, s32[8,2]{0,1:T(2,128)S(1)}, f32[8,128,128]{2,1,0:T(8,128)S(1)}, s32[]{:T(128)}) while((s32[]{:T(128)}, f32[1024,1024]{0,1:T(8,128)}, s32[8,2]{0,1:T(2,128)S(1)}, f32[8,128,128]{2,1,0:T(8,128)S(1)}, s32[]{:T(128)}) %tuple.56), condition=%wide.while_cond, body=%wide.while_body.sunk | while | flops 2 | bytes 393329 | solution.py:102
  1003.2 78.8 %custom-call.71 = f32[8,128,128]{1,2,0:T(8,128)S(1)} custom-call(f32[8,128,128]{2,1,0:T(8,128)S(1)} %get-tuple-element.16), custom_call_target="InvertDiagBlocksLowerTriangular" | custom-call | tf_op jit(solution)/shard_map/triangular_solve | solution.py:102
  1103.0 5.8 fusion.124
  (176 shorter events, 89.9 us)
Async XLA Ops:
  6.5 293.6 %all-reduce.5.cloned.1.call-start = ((), (), s32[]{:S(2)}) async-start(), calls=%async_computation | async-start | bytes 8388608 | tf_op jit(solution)/shard_map/psum | solution.py:98
  229.6 189.6 %all-reduce.7.cloned.1.call-start = ((), (), s32[]{:S(2)}) async-start(), calls=%async_computation.1 | async-start | bytes 8388608 | tf_op jit(solution)/shard_map/psum | solution.py:98
  300.1 119.2 %copy-start.2 = (f32[32,1,32]{2,1,0:T(1,128)S(1)}, f32[32,1,32]{2,1,0:T(1,128)}, u32[]{:S(2)}) copy-start(f32[32,1,32]{2,1,0:T(1,128)} %get-tuple-element.8) | copy-start | bytes 12292
  300.2 444.6 %all-reduce.9.cloned.1.call-start = ((), (), s32[]{:S(2)}) async-start(), calls=%async_computation.2 | async-start | bytes 8388608 | tf_op jit(solution)/shard_map/psum | solution.py:98
  763.1 2.0 copy-start.1
  1103.0 5.8 copy-start
Sparse Core Ops, SparseCore 0:
  229.8 70.3 all-reduce.4
  302.9 116.3 all-reduce.6
  421.8 322.9 all-reduce.8

commit v5 on v2

--- a/solution.py
+++ b/solution.py
@@ -9,6 +9,72 @@
 
 SLABS = 32
 SLAB_COLS = 16384
+
+
+def solve_kernel(block, l_ref, dinv_ref, b_ref, c_ref, y_ref, r_ref):
+    n = l_ref.shape[0]
+    nb = n // block
+    lane = lax.broadcasted_iota(jnp.int32, (1, block), 1)
+    hi = lax.Precision.HIGHEST
+    for q in range(nb):
+        lo = q * block
+        r_q = b_ref[:, lo:lo + block]
+        if q > 0:
+            prev = jnp.broadcast_to(y_ref[:, :lo], (8, lo))
+            r_q = r_q - lax.dot_general(prev, l_ref[lo:lo + block, :lo], (((1,), (1,)), ((), ())),
+                                        precision=hi, preferred_element_type=jnp.float32)[0:1]
+
+        def fwd(g, y_q, lo=lo, r_q=r_q):
+            tile = l_ref[pl.ds(pl.multiple_of(lo + g * 8, 8), 8), lo:lo + block]
+            for r in range(8):
+                ii = g * 8 + r
+                row = jnp.where(lane < ii, tile[r:r + 1, :], 0.0)
+                ri = jnp.sum(jnp.where(lane == ii, r_q, 0.0), axis=1, keepdims=True)
+                s = jnp.sum(row * y_q, axis=1, keepdims=True)
+                yi = (ri - s) * dinv_ref[lo + ii]
+                y_q = jnp.where(lane == ii, yi, y_q)
+            return y_q
+
+        y_ref[:, lo:lo + block] = lax.fori_loop(0, block // 8, fwd, jnp.zeros((1, block), jnp.float32))
+    r_ref[...] = y_ref[...]
+    for q in reversed(range(nb)):
+        lo = q * block
+
+        def bwd(k, carry, lo=lo):
+            r_q, c_q = carry
+            g = block // 8 - 1 - k
+            tile = l_ref[pl.ds(pl.multiple_of(lo + g * 8, 8), 8), lo:lo + block]
+            for r in reversed(range(8)):
+                jj = g * 8 + r
+                rj = jnp.sum(jnp.where(lane == jj, r_q, 0.0), axis=1, keepdims=True)
+                cj = rj * dinv_ref[lo + jj]
+                row = jnp.where(lane < jj, tile[r:r + 1, :], 0.0)
+                r_q = r_q - cj * row
+                c_q = jnp.where(lane == jj, cj, c_q)
+            return r_q, c_q
+
+        r_q = r_ref[:, lo:lo + block]
+        _, c_q = lax.fori_loop(0, block // 8, bwd, (r_q, jnp.zeros((1, block), jnp.float32)))
+        c_ref[:, lo:lo + block] = c_q
+        if q > 0:
+            cb = jnp.broadcast_to(c_q, (8, block))
+            r_ref[:, :lo] = r_ref[:, :lo] - jnp.dot(
+                cb, l_ref[lo:lo + block, :lo], precision=hi, preferred_element_type=jnp.float32)[0:1]
+
+
+def cho_solve(factor, rhs, block=128):
+    n = factor.shape[0]
+    dinv = 1.0 / jnp.diagonal(factor)
+    out = pl.pallas_call(
+        functools.partial(solve_kernel, block),
+        out_shape=jax.ShapeDtypeStruct((1, n), jnp.float32),
+        in_specs=[pl.BlockSpec(memory_space=pltpu.VMEM),
+                  pl.BlockSpec(memory_space=pltpu.SMEM),
+                  pl.BlockSpec(memory_space=pltpu.VMEM)],
+        out_specs=pl.BlockSpec(memory_space=pltpu.VMEM),
+        scratch_shapes=[pltpu.VMEM((1, n), jnp.float32), pltpu.VMEM((1, n), jnp.float32)],
+    )(factor, dinv, rhs.reshape(1, n))
+    return out.reshape(n)
 
 
 def exchange_kernel(n, width, jac_ref, en_ref, cols_ref, en_all_ref,
@@ -98,10 +164,7 @@
     gram = lax.psum(partial_gram, ("smp", "col", "slab"))
     shift = 0.01 * jnp.trace(gram) / samples
     factor = jnp.linalg.cholesky(gram + shift * jnp.eye(samples, dtype=jnp.float32))
-    middle = lax.linalg.triangular_solve(factor, eps[:, None], left_side=True, lower=True)
-    coeffs = lax.linalg.triangular_solve(
-        factor, middle, left_side=True, lower=True, transpose_a=True
-    )[:, 0]
+    coeffs = cho_solve(factor, eps)
     delta = jnp.dot(coeffs, centered.astype(jnp.float32), precision=lax.Precision.HIGHEST)
     squared = jnp.dot(coeffs, jnp.dot(gram, coeffs, precision=lax.Precision.HIGHEST),
                       precision=lax.Precision.HIGHEST)

time: 802 us -> 933 us (1.16)
  Pallas kernels: 186 us -> 421 us
  other arithmetic: 278 us -> 205 us
  matrix products: 79.9 us -> 63.4 us
  local copies, waits for them, and re-layouts: 55.5 us -> 41.4 us
    pallas_call x0 -> x1, Pallas kernels: none -> 236 us  [cho_solve(): pl.pallas_call(functools.partial(solve_kernel, block), out_shape=jax.Shap...]
    another operation x3 -> x0, other arithmetic: 83.6 us -> none  [shards(): lax.linalg.triangular_solve(factor, middle, left_side=True, lower=True, t...]
    another operation x54 -> x0, local copies, waits for them, and re-layouts: 25 us -> none
    another operation x30 -> x0, matrix products: 20.6 us -> none  [the longest x15 10.7 us: shards(): lax.linalg.triangular_solve(factor, middle, left_side=True, lower=True, t...]
    gather x0 -> x1, local copies, waits for them, and re-layouts: none -> 17.2 us  [cho_solve(): dinv = 1.0 / jnp.diagonal(factor)]
  transfers between devices with their start and end apart: 1 -> 1, of which waited for: 1 -> 1; matrix products, arithmetic and copies ran while one was open for 2% -> 1% of each run, Pallas kernels for 0% -> 0%
where the time goes in v5:
time: 933 us; the launch traced here: 928 us
  Pallas kernels  421 us (45%)
  other arithmetic  205 us (22%)
  waiting for transfers between devices  176 us (19%)
  matrix products  63.4 us (7%)
  local copies, waits for them, and re-layouts  41.4 us (4%)
  between operations  20.9 us (2%)
    pallas_call x1, Pallas kernels, cho_solve(): pl.pallas_call(functools.partial(solve_kernel, block), out_shape=jax.Shap...  236 us
    pallas_call x1, Pallas kernels, exchange(): pl.pallas_call(functools.partial(exchange_kernel, n, width), out_shape=(j...  186 us
    psum x1, waiting for transfers between devices, shards(): gram = lax.psum(partial_gram, ('smp', 'col', 'slab'))  176 us
    another operation x30, other arithmetic, shards(): jnp.linalg.cholesky(gram + shift * jnp.eye(samples, dtype=jnp.float32))  172 us
    dot_general x1, matrix products, shards(): jnp.dot(centered, centered.T, preferred_element_type=jnp.float32)  28.8 us
    another operation x14, matrix products, shards(): jnp.linalg.cholesky(gram + shift * jnp.eye(samples, dtype=jnp.float32))  23.2 us
  transfers between devices with their start and end apart: 1, of which 1 were waited for; matrix products, arithmetic and copies ran while one was open for 1% of the time, Pallas kernels for 0%

profile of v5, /device:TPU:8, one launch (start us, length us, event | category | flops | bytes accessed | tf_op | source)
XLA Modules:
  0.0 927.7 jit_solution(2969835625829282858)
XLA Ops:
  6.5 185.8 %shard_map.28 = (bf16[32,32,16,256]{3,2,1,0:T(8,128)(2,1)}, f32[32,1,32]{2,1,0:T(1,128)}) custom-call(bf16[32,16,8192]{2,1,0:T(8,128)(2,1)} %jac_ref.1, f32[1,32]{1,0:T(1,128)} %bitcast.68), custom_call_target="tpu_custom_call" | custom-call | tf_op jit(solution)/shard_map/pallas_call | solution.py:130
  192.4 4.5 convert_reduce_fusion
  196.9 8.9 fusion.1
  205.8 28.8 %fusion.5 = f32[1024,1024]{1,0:T(8,128)} fusion(bf16[1024,16,256]{2,1,0:T(8,128)(2,1)} %bitcast.63), kind=kOutput, calls=%fused_computation.14 | convolution fusion | flops 8589934592 | bytes 12582912 | tf_op jit(solution)/shard_map/dot_general | solution.py:163
  237.3 12.2 %copy.11 = bf16[128,8,16,256]{3,1,2,0:T(8,128)(2,1)} copy(bf16[128,8,16,256]{3,2,1,0:T(8,128)(2,1)} %bitcast.64) | data formatting | bytes 16777216
  249.6 175.9 %all-reduce.3.cloned.1.call-done = f32[1024,1024]{1,0:T(8,128)} async-done(((f32[1024,1024]{1,0:T(8,128)}), f32[1024,1024]{1,0:T(8,128)}) %all-reduce.3.cloned.1.call-update) | async-done | bytes 4194320 | tf_op jit(solution)/shard_map/psum | solution.py:164
  425.4 2.9 select_reduce_fusion
  429.0 4.8 select_add_fusion
  433.9 5.5 copy.8
  439.4 4.5 fusion.4
  445.8 11.7 %cholesky.222 = f32[128,128]{1,0:T(8,128)S(1)} custom-call(f32[128,128]{1,0:T(8,128)S(1)} %cholesky.577), custom_call_target="Cholesky" | custom-call | tf_op jit(solution)/shard_map/jit(cholesky)/cholesky | solution.py:166
  457.6 2.5 cholesky.254
  460.1 9.8 %custom-call.59 = f32[1,128,128]{1,2,0:T(8,128)S(1)} custom-call(f32[1,128,128]{2,1,0:T(8,128)S(1)} %get-tuple-element.30), custom_call_target="InvertDiagBlocksLowerTriangular" | custom-call | tf_op jit(solution)/shard_map/jit(cholesky)/cholesky | solution.py:166
  473.8 11.9 %cholesky.243 = f32[128,128]{1,0:T(8,128)S(1)} custom-call(f32[128,128]{1,0:T(8,128)S(1)} %cholesky.581), custom_call_target="Cholesky" | custom-call | tf_op jit(solution)/shard_map/jit(cholesky)/cholesky | solution.py:166
  486.4 9.8 %custom-call.60 = f32[1,128,128]{1,2,0:T(8,128)S(1)} custom-call(f32[1,128,128]{2,1,0:T(8,128)S(1)} %get-tuple-element.27), custom_call_target="InvertDiagBlocksLowerTriangular" | custom-call | tf_op jit(solution)/shard_map/jit(cholesky)/cholesky | solution.py:166
  499.5 11.7 %cholesky.466 = f32[128,128]{1,0:T(8,128)S(1)} custom-call(f32[128,128]{1,0:T(8,128)S(1)} %cholesky.586), custom_call_target="Cholesky" | custom-call | tf_op jit(solution)/shard_map/jit(cholesky)/cholesky | solution.py:166
  512.6 9.8 %custom-call.61 = f32[1,128,128]{1,2,0:T(8,128)S(1)} custom-call(f32[1,128,128]{2,1,0:T(8,128)S(1)} %get-tuple-element.24), custom_call_target="InvertDiagBlocksLowerTriangular" | custom-call | tf_op jit(solution)/shard_map/jit(cholesky)/cholesky | solution.py:166
  523.6 2.4 convolution_subtract_fusion.2
  526.0 12.1 %cholesky.485 = f32[128,128]{1,0:T(8,128)S(1)} custom-call(f32[128,128]{1,0:T(8,128)S(1)} %cholesky.591), custom_call_target="Cholesky" | custom-call | tf_op jit(solution)/shard_map/jit(cholesky)/cholesky | solution.py:166
  539.4 9.8 %custom-call.62 = f32[1,128,128]{1,2,0:T(8,128)S(1)} custom-call(f32[1,128,128]{2,1,0:T(8,128)S(1)} %get-tuple-element.21), custom_call_target="InvertDiagBlocksLowerTriangular" | custom-call | tf_op jit(solution)/shard_map/jit(cholesky)/cholesky | solution.py:166
  552.6 11.7 %cholesky.504 = f32[128,128]{1,0:T(8,128)S(1)} custom-call(f32[128,128]{1,0:T(8,128)S(1)} %cholesky.596), custom_call_target="Cholesky" | custom-call | tf_op jit(solution)/shard_map/jit(cholesky)/cholesky | solution.py:166
  565.6 9.9 %custom-call.63 = f32[1,128,128]{1,2,0:T(8,128)S(1)} custom-call(f32[1,128,128]{2,1,0:T(8,128)S(1)} %get-tuple-element.18), custom_call_target="InvertDiagBlocksLowerTriangular" | custom-call | tf_op jit(solution)/shard_map/jit(cholesky)/cholesky | solution.py:166
  578.9 11.7 %cholesky.524 = f32[128,128]{1,0:T(8,128)S(1)} custom-call(f32[128,128]{1,0:T(8,128)S(1)} %cholesky.601), custom_call_target="Cholesky" | custom-call | tf_op jit(solution)/shard_map/jit(cholesky)/cholesky | solution.py:166
  592.0 9.8 %custom-call.64 = f32[1,128,128]{1,2,0:T(8,128)S(1)} custom-call(f32[1,128,128]{2,1,0:T(8,128)S(1)} %get-tuple-element.15), custom_call_target="InvertDiagBlocksLowerTriangular" | custom-call | tf_op jit(solution)/shard_map/jit(cholesky)/cholesky | solution.py:166
  604.8 11.9 %cholesky.544 = f32[128,128]{1,0:T(8,128)S(1)} custom-call(f32[128,128]{1,0:T(8,128)S(1)} %cholesky.606), custom_call_target="Cholesky" | custom-call | tf_op jit(solution)/shard_map/jit(cholesky)/cholesky | solution.py:166
  618.0 9.8 %custom-call.65 = f32[1,128,128]{1,2,0:T(8,128)S(1)} custom-call(f32[1,128,128]{2,1,0:T(8,128)S(1)} %get-tuple-element.12), custom_call_target="InvertDiagBlocksLowerTriangular" | custom-call | tf_op jit(solution)/shard_map/jit(cholesky)/cholesky | solution.py:166
  630.4 11.7 %cholesky.562 = f32[128,128]{1,0:T(8,128)S(1)} custom-call(f32[128,128]{1,0:T(8,128)S(1)} %convolution_subtract_fusion.6), custom_call_target="Cholesky" | custom-call | tf_op jit(solution)/shard_map/jit(cholesky)/cholesky | solution.py:166
  649.0 4.8 select_select_fusion.l_ref
  653.9 17.2 %gather_fusion = f32[1024]{0:T(1024)S(1)} fusion(f32[1024,1024]{1,0:T(8,128)} %select_select_fusion.l_ref, s32[1024]{0:T(1024)S(1)} %bitcast.61), kind=kCustom, calls=%fused_computation | custom fusion | bytes 16384 | tf_op jit(solution)/shard_map/jit(diagonal)/cond/branch_0_fun/gather | solution.py:67
  671.6 235.6 %shard_map.29 = f32[1,1024]{1,0:T(1,128)} custom-call(f32[1024,1024]{1,0:T(8,128)} %select_select_fusion.l_ref, f32[1024]{0:T(1024)} %broadcast_divide_fusion.dinv_ref, f32[1,1024]{1,0:T(1,128)} %div.55.b_ref), custom_call_target="tpu_custom_call" | custom-call | tf_op jit(solution)/shard_map/pallas_call | solution.py:68
  907.3 5.8 fusion.37
  914.3 5.7 fusion.35
  (52 shorter events, 35.9 us)
Async XLA Ops:
  6.5 418.9 %all-reduce.3.cloned.1.call-start = ((), (), s32[]{:S(2)}) async-start(), calls=%async_computation | async-start | bytes 8388608 | tf_op jit(solution)/shard_map/psum | solution.py:164
  234.6 0.7 copy-start.2
  443.8 2.0 copy-start
  907.3 5.8 copy-start.1
Sparse Core Ops, SparseCore 0:
  234.7 190.6 all-reduce.2

commit v6 on v2

--- a/solution.py
+++ b/solution.py
@@ -26,7 +26,7 @@
     local_en.start()
     sends = []
     for k in range(1, n):
-        t = lax.rem(me + k, n)
+        t = jnp.bitwise_xor(me, jnp.where(col == 0, k, n - k))
         dev = (t, col, slab)
         c = pltpu.make_async_remote_copy(
             src_ref=piece(t), dst_ref=cols_ref.at[me],
@@ -40,7 +40,7 @@
         e.start()
         sends.append((c, e))
     for k in range(1, n):
-        s = lax.rem(me + n - k, n)
+        s = jnp.bitwise_xor(me, k)
         dev = (s, col, slab)
         pltpu.make_async_remote_copy(
             src_ref=piece(me), dst_ref=cols_ref.at[s],

time: 802 us -> 704 us (0.88)
  Pallas kernels: 186 us -> 125 us
  waiting for transfers between devices: 176 us -> 138 us
    pallas_call x1, Pallas kernels: 186 us -> 125 us  [exchange(): pl.pallas_call(functools.partial(exchange_kernel, n, width), out_shape=(j...]
    psum x1, waiting for transfers between devices: 176 us -> 138 us  [shards(): gram = lax.psum(partial_gram, ('smp', 'col', 'slab'))]
where the time goes in v6:
time: 704 us; the launch traced here: 698 us
  other arithmetic  278 us (39%)
  waiting for transfers between devices  138 us (20%)
  Pallas kernels  125 us (18%)
  matrix products  79.9 us (11%)
  local copies, waits for them, and re-layouts  55.5 us (8%)
  between operations  20.8 us (3%)
    another operation x30, other arithmetic, shards(): jnp.linalg.cholesky(gram + shift * jnp.eye(samples, dtype=jnp.float32))  167 us
    psum x1, waiting for transfers between devices, shards(): gram = lax.psum(partial_gram, ('smp', 'col', 'slab'))  138 us
    pallas_call x1, Pallas kernels, exchange(): pl.pallas_call(functools.partial(exchange_kernel, n, width), out_shape=(j...  125 us
    another operation x3, other arithmetic, shards(): lax.linalg.triangular_solve(factor, middle, left_side=True, lower=True, t...  83.6 us
    another operation x14, matrix products, shards(): jnp.linalg.cholesky(gram + shift * jnp.eye(samples, dtype=jnp.float32))  27.2 us
    another operation x40, local copies, waits for them, and re-layouts  24.2 us
    dot_general x1, matrix products, shards(): jnp.dot(centered, centered.T, preferred_element_type=jnp.float32)  24.1 us
    unnamed x25, local copies, waits for them, and re-layouts  15.2 us
  transfers between devices with their start and end apart: 1, of which 1 were waited for; matrix products, arithmetic and copies ran while one was open for 2% of the time, Pallas kernels for 0%

profile of v6, /device:TPU:8, one launch (start us, length us, event | category | flops | bytes accessed | tf_op | source)
XLA Modules:
  0.0 698.0 jit_solution(6239516851526093918)
XLA Ops:
  6.5 125.5 %shard_map.28 = (bf16[32,32,16,256]{3,2,1,0:T(8,128)(2,1)}, f32[32,1,32]{2,1,0:T(1,128)}) custom-call(bf16[32,16,8192]{2,1,0:T(8,128)(2,1)} %jac_ref.1, f32[1,32]{1,0:T(1,128)} %bitcast.342), custom_call_target="tpu_custom_call" | custom-call | tf_op jit(solution)/shard_map/pallas_call | solution.py:64
  132.0 4.5 convert_reduce_fusion
  136.6 8.9 %fusion.1 = bf16[32,32,16,256]{3,2,1,0:T(8,128)(2,1)} fusion(bf16[32,32,16,256]{3,2,1,0:T(8,128)(2,1)} %get-tuple-element.7, f32[16,256]{1,0:T(8,128)S(1)} %broadcast_multiply_fusion.1), kind=kLoop, calls=%fused_computation.5 | loop fusion | flops 16777216 | bytes 16793600 | tf_op jit(solution)/shard_map/convert_element_type | solution.py:95
  145.5 24.1 %fusion.5 = f32[1024,1024]{0,1:T(8,128)} fusion(bf16[1024,16,256]{2,1,0:T(8,128)(2,1)} %bitcast.328), kind=kOutput, calls=%fused_computation.15 | convolution fusion | flops 8589934592 | bytes 12582912 | tf_op jit(solution)/shard_map/dot_general | solution.py:97
  172.3 12.2 %copy.34 = bf16[128,8,16,256]{3,1,2,0:T(8,128)(2,1)} copy(bf16[128,8,16,256]{3,2,1,0:T(8,128)(2,1)} %bitcast.329) | data formatting | bytes 16777216
  184.5 138.2 %all-reduce.3.cloned.1.call-done = f32[1024,1024]{0,1:T(8,128)} async-done(((f32[1024,1024]{0,1:T(8,128)}), f32[1024,1024]{0,1:T(8,128)}) %all-reduce.3.cloned.1.call-update) | async-done | bytes 4194320 | tf_op jit(solution)/shard_map/psum | solution.py:98
  326.1 4.8 select_add_fusion
  331.0 5.6 copy.6
  336.5 4.5 fusion.4
  343.0 11.7 %cholesky.222 = f32[128,128]{1,0:T(8,128)S(1)} custom-call(f32[128,128]{1,0:T(8,128)S(1)} %cholesky.577), custom_call_target="Cholesky" | custom-call | tf_op jit(solution)/shard_map/jit(cholesky)/cholesky | solution.py:100
  354.9 9.8 %custom-call.64 = f32[1,128,128]{1,2,0:T(8,128)S(1)} custom-call(f32[1,128,128]{2,1,0:T(8,128)S(1)} %get-tuple-element.52), custom_call_target="InvertDiagBlocksLowerTriangular" | custom-call | tf_op jit(solution)/shard_map/jit(cholesky)/cholesky | solution.py:100
  368.0 11.7 %cholesky.243 = f32[128,128]{1,0:T(8,128)S(1)} custom-call(f32[128,128]{1,0:T(8,128)S(1)} %cholesky.581), custom_call_target="Cholesky" | custom-call | tf_op jit(solution)/shard_map/jit(cholesky)/cholesky | solution.py:100
  382.7 9.8 %custom-call.65 = f32[1,128,128]{1,2,0:T(8,128)S(1)} custom-call(f32[1,128,128]{2,1,0:T(8,128)S(1)} %get-tuple-element.50), custom_call_target="InvertDiagBlocksLowerTriangular" | custom-call | tf_op jit(solution)/shard_map/jit(cholesky)/cholesky | solution.py:100
  398.0 11.7 %cholesky.466 = f32[128,128]{1,0:T(8,128)S(1)} custom-call(f32[128,128]{1,0:T(8,128)S(1)} %cholesky.586), custom_call_target="Cholesky" | custom-call | tf_op jit(solution)/shard_map/jit(cholesky)/cholesky | solution.py:100
  410.5 9.8 %custom-call.66 = f32[1,128,128]{1,2,0:T(8,128)S(1)} custom-call(f32[1,128,128]{2,1,0:T(8,128)S(1)} %get-tuple-element.48), custom_call_target="InvertDiagBlocksLowerTriangular" | custom-call | tf_op jit(solution)/shard_map/jit(cholesky)/cholesky | solution.py:100
  421.6 3.3 convolution_subtract_fusion.2
  424.9 11.7 %cholesky.485 = f32[128,128]{1,0:T(8,128)S(1)} custom-call(f32[128,128]{1,0:T(8,128)S(1)} %cholesky.591), custom_call_target="Cholesky" | custom-call | tf_op jit(solution)/shard_map/jit(cholesky)/cholesky | solution.py:100
  437.4 9.8 %custom-call.67 = f32[1,128,128]{1,2,0:T(8,128)S(1)} custom-call(f32[1,128,128]{2,1,0:T(8,128)S(1)} %get-tuple-element.46), custom_call_target="InvertDiagBlocksLowerTriangular" | custom-call | tf_op jit(solution)/shard_map/jit(cholesky)/cholesky | solution.py:100
  448.3 3.2 convolution_subtract_fusion.3
  451.5 11.9 %cholesky.504 = f32[128,128]{1,0:T(8,128)S(1)} custom-call(f32[128,128]{1,0:T(8,128)S(1)} %cholesky.596), custom_call_target="Cholesky" | custom-call | tf_op jit(solution)/shard_map/jit(cholesky)/cholesky | solution.py:100
  464.2 9.8 %custom-call.68 = f32[1,128,128]{1,2,0:T(8,128)S(1)} custom-call(f32[1,128,128]{2,1,0:T(8,128)S(1)} %get-tuple-element.44), custom_call_target="InvertDiagBlocksLowerTriangular" | custom-call | tf_op jit(solution)/shard_map/jit(cholesky)/cholesky | solution.py:100
  475.1 3.1 convolution_subtract_fusion.4
  478.2 11.7 %cholesky.524 = f32[128,128]{1,0:T(8,128)S(1)} custom-call(f32[128,128]{1,0:T(8,128)S(1)} %cholesky.601), custom_call_target="Cholesky" | custom-call | tf_op jit(solution)/shard_map/jit(cholesky)/cholesky | solution.py:100
  490.7 9.8 %custom-call.69 = f32[1,128,128]{1,2,0:T(8,128)S(1)} custom-call(f32[1,128,128]{2,1,0:T(8,128)S(1)} %get-tuple-element.42), custom_call_target="InvertDiagBlocksLowerTriangular" | custom-call | tf_op jit(solution)/shard_map/jit(cholesky)/cholesky | solution.py:100
  501.5 3.1 convolution_subtract_fusion.5
  504.6 11.7 %cholesky.544 = f32[128,128]{1,0:T(8,128)S(1)} custom-call(f32[128,128]{1,0:T(8,128)S(1)} %cholesky.606), custom_call_target="Cholesky" | custom-call | tf_op jit(solution)/shard_map/jit(cholesky)/cholesky | solution.py:100
  517.1 9.8 %custom-call.70 = f32[1,128,128]{1,2,0:T(8,128)S(1)} custom-call(f32[1,128,128]{2,1,0:T(8,128)S(1)} %get-tuple-element.40), custom_call_target="InvertDiagBlocksLowerTriangular" | custom-call | tf_op jit(solution)/shard_map/jit(cholesky)/cholesky | solution.py:100
  529.9 11.7 %cholesky.562 = f32[128,128]{1,0:T(8,128)S(1)} custom-call(f32[128,128]{1,0:T(8,128)S(1)} %convolution_subtract_fusion.6), custom_call_target="Cholesky" | custom-call | tf_op jit(solution)/shard_map/jit(cholesky)/cholesky | solution.py:100
  551.8 4.9 select_select_fusion
  556.7 24.5 %while.1 = (s32[]{:T(128)}, f32[1024,1024]{0,1:T(8,128)}, s32[8,2]{0,1:T(2,128)S(1)}, f32[8,128,128]{2,1,0:T(8,128)S(1)}, s32[]{:T(128)}) while((s32[]{:T(128)}, f32[1024,1024]{0,1:T(8,128)}, s32[8,2]{0,1:T(2,128)S(1)}, f32[8,128,128]{2,1,0:T(8,128)S(1)}, s32[]{:T(128)}) %tuple.56), condition=%wide.while_cond, body=%wide.while_body.sunk | while | flops 2 | bytes 393329 | solution.py:102
  581.2 78.8 %custom-call.71 = f32[8,128,128]{1,2,0:T(8,128)S(1)} custom-call(f32[8,128,128]{2,1,0:T(8,128)S(1)} %get-tuple-element.16), custom_call_target="InvertDiagBlocksLowerTriangular" | custom-call | tf_op jit(solution)/shard_map/triangular_solve | solution.py:102
  680.9 5.8 fusion.124
  (170 shorter events, 84.2 us)
Async XLA Ops:
  6.5 316.1 %all-reduce.3.cloned.1.call-start = ((), (), s32[]{:S(2)}) async-start(), calls=%async_computation | async-start | bytes 8388608 | tf_op jit(solution)/shard_map/psum | solution.py:98
  169.5 0.7 copy-start.2
  341.0 2.0 copy-start.1
  680.9 5.8 copy-start
Sparse Core Ops, SparseCore 0:
  169.7 152.9 all-reduce.2

commit v7 on v6

--- a/solution.py
+++ b/solution.py
@@ -20,6 +20,11 @@
     def piece(t):
         return jac_ref.at[:, :, pl.ds(pl.multiple_of(t * width, width), width)]
 
+    barrier = pltpu.get_barrier_semaphore()
+    for k in range(1, n):
+        pl.semaphore_signal(barrier, inc=1, device_id=(jnp.bitwise_xor(me, k), col, slab),
+                            device_id_type=pl.DeviceIdType.MESH)
+    pl.semaphore_wait(barrier, n - 1)
     local = pltpu.make_async_copy(piece(me), cols_ref.at[me], local_sems.at[0])
     local.start()
     local_en = pltpu.make_async_copy(en_ref, en_all_ref.at[me], local_sems.at[1])
@@ -76,7 +81,7 @@
             pltpu.SemaphoreType.DMA((n,)),
             pltpu.SemaphoreType.DMA((2,)),
         ],
-        compiler_params=pltpu.CompilerParams(has_side_effects=True),
+        compiler_params=pltpu.CompilerParams(collective_id=0, has_side_effects=True),
     )(jacobian, en)
 
 
@@ -97,7 +102,8 @@
     partial_gram = jnp.dot(centered, centered.T, preferred_element_type=jnp.float32)
     gram = lax.psum(partial_gram, ("smp", "col", "slab"))
     shift = 0.01 * jnp.trace(gram) / samples
-    factor = jnp.linalg.cholesky(gram + shift * jnp.eye(samples, dtype=jnp.float32))
+    factor = lax.linalg.cholesky(gram + shift * jnp.eye(samples, dtype=jnp.float32),
+                                 symmetrize_input=False)
     middle = lax.linalg.triangular_solve(factor, eps[:, None], left_side=True, lower=True)
     coeffs = lax.linalg.triangular_solve(
         factor, middle, left_side=True, lower=True, transpose_a=True

time: 704 us -> 686 us (0.974)
  local copies, waits for them, and re-layouts: 55.5 us -> 42.5 us
    pallas_call x1, Pallas kernels: 125 us -> 118 us  [exchange(): pl.pallas_call(functools.partial(exchange_kernel, n, width), out_shape=(j...]
    another operation x65 -> x32, local copies, waits for them, and re-layouts: 33.5 us -> 26 us
where the time goes in v7:
time: 686 us; the launch traced here: 680 us
  other arithmetic  276 us (40%)
  waiting for transfers between devices  141 us (21%)
  Pallas kernels  118 us (17%)
  matrix products  81.4 us (12%)
  local copies, waits for them, and re-layouts  42.5 us (6%)
  between operations  20.8 us (3%)
    another operation x30, other arithmetic, shards(): lax.linalg.cholesky(gram + shift * jnp.eye(samples, dtype=jnp.float32), s...  173 us
    psum x1, waiting for transfers between devices, shards(): gram = lax.psum(partial_gram, ('smp', 'col', 'slab'))  141 us
    pallas_call x1, Pallas kernels, exchange(): pl.pallas_call(functools.partial(exchange_kernel, n, width), out_shape=(j...  118 us
    another operation x3, other arithmetic, shards(): lax.linalg.triangular_solve(factor, middle, left_side=True, lower=True, t...  83.4 us
    dot_general x1, matrix products, shards(): jnp.dot(centered, centered.T, preferred_element_type=jnp.float32)  28.3 us
    another operation x24, local copies, waits for them, and re-layouts  23.4 us
    another operation x14, matrix products, shards(): lax.linalg.cholesky(gram + shift * jnp.eye(samples, dtype=jnp.float32), s...  23.1 us
    unnamed x25, local copies, waits for them, and re-layouts  15.2 us
  transfers between devices with their start and end apart: 1, of which 1 were waited for; matrix products, arithmetic and copies ran while one was open for 2% of the time, Pallas kernels for 0%

profile of v7, /device:TPU:8, one launch (start us, length us, event | category | flops | bytes accessed | tf_op | source)
XLA Modules:
  0.0 680.0 jit_solution(13346487171752106119)
XLA Ops:
  6.5 117.6 %shard_map.28 = (bf16[32,32,16,256]{3,2,1,0:T(8,128)(2,1)}, f32[32,1,32]{2,1,0:T(1,128)}) custom-call(bf16[32,16,8192]{2,1,0:T(8,128)(2,1)} %jac_ref.1, f32[1,32]{1,0:T(1,128)} %bitcast.340), custom_call_target="tpu_custom_call" | custom-call | tf_op jit(solution)/shard_map/pallas_call | solution.py:69
  124.1 4.5 convert_reduce_fusion
  128.7 8.9 %fusion.1 = bf16[32,32,16,256]{3,2,1,0:T(8,128)(2,1)} fusion(bf16[32,32,16,256]{3,2,1,0:T(8,128)(2,1)} %get-tuple-element.7, f32[16,256]{1,0:T(8,128)S(1)} %broadcast_multiply_fusion.1), kind=kLoop, calls=%fused_computation.5 | loop fusion | flops 16777216 | bytes 16793600 | tf_op jit(solution)/shard_map/convert_element_type | solution.py:100
  137.6 28.3 %fusion.4 = f32[1024,1024]{1,0:T(8,128)} fusion(bf16[1024,16,256]{2,1,0:T(8,128)(2,1)} %bitcast.326), kind=kOutput, calls=%fused_computation.13 | convolution fusion | flops 8589934592 | bytes 12582912 | tf_op jit(solution)/shard_map/dot_general | solution.py:102
  168.7 12.2 %copy.7 = bf16[128,8,16,256]{3,1,2,0:T(8,128)(2,1)} copy(bf16[128,8,16,256]{3,2,1,0:T(8,128)(2,1)} %bitcast.327) | data formatting | bytes 16777216
  181.0 141.1 %all-reduce.3.cloned.1.call-done = f32[1024,1024]{1,0:T(8,128)} async-done(((f32[1024,1024]{1,0:T(8,128)}), f32[1024,1024]{1,0:T(8,128)}) %all-reduce.3.cloned.1.call-update) | async-done | bytes 4194320 | tf_op jit(solution)/shard_map/psum | solution.py:103
  322.1 2.9 select_reduce_fusion
  325.6 2.6 select_add_fusion
  330.1 11.7 %cholesky.222 = f32[128,128]{1,0:T(8,128)S(1)} custom-call(f32[128,128]{1,0:T(8,128)S(1)} %cholesky.577), custom_call_target="Cholesky" | custom-call | tf_op jit(solution)/shard_map/cholesky | solution.py:105
  341.9 2.5 cholesky.254
  344.3 10.2 %custom-call.49 = f32[1,128,128]{1,2,0:T(8,128)S(1)} custom-call(f32[1,128,128]{2,1,0:T(8,128)S(1)} %get-tuple-element.56), custom_call_target="InvertDiagBlocksLowerTriangular" | custom-call | tf_op jit(solution)/shard_map/cholesky | solution.py:105
  354.5 2.4 constant_dynamic-update-slice_fusion.50
  358.5 11.7 %cholesky.243 = f32[128,128]{1,0:T(8,128)S(1)} custom-call(f32[128,128]{1,0:T(8,128)S(1)} %cholesky.581), custom_call_target="Cholesky" | custom-call | tf_op jit(solution)/shard_map/cholesky | solution.py:105
  370.9 9.8 %custom-call.50 = f32[1,128,128]{1,2,0:T(8,128)S(1)} custom-call(f32[1,128,128]{2,1,0:T(8,128)S(1)} %get-tuple-element.53), custom_call_target="InvertDiagBlocksLowerTriangular" | custom-call | tf_op jit(solution)/shard_map/cholesky | solution.py:105
  384.0 11.9 %cholesky.466 = f32[128,128]{1,0:T(8,128)S(1)} custom-call(f32[128,128]{1,0:T(8,128)S(1)} %cholesky.586), custom_call_target="Cholesky" | custom-call | tf_op jit(solution)/shard_map/cholesky | solution.py:105
  397.2 9.8 %custom-call.51 = f32[1,128,128]{1,2,0:T(8,128)S(1)} custom-call(f32[1,128,128]{2,1,0:T(8,128)S(1)} %get-tuple-element.50), custom_call_target="InvertDiagBlocksLowerTriangular" | custom-call | tf_op jit(solution)/shard_map/cholesky | solution.py:105
  408.2 2.3 convolution_subtract_fusion.2
  410.6 11.7 %cholesky.485 = f32[128,128]{1,0:T(8,128)S(1)} custom-call(f32[128,128]{1,0:T(8,128)S(1)} %cholesky.591), custom_call_target="Cholesky" | custom-call | tf_op jit(solution)/shard_map/cholesky | solution.py:105
  423.6 9.8 %custom-call.52 = f32[1,128,128]{1,2,0:T(8,128)S(1)} custom-call(f32[1,128,128]{2,1,0:T(8,128)S(1)} %get-tuple-element.47), custom_call_target="InvertDiagBlocksLowerTriangular" | custom-call | tf_op jit(solution)/shard_map/cholesky | solution.py:105
  434.5 2.3 convolution_subtract_fusion.3
  436.8 11.9 %cholesky.504 = f32[128,128]{1,0:T(8,128)S(1)} custom-call(f32[128,128]{1,0:T(8,128)S(1)} %cholesky.596), custom_call_target="Cholesky" | custom-call | tf_op jit(solution)/shard_map/cholesky | solution.py:105
  450.0 9.8 %custom-call.53 = f32[1,128,128]{1,2,0:T(8,128)S(1)} custom-call(f32[1,128,128]{2,1,0:T(8,128)S(1)} %get-tuple-element.44), custom_call_target="InvertDiagBlocksLowerTriangular" | custom-call | tf_op jit(solution)/shard_map/cholesky | solution.py:105
  463.2 11.7 %cholesky.524 = f32[128,128]{1,0:T(8,128)S(1)} custom-call(f32[128,128]{1,0:T(8,128)S(1)} %cholesky.601), custom_call_target="Cholesky" | custom-call | tf_op jit(solution)/shard_map/cholesky | solution.py:105
  476.2 10.2 %custom-call.54 = f32[1,128,128]{1,2,0:T(8,128)S(1)} custom-call(f32[1,128,128]{2,1,0:T(8,128)S(1)} %get-tuple-element.41), custom_call_target="InvertDiagBlocksLowerTriangular" | custom-call | tf_op jit(solution)/shard_map/cholesky | solution.py:105
  489.4 11.7 %cholesky.544 = f32[128,128]{1,0:T(8,128)S(1)} custom-call(f32[128,128]{1,0:T(8,128)S(1)} %cholesky.606), custom_call_target="Cholesky" | custom-call | tf_op jit(solution)/shard_map/cholesky | solution.py:105
  502.4 9.8 %custom-call.55 = f32[1,128,128]{1,2,0:T(8,128)S(1)} custom-call(f32[1,128,128]{2,1,0:T(8,128)S(1)} %get-tuple-element.38), custom_call_target="InvertDiagBlocksLowerTriangular" | custom-call | tf_op jit(solution)/shard_map/cholesky | solution.py:105
  514.9 11.9 %cholesky.562 = f32[128,128]{1,0:T(8,128)S(1)} custom-call(f32[128,128]{1,0:T(8,128)S(1)} %convolution_subtract_fusion.6), custom_call_target="Cholesky" | custom-call | tf_op jit(solution)/shard_map/cholesky | solution.py:105
  533.6 4.8 select_select_fusion
  538.4 23.6 %while.1 = (s32[]{:T(128)}, f32[1024,1024]{1,0:T(8,128)}, s32[8,2]{0,1:T(2,128)S(1)}, f32[8,128,128]{2,1,0:T(8,128)S(1)}, s32[]{:T(128)}) while((s32[]{:T(128)}, f32[1024,1024]{1,0:T(8,128)}, s32[8,2]{0,1:T(2,128)S(1)}, f32[8,128,128]{2,1,0:T(8,128)S(1)}, s32[]{:T(128)}) %tuple.63), condition=%wide.while_cond, body=%wide.while_body.sunk | while | flops 2 | bytes 131181 | solution.py:108
  562.0 78.6 %custom-call.56 = f32[8,128,128]{1,2,0:T(8,128)S(1)} custom-call(f32[8,128,128]{2,1,0:T(8,128)S(1)} %get-tuple-element.16), custom_call_target="InvertDiagBlocksLowerTriangular" | custom-call | tf_op jit(solution)/shard_map/triangular_solve | solution.py:108
  661.7 3.6 fusion.122
  666.7 5.7 fusion.123
  (135 shorter events, 75.1 us)
Async XLA Ops:
  6.5 315.5 %all-reduce.3.cloned.1.call-start = ((), (), s32[]{:S(2)}) async-start(), calls=%async_computation | async-start | bytes 8388608 | tf_op jit(solution)/shard_map/psum | solution.py:103
  165.9 0.7 copy-start.2
  328.1 2.0 copy-start.1
  640.6 21.1 %copy-start = (f32[1024,1024]{1,0:T(8,128)S(1)}, f32[1024,1024]{1,0:T(8,128)}, u32[]{:S(2)}) copy-start(f32[1024,1024]{1,0:T(8,128)} %all-reduce.3.cloned.1.call-done) | copy-start | bytes 12582916
Sparse Core Ops, SparseCore 0:
  166.0 156.0 all-reduce.2

commit v8 on v7

--- a/solution.py
+++ b/solution.py
@@ -83,6 +83,118 @@
         ],
         compiler_params=pltpu.CompilerParams(collective_id=0, has_side_effects=True),
     )(jacobian, en)
+
+
+def reduce_kernel(n, parts, p_ref, out_ref, rs_buf, ar_buf, acc_ref, rs_send, rs_recv,
+                  ar_send, ar_recv, ag_send, ag_recv, local_sem):
+    me = lax.axis_index("smp")
+    col = lax.axis_index("col")
+    slab = lax.axis_index("slab")
+    cs = col * 2 + slab
+    mesh_id = pl.DeviceIdType.MESH
+
+    def peer(k):
+        return jnp.bitwise_xor(me, jnp.where(col == 0, k, n - k))
+
+    barrier = pltpu.get_barrier_semaphore()
+    for k in range(1, n):
+        pl.semaphore_signal(barrier, inc=1, device_id=(jnp.bitwise_xor(me, k), col, slab),
+                            device_id_type=mesh_id)
+    for k in range(1, parts):
+        other = jnp.bitwise_xor(cs, k)
+        pl.semaphore_signal(barrier, inc=1, device_id=(me, other // 2, other % 2),
+                            device_id_type=mesh_id)
+    pl.semaphore_wait(barrier, n - 1 + parts - 1)
+
+    sends = []
+    for k in range(1, n):
+        t = peer(k)
+        c = pltpu.make_async_remote_copy(
+            src_ref=p_ref.at[t], dst_ref=rs_buf.at[me], send_sem=rs_send.at[t],
+            recv_sem=rs_recv.at[me], device_id=(t, col, slab), device_id_type=mesh_id)
+        c.start()
+        sends.append(c)
+    rs_buf[pl.ds(me, 1)] = p_ref[pl.ds(me, 1)]
+    for k in range(1, n):
+        s = jnp.bitwise_xor(me, k)
+        pltpu.make_async_remote_copy(
+            src_ref=p_ref.at[s], dst_ref=rs_buf.at[s], send_sem=rs_send.at[s],
+            recv_sem=rs_recv.at[s], device_id=(s, col, slab), device_id_type=mesh_id).wait_recv()
+    total = rs_buf[0]
+    for s in range(1, n):
+        total = total + rs_buf[s]
+    ar_buf[pl.ds(cs, 1)] = total[None]
+    for k in range(1, parts):
+        other = jnp.bitwise_xor(cs, k)
+        c = pltpu.make_async_remote_copy(
+            src_ref=ar_buf.at[cs], dst_ref=ar_buf.at[cs], send_sem=ar_send.at[other],
+            recv_sem=ar_recv.at[cs], device_id=(me, other // 2, other % 2), device_id_type=mesh_id)
+        c.start()
+        sends.append(c)
+    for k in range(1, parts):
+        other = jnp.bitwise_xor(cs, k)
+        pltpu.make_async_remote_copy(
+            src_ref=ar_buf.at[other], dst_ref=ar_buf.at[other], send_sem=ar_send.at[other],
+            recv_sem=ar_recv.at[other], device_id=(me, other // 2, other % 2),
+            device_id_type=mesh_id).wait_recv()
+    total = ar_buf[0]
+    for j in range(1, parts):
+        total = total + ar_buf[j]
+    acc_ref[...] = total
+    local = pltpu.make_async_copy(acc_ref, out_ref.at[me], local_sem.at[0])
+    local.start()
+    for k in range(1, n):
+        t = peer(k)
+        c = pltpu.make_async_remote_copy(
+            src_ref=acc_ref, dst_ref=out_ref.at[me], send_sem=ag_send.at[t],
+            recv_sem=ag_recv.at[me], device_id=(t, col, slab), device_id_type=mesh_id)
+        c.start()
+        sends.append(c)
+    for k in range(1, n):
+        s = jnp.bitwise_xor(me, k)
+        pltpu.make_async_remote_copy(
+            src_ref=acc_ref, dst_ref=out_ref.at[s], send_sem=ag_send.at[s],
+            recv_sem=ag_recv.at[s], device_id=(s, col, slab), device_id_type=mesh_id).wait_recv()
+    for c in sends:
+        c.wait_send()
+    local.wait()
+
+
+def lower_psum(partial, n, parts, block=128):
+    size = partial.shape[0]
+    nb = size // block
+    pairs = [(i, j) for i in range(nb) for j in range(i + 1)]
+    packed = jnp.concatenate(
+        [partial[i * block:(i + 1) * block, j * block:(j + 1) * block] for i, j in pairs], axis=0)
+    rows = packed.shape[0] // n
+    packed = packed.reshape(n, rows, block)
+    reduced = pl.pallas_call(
+        functools.partial(reduce_kernel, n, parts),
+        out_shape=jax.ShapeDtypeStruct((n, rows, block), jnp.float32),
+        in_specs=[pl.BlockSpec(memory_space=pltpu.VMEM)],
+        out_specs=pl.BlockSpec(memory_space=pl.ANY),
+        scratch_shapes=[
+            pltpu.VMEM((n, rows, block), jnp.float32),
+            pltpu.VMEM((parts, rows, block), jnp.float32),
+            pltpu.VMEM((rows, block), jnp.float32),
+            pltpu.SemaphoreType.DMA((n,)),
+            pltpu.SemaphoreType.DMA((n,)),
+            pltpu.SemaphoreType.DMA((parts,)),
+            pltpu.SemaphoreType.DMA((parts,)),
+            pltpu.SemaphoreType.DMA((n,)),
+            pltpu.SemaphoreType.DMA((n,)),
+            pltpu.SemaphoreType.DMA((1,)),
+        ],
+        compiler_params=pltpu.CompilerParams(collective_id=1, has_side_effects=True),
+    )(packed)
+    blocks = reduced.reshape(len(pairs), block, block)
+    where = {p: k for k, p in enumerate(pairs)}
+    zero = jnp.zeros((block, block), jnp.float32)
+    lower = jnp.concatenate([
+        jnp.concatenate([blocks[where[(i, j)]] if j <= i else zero for j in range(nb)], axis=1)
+        for i in range(nb)], axis=0)
+    diag = jnp.stack([blocks[where[(i, i)]] for i in range(nb)])
+    return lower, diag
 
 
 def shards(n, jacobian, local_energy):
@@ -100,7 +212,8 @@
         ((values - mean_row) / root_count).astype(jnp.bfloat16).reshape(samples, slab_count * width)
     )
     partial_gram = jnp.dot(centered, centered.T, preferred_element_type=jnp.float32)
-    gram = lax.psum(partial_gram, ("smp", "col", "slab"))
+    parts = lax.psum(1, ("col", "slab"))
+    gram, diag = lower_psum(partial_gram, n, parts)
     shift = 0.01 * jnp.trace(gram) / samples
     factor = lax.linalg.cholesky(gram + shift * jnp.eye(samples, dtype=jnp.float32),
                                  symmetrize_input=False)
@@ -109,8 +222,11 @@
         factor, middle, left_side=True, lower=True, transpose_a=True
     )[:, 0]
     delta = jnp.dot(coeffs, centered.astype(jnp.float32), precision=lax.Precision.HIGHEST)
-    squared = jnp.dot(coeffs, jnp.dot(gram, coeffs, precision=lax.Precision.HIGHEST),
-                      precision=lax.Precision.HIGHEST)
+    hi = lax.Precision.HIGHEST
+    blocked = coeffs.reshape(diag.shape[0], diag.shape[1])
+    full_c = (jnp.dot(gram, coeffs, precision=hi) + jnp.dot(coeffs, gram, precision=hi)
+              - jnp.einsum("bij,bj->bi", diag, blocked, precision=hi).reshape(-1))
+    squared = jnp.dot(coeffs, full_c, precision=hi)
     limit = 0.3 * jnp.sqrt(jnp.float32(SLABS * SLAB_COLS))
     scaled = -jnp.minimum(1.0, limit / jnp.sqrt(squared)) * delta
     return scaled.reshape(slab_count, width)

time: 686 us -> 614 us (0.90)
  waiting for transfers between devices: 141 us -> 0 us
  Pallas kernels: 118 us -> 195 us
  local copies, waits for them, and re-layouts: 42.5 us -> 55.6 us
  between operations: 20.8 us -> 8.33 us
  matrix products: 81.4 us -> 72.7 us
    psum x1 -> x0, waiting for transfers between devices: 141 us -> none  [shards(): gram = lax.psum(partial_gram, ('smp', 'col', 'slab'))]
    pallas_call x0 -> x1, Pallas kernels: none -> 77.1 us  [lower_psum(): pl.pallas_call(functools.partial(reduce_kernel, n, parts), out_shape=jax....]
    dot_general x1, matrix products: 28.3 us -> 13.9 us  [shards(): jnp.dot(centered, centered.T, preferred_element_type=jnp.float32)]
    unnamed x25 -> x106, local copies, waits for them, and re-layouts: 15.2 us -> 27.3 us
    another operation x24 -> x25, local copies, waits for them, and re-layouts: 23.4 us -> 24.3 us
  transfers between devices with their start and end apart: 1 -> 0, of which waited for: 1 -> 0; matrix products, arithmetic and copies ran while one was open for 2% -> 0% of each run, Pallas kernels for 0% -> 0%
where the time goes in v8:
time: 614 us; the launch traced here: 605 us
  other arithmetic  274 us (45%)
  Pallas kernels  195 us (32%)
  matrix products  72.7 us (12%)
  local copies, waits for them, and re-layouts  55.6 us (9%)
  between operations  8.33 us (1%)
    another operation x30, other arithmetic, shards(): lax.linalg.cholesky(gram + shift * jnp.eye(samples, dtype=jnp.float32), s...  172 us
    pallas_call x1, Pallas kernels, exchange(): pl.pallas_call(functools.partial(exchange_kernel, n, width), out_shape=(j...  118 us
    another operation x3, other arithmetic, shards(): lax.linalg.triangular_solve(factor, middle, left_side=True, lower=True, t...  83.8 us
    pallas_call x1, Pallas kernels, lower_psum(): pl.pallas_call(functools.partial(reduce_kernel, n, parts), out_shape=jax....  77.1 us
    unnamed x106, local copies, waits for them, and re-layouts  27.3 us
    another operation x14, matrix products, shards(): lax.linalg.cholesky(gram + shift * jnp.eye(samples, dtype=jnp.float32), s...  23.6 us
    another operation x24, local copies, waits for them, and re-layouts  23.3 us
    dot_general x1, matrix products, shards(): jnp.dot(centered, centered.T, preferred_element_type=jnp.float32)  13.9 us

profile of v8, /device:TPU:8, one launch (start us, length us, event | category | flops | bytes accessed | tf_op | source)
XLA Modules:
  0.0 605.3 jit_solution(5095091881013923835)
XLA Ops:
  0.0 117.6 %shard_map.28 = (bf16[32,32,16,256]{3,2,1,0:T(8,128)(2,1)}, f32[32,1,32]{2,1,0:T(1,128)}) custom-call(bf16[32,16,8192]{2,1,0:T(8,128)(2,1)} %jac_ref.1, f32[1,32]{1,0:T(1,128)} %bitcast.520), custom_call_target="tpu_custom_call" | custom-call | tf_op jit(solution)/shard_map/pallas_call | solution.py:69
  117.6 4.5 convert_reduce_fusion
  122.1 8.9 %fusion.1 = bf16[32,32,16,256]{3,2,1,0:T(8,128)(2,1)} fusion(bf16[32,32,16,256]{3,2,1,0:T(8,128)(2,1)} %get-tuple-element.7, f32[16,256]{1,0:T(8,128)S(1)} %broadcast_multiply_fusion.1), kind=kLoop, calls=%fused_computation.5 | loop fusion | flops 16777216 | bytes 16793600 | tf_op jit(solution)/shard_map/convert_element_type | solution.py:212
  131.0 13.9 %fusion.4 = f32[1024,1024]{1,0:T(8,128)S(1)} fusion(bf16[1024,16,256]{2,1,0:T(8,128)(2,1)} %bitcast.465), kind=kOutput, calls=%fused_computation.13 | convolution fusion | flops 8589934592 | bytes 12582912 | tf_op jit(solution)/shard_map/dot_general | solution.py:214
  147.1 77.1 %shard_map.29 = f32[32,144,128]{2,1,0:T(8,128)} custom-call(f32[32,144,128]{2,1,0:T(8,128)} %bitcast.505), custom_call_target="tpu_custom_call" | custom-call | tf_op jit(solution)/shard_map/pallas_call | solution.py:171
  237.9 2.6 select_add_fusion
  242.5 11.7 %cholesky.221 = f32[128,128]{1,0:T(8,128)S(1)} custom-call(f32[128,128]{1,0:T(8,128)S(1)} %cholesky.574), custom_call_target="Cholesky" | custom-call | tf_op jit(solution)/shard_map/cholesky | solution.py:218
  254.2 2.5 cholesky.250
  256.7 9.8 %custom-call.49 = f32[1,128,128]{1,2,0:T(8,128)S(1)} custom-call(f32[1,128,128]{2,1,0:T(8,128)S(1)} %get-tuple-element.63), custom_call_target="InvertDiagBlocksLowerTriangular" | custom-call | tf_op jit(solution)/shard_map/cholesky | solution.py:218
  266.5 2.3 constant_dynamic-update-slice_fusion.98
  270.4 11.9 %cholesky.241 = f32[128,128]{1,0:T(8,128)S(1)} custom-call(f32[128,128]{1,0:T(8,128)S(1)} %cholesky.578), custom_call_target="Cholesky" | custom-call | tf_op jit(solution)/shard_map/cholesky | solution.py:218
  284.9 9.8 %custom-call.50 = f32[1,128,128]{1,2,0:T(8,128)S(1)} custom-call(f32[1,128,128]{2,1,0:T(8,128)S(1)} %get-tuple-element.60), custom_call_target="InvertDiagBlocksLowerTriangular" | custom-call | tf_op jit(solution)/shard_map/cholesky | solution.py:218
  298.1 11.7 %cholesky.463 = f32[128,128]{1,0:T(8,128)S(1)} custom-call(f32[128,128]{1,0:T(8,128)S(1)} %cholesky.583), custom_call_target="Cholesky" | custom-call | tf_op jit(solution)/shard_map/cholesky | solution.py:218
  311.7 9.8 %custom-call.51 = f32[1,128,128]{1,2,0:T(8,128)S(1)} custom-call(f32[1,128,128]{2,1,0:T(8,128)S(1)} %get-tuple-element.57), custom_call_target="InvertDiagBlocksLowerTriangular" | custom-call | tf_op jit(solution)/shard_map/cholesky | solution.py:218
  323.2 2.3 convolution_subtract_fusion.2
  325.5 11.7 %cholesky.482 = f32[128,128]{1,0:T(8,128)S(1)} custom-call(f32[128,128]{1,0:T(8,128)S(1)} %cholesky.588), custom_call_target="Cholesky" | custom-call | tf_op jit(solution)/shard_map/cholesky | solution.py:218
  339.2 9.8 %custom-call.52 = f32[1,128,128]{1,2,0:T(8,128)S(1)} custom-call(f32[1,128,128]{2,1,0:T(8,128)S(1)} %get-tuple-element.54), custom_call_target="InvertDiagBlocksLowerTriangular" | custom-call | tf_op jit(solution)/shard_map/cholesky | solution.py:218
  350.1 2.3 convolution_subtract_fusion.3
  352.4 11.8 %cholesky.501 = f32[128,128]{1,0:T(8,128)S(1)} custom-call(f32[128,128]{1,0:T(8,128)S(1)} %cholesky.593), custom_call_target="Cholesky" | custom-call | tf_op jit(solution)/shard_map/cholesky | solution.py:218
  366.2 9.8 %custom-call.53 = f32[1,128,128]{1,2,0:T(8,128)S(1)} custom-call(f32[1,128,128]{2,1,0:T(8,128)S(1)} %get-tuple-element.51), custom_call_target="InvertDiagBlocksLowerTriangular" | custom-call | tf_op jit(solution)/shard_map/cholesky | solution.py:218
  379.3 11.7 %cholesky.521 = f32[128,128]{1,0:T(8,128)S(1)} custom-call(f32[128,128]{1,0:T(8,128)S(1)} %cholesky.598), custom_call_target="Cholesky" | custom-call | tf_op jit(solution)/shard_map/cholesky | solution.py:218
  393.0 9.8 %custom-call.54 = f32[1,128,128]{1,2,0:T(8,128)S(1)} custom-call(f32[1,128,128]{2,1,0:T(8,128)S(1)} %get-tuple-element.48), custom_call_target="InvertDiagBlocksLowerTriangular" | custom-call | tf_op jit(solution)/shard_map/cholesky | solution.py:218
  405.8 11.9 %cholesky.541 = f32[128,128]{1,0:T(8,128)S(1)} custom-call(f32[128,128]{1,0:T(8,128)S(1)} %cholesky.603), custom_call_target="Cholesky" | custom-call | tf_op jit(solution)/shard_map/cholesky | solution.py:218
  419.7 9.8 %custom-call.55 = f32[1,128,128]{1,2,0:T(8,128)S(1)} custom-call(f32[1,128,128]{2,1,0:T(8,128)S(1)} %get-tuple-element.45), custom_call_target="InvertDiagBlocksLowerTriangular" | custom-call | tf_op jit(solution)/shard_map/cholesky | solution.py:218
  432.1 11.7 %cholesky.559 = f32[128,128]{1,0:T(8,128)S(1)} custom-call(f32[128,128]{1,0:T(8,128)S(1)} %convolution_subtract_fusion.6), custom_call_target="Cholesky" | custom-call | tf_op jit(solution)/shard_map/cholesky | solution.py:218
  445.8 4.8 select_select_fusion
  450.6 23.4 %while.1 = (s32[]{:T(128)}, f32[1024,1024]{1,0:T(8,128)}, s32[8,2]{0,1:T(2,128)S(1)}, f32[8,128,128]{2,1,0:T(8,128)S(1)}, s32[]{:T(128)}) while((s32[]{:T(128)}, f32[1024,1024]{1,0:T(8,128)}, s32[8,2]{0,1:T(2,128)S(1)}, f32[8,128,128]{2,1,0:T(8,128)S(1)}, s32[]{:T(128)}) %tuple.69), condition=%wide.while_cond, body=%wide.while_body.sunk | while | flops 2 | bytes 131181 | solution.py:221
  474.0 79.0 %custom-call.56 = f32[8,128,128]{1,2,0:T(8,128)S(1)} custom-call(f32[8,128,128]{2,1,0:T(8,128)S(1)} %get-tuple-element.16), custom_call_target="InvertDiagBlocksLowerTriangular" | custom-call | tf_op jit(solution)/shard_map/triangular_solve | solution.py:221
  576.2 4.3 fusion.145
  580.5 3.6 fusion.144
  586.4 12.4 %copy.9 = bf16[128,8,16,256]{3,1,2,0:T(8,128)(2,1)} copy(bf16[128,8,16,256]{3,2,1,0:T(8,128)(2,1)} %bitcast.466) | data formatting | bytes 16777216
  598.8 5.7 fusion.146
  (225 shorter events, 90.1 us)
Async XLA Ops:
  145.6 1.5 copy-start.4
  224.2 9.9 %copy-start.2 = (f32[32,144,128]{2,1,0:T(8,128)S(1)}, f32[32,144,128]{2,1,0:T(8,128)}, u32[]{:S(2)}) copy-start(f32[32,144,128]{2,1,0:T(8,128)} %shard_map.29) | copy-start | bytes 7077892
  234.6 2.0 copy-start
  240.5 2.0 copy-start.3
  445.8 107.3 %copy-start.5 = (f32[32,1,32]{2,1,0:T(1,128)S(1)}, f32[32,1,32]{2,1,0:T(1,128)}, u32[]{:S(2)}) copy-start(f32[32,1,32]{2,1,0:T(1,128)} %get-tuple-element.8) | copy-start | bytes 12292
  563.9 16.6 %copy-start.1 = (f32[1024,1024]{1,0:T(8,128)S(1)}, f32[1024,1024]{1,0:T(8,128)}, u32[]{:S(2)}) copy-start(f32[1024,1024]{1,0:T(8,128)} %copy-done) | copy-start | bytes 12582916

commit v9 on v8

--- a/solution.py
+++ b/solution.py
@@ -195,6 +195,40 @@
         for i in range(nb)], axis=0)
     diag = jnp.stack([blocks[where[(i, i)]] for i in range(nb)])
     return lower, diag
+
+
+def cholesky_solve(a, rhs, block=128):
+    n = a.shape[0]
+    nb = n // block
+    hi = lax.Precision.HIGHEST
+    eye = jnp.eye(block, dtype=jnp.float32)
+    inverses, panels, factors = [], [], []
+    for k in range(nb):
+        lo = k * block
+        lkk = lax.linalg.cholesky(a[lo:lo + block, lo:lo + block], symmetrize_input=False)
+        inv = lax.linalg.triangular_solve(lkk, eye, left_side=True, lower=True)
+        factors.append(lkk)
+        inverses.append(inv)
+        if k < nb - 1:
+            panel = jnp.dot(a[lo + block:, lo:lo + block], inv.T, precision=hi)
+            panels.append(panel)
+            a = a.at[lo + block:, lo + block:].add(-jnp.dot(panel, panel.T, precision=hi))
+    ys = []
+    for k in range(nb):
+        lo = k * block
+        r = rhs[lo:lo + block]
+        if k > 0:
+            strip = jnp.concatenate(
+                [panels[j][(k - j - 1) * block:(k - j) * block] for j in range(k)], axis=1)
+            r = r - jnp.dot(strip, jnp.concatenate(ys), precision=hi)
+        ys.append(jnp.dot(inverses[k], r, precision=hi))
+    cs = [None] * nb
+    for k in reversed(range(nb)):
+        r = ys[k]
+        if k < nb - 1:
+            r = r - jnp.dot(jnp.concatenate(cs[k + 1:]), panels[k], precision=hi)
+        cs[k] = jnp.dot(r, inverses[k], precision=hi)
+    return jnp.concatenate(cs)
 
 
 def shards(n, jacobian, local_energy):
@@ -215,12 +249,7 @@
     parts = lax.psum(1, ("col", "slab"))
     gram, diag = lower_psum(partial_gram, n, parts)
     shift = 0.01 * jnp.trace(gram) / samples
-    factor = lax.linalg.cholesky(gram + shift * jnp.eye(samples, dtype=jnp.float32),
-                                 symmetrize_input=False)
-    middle = lax.linalg.triangular_solve(factor, eps[:, None], left_side=True, lower=True)
-    coeffs = lax.linalg.triangular_solve(
-        factor, middle, left_side=True, lower=True, transpose_a=True
-    )[:, 0]
+    coeffs = cholesky_solve(gram + shift * jnp.eye(samples, dtype=jnp.float32), eps)
     delta = jnp.dot(coeffs, centered.astype(jnp.float32), precision=lax.Precision.HIGHEST)
     hi = lax.Precision.HIGHEST
     blocked = coeffs.reshape(diag.shape[0], diag.shape[1])

time: 614 us -> 555 us (0.904)
  other arithmetic: 274 us -> 203 us
  local copies, waits for them, and re-layouts: 55.6 us -> 78.3 us
  matrix products: 72.7 us -> 65.7 us
    another operation x33 -> x40, other arithmetic: 256 us -> 184 us  [the longest x24 100 us: cholesky_solve(): lax.linalg.cholesky(a[lo:lo + block, lo:lo + block], symmetrize_input=False)]
    another operation x44 -> x8, matrix products: 44.3 us -> 2.28 us  [cholesky_solve(): inv = lax.linalg.triangular_solve(lkk, eye, left_side=True, lower=True)]
    unnamed x106 -> x147, local copies, waits for them, and re-layouts: 27.3 us -> 62.1 us
    dot_general x0 -> x44, matrix products: none -> 32.8 us  [the longest x7 14 us: cholesky_solve(): jnp.dot(panel, panel.T, precision=hi)]
    another operation x46 -> x0, local copies, waits for them, and re-layouts: 26.6 us -> none
    concatenate x0 -> x15, local copies, waits for them, and re-layouts: none -> 10.6 us  [the longest x7 5.84 us: cholesky_solve(): r = r - jnp.dot(jnp.concatenate(cs[k + 1:]), panels[k], precision=hi)]
where the time goes in v9:
time: 555 us; the launch traced here: 546 us
  other arithmetic  203 us (37%)
  Pallas kernels  195 us (35%)
  local copies, waits for them, and re-layouts  78.3 us (14%)
  matrix products  65.7 us (12%)
    pallas_call x1, Pallas kernels, exchange(): pl.pallas_call(functools.partial(exchange_kernel, n, width), out_shape=(j...  118 us
    another operation x24, other arithmetic, cholesky_solve(): lax.linalg.cholesky(a[lo:lo + block, lo:lo + block], symmetrize_input=False)  100 us
    another operation x16, other arithmetic, cholesky_solve(): inv = lax.linalg.triangular_solve(lkk, eye, left_side=True, lower=True)  83.3 us
    pallas_call x1, Pallas kernels, lower_psum(): pl.pallas_call(functools.partial(reduce_kernel, n, parts), out_shape=jax....  77.1 us
    unnamed x147, local copies, waits for them, and re-layouts  62.1 us
    dot_general x7, matrix products, cholesky_solve(): jnp.dot(panel, panel.T, precision=hi)  14 us
    dot_general x1, matrix products, shards(): jnp.dot(centered, centered.T, preferred_element_type=jnp.float32)  13.9 us

profile of v9, /device:TPU:8, one launch (start us, length us, event | category | flops | bytes accessed | tf_op | source)
XLA Modules:
  0.0 545.6 jit_solution(16269984733440792027)
XLA Ops:
  0.1 117.7 %shard_map.28 = (bf16[32,32,16,256]{3,2,1,0:T(8,128)(2,1)}, f32[32,1,32]{2,1,0:T(1,128)}) custom-call(bf16[32,16,8192]{2,1,0:T(8,128)(2,1)} %jac_ref.1, f32[1,32]{1,0:T(1,128)} %bitcast.494), custom_call_target="tpu_custom_call" | custom-call | tf_op jit(solution)/shard_map/pallas_call | solution.py:69
  124.5 4.5 convert_reduce_fusion
  129.6 8.9 %multiply_convert_fusion.1 = bf16[32,32,16,256]{3,2,1,0:T(8,128)(2,1)} fusion(f32[16,256]{1,0:T(8,128)S(1)} %get-tuple-element.137, bf16[32,32,16,256]{3,2,1,0:T(8,128)(2,1)} %get-tuple-element.93), kind=kLoop, calls=%fused_computation.1 | loop fusion | flops 16777216 | bytes 16793600 | tf_op jit(solution)/shard_map/convert_element_type | solution.py:246
  138.5 13.9 %fusion.5 = f32[1024,1024]{1,0:T(8,128)S(1)} fusion(bf16[1024,16,256]{2,1,0:T(8,128)(2,1)} %bitcast.473), kind=kOutput, calls=%fused_computation.13 | convolution fusion | flops 8589934592 | bytes 12582912 | tf_op jit(solution)/shard_map/dot_general | solution.py:248
  154.5 77.1 %shard_map.29 = f32[32,144,128]{2,1,0:T(8,128)} custom-call(f32[32,144,128]{2,1,0:T(8,128)} %bitcast.474), custom_call_target="tpu_custom_call" | custom-call | tf_op jit(solution)/shard_map/pallas_call | solution.py:171
  242.0 1.9 copy-done
  245.3 2.6 select_add_fusion
  247.9 2.0 copy-done.2
  249.9 11.7 %custom-call.20 = f32[128,128]{1,0:T(8,128)S(1)} custom-call(f32[128,128]{1,0:T(8,128)S(1)} %slice.784), custom_call_target="Cholesky" | custom-call | tf_op jit(solution)/shard_map/cholesky/custom-call.1 | solution.py:208
  262.9 9.8 %custom-call.21 = f32[1,128,128]{1,2,0:T(8,128)S(1)} custom-call(f32[1,128,128]{2,1,0:T(8,128)S(1)} %fusion.83), custom_call_target="InvertDiagBlocksLowerTriangular" | custom-call | tf_op jit(solution)/shard_map/triangular_solve/custom-call.0 | solution.py:209
  274.6 1.6 fusion.40
  276.2 5.1 slice_add_fusion
  283.0 11.7 %custom-call.22 = f32[128,128]{1,0:T(8,128)S(1)} custom-call(f32[128,128]{1,0:T(8,128)S(1)} %slice.788), custom_call_target="Cholesky" | custom-call | tf_op jit(solution)/shard_map/cholesky/custom-call.1 | solution.py:208
  296.1 9.8 %custom-call.23 = f32[1,128,128]{1,2,0:T(8,128)S(1)} custom-call(f32[1,128,128]{2,1,0:T(8,128)S(1)} %fusion.84), custom_call_target="InvertDiagBlocksLowerTriangular" | custom-call | tf_op jit(solution)/shard_map/triangular_solve/custom-call.0 | solution.py:209
  309.3 3.8 slice_add_fusion.1
  313.0 12.1 %custom-call.24 = f32[128,128]{1,0:T(8,128)S(1)} custom-call(f32[128,128]{1,0:T(8,128)S(1)} %slice.793), custom_call_target="Cholesky" | custom-call | tf_op jit(solution)/shard_map/cholesky/custom-call.1 | solution.py:208
  326.6 9.8 %custom-call.25 = f32[1,128,128]{1,2,0:T(8,128)S(1)} custom-call(f32[1,128,128]{2,1,0:T(8,128)S(1)} %fusion.85), custom_call_target="InvertDiagBlocksLowerTriangular" | custom-call | tf_op jit(solution)/shard_map/triangular_solve/custom-call.0 | solution.py:209
  340.5 11.7 %custom-call.26 = f32[128,128]{1,0:T(8,128)S(1)} custom-call(f32[128,128]{1,0:T(8,128)S(1)} %slice.799), custom_call_target="Cholesky" | custom-call | tf_op jit(solution)/shard_map/cholesky/custom-call.1 | solution.py:208
  353.4 9.8 %custom-call.27 = f32[1,128,128]{1,2,0:T(8,128)S(1)} custom-call(f32[1,128,128]{2,1,0:T(8,128)S(1)} %fusion.86), custom_call_target="InvertDiagBlocksLowerTriangular" | custom-call | tf_op jit(solution)/shard_map/triangular_solve/custom-call.0 | solution.py:209
  365.0 2.3 fusion.8
  367.4 11.7 %custom-call.28 = f32[128,128]{1,0:T(8,128)S(1)} custom-call(f32[128,128]{1,0:T(8,128)S(1)} %slice.806), custom_call_target="Cholesky" | custom-call | tf_op jit(solution)/shard_map/cholesky/custom-call.1 | solution.py:208
  380.3 9.8 %custom-call.29 = f32[1,128,128]{1,2,0:T(8,128)S(1)} custom-call(f32[1,128,128]{2,1,0:T(8,128)S(1)} %fusion.87), custom_call_target="InvertDiagBlocksLowerTriangular" | custom-call | tf_op jit(solution)/shard_map/triangular_solve/custom-call.0 | solution.py:209
  391.5 11.9 %custom-call.30 = f32[128,128]{1,0:T(8,128)S(1)} custom-call(f32[128,128]{1,0:T(8,128)S(1)} %slice.814), custom_call_target="Cholesky" | custom-call | tf_op jit(solution)/shard_map/cholesky/custom-call.1 | solution.py:208
  404.6 9.8 %custom-call.31 = f32[1,128,128]{1,2,0:T(8,128)S(1)} custom-call(f32[1,128,128]{2,1,0:T(8,128)S(1)} %fusion.88), custom_call_target="InvertDiagBlocksLowerTriangular" | custom-call | tf_op jit(solution)/shard_map/triangular_solve/custom-call.0 | solution.py:209
  415.4 11.7 %custom-call.32 = f32[128,128]{1,0:T(8,128)S(1)} custom-call(f32[128,128]{1,0:T(8,128)S(1)} %slice.823), custom_call_target="Cholesky" | custom-call | tf_op jit(solution)/shard_map/cholesky/custom-call.1 | solution.py:208
  428.3 9.8 %custom-call.33 = f32[1,128,128]{1,2,0:T(8,128)S(1)} custom-call(f32[1,128,128]{2,1,0:T(8,128)S(1)} %fusion.89), custom_call_target="InvertDiagBlocksLowerTriangular" | custom-call | tf_op jit(solution)/shard_map/triangular_solve/custom-call.0 | solution.py:209
  454.3 12.2 %custom-call.34 = f32[128,128]{1,0:T(8,128)S(1)} custom-call(f32[128,128]{1,0:T(8,128)S(1)} %fusion.11), custom_call_target="Cholesky" | custom-call | tf_op jit(solution)/shard_map/cholesky/custom-call.1 | solution.py:208
  467.9 9.8 %custom-call.35 = f32[1,128,128]{1,2,0:T(8,128)S(1)} custom-call(f32[1,128,128]{2,1,0:T(8,128)S(1)} %fusion.90), custom_call_target="InvertDiagBlocksLowerTriangular" | custom-call | tf_op jit(solution)/shard_map/triangular_solve/custom-call.0 | solution.py:209
  510.1 4.3 fusion.132
  514.4 3.8 fusion.131
  519.6 17.6 %copy.9 = f32[128,8,16,256]{3,1,2,0:T(8,128)} copy(bf16[128,8,16,256]{3,2,1,0:T(8,128)(2,1)} %bitcast.433) | data formatting | bytes 25165824
  537.2 7.7 %fusion = f32[1,4096]{1,0:T(1,128)S(1)} fusion(f32[1024,1]{0,1:T(1,128)S(1)} %bitcast.478, f32[1024,4096]{1,0:T(8,128)} %bitcast.434, f32[4096]{0:T(1024)S(1)} %bitcast.479), kind=kOutput, calls=%fused_computation.2 | convolution fusion | flops 62914560 | bytes 16814080 | tf_op jit(solution)/shard_map/dot_general | solution.py:253
  (277 shorter events, 94.2 us)
Async XLA Ops:
  153.1 1.4 copy-start.6
  231.6 9.9 %copy-start.3 = (f32[32,144,128]{2,1,0:T(8,128)S(1)}, f32[32,144,128]{2,1,0:T(8,128)}, u32[]{:S(2)}) copy-start(f32[32,144,128]{2,1,0:T(8,128)} %shard_map.29) | copy-start | bytes 7077892
  238.7 3.2 copy-start.13
  242.0 1.9 copy-start
  247.9 2.0 copy-start.2
  273.0 1.5 copy-start.11
  281.3 1.7 copy-start.4
  306.2 1.5 copy-start.7
  336.7 0.6 copy-start.9
  339.3 1.2 copy-start.5
  365.0 74.4 %copy-start.10 = (f32[128,128]{1,0:T(8,128)S(1)}, f32[128,128]{1,0:T(8,128)}, u32[]{:S(2)}) copy-start(f32[128,128]{1,0:T(8,128)} %copy-done.9) | copy-start | bytes 196612
  438.4 60.1 %copy-start.8 = (f32[128,128]{1,0:T(8,128)S(1)}, f32[128,128]{1,0:T(8,128)}, u32[]{:S(2)}) copy-start(f32[128,128]{1,0:T(8,128)} %copy-done.7) | copy-start | bytes 196612
  438.5 70.4 %copy-start.12 = (f32[128,128]{1,0:T(8,128)S(1)}, f32[128,128]{1,0:T(8,128)}, u32[]{:S(2)}) copy-start(f32[128,128]{1,0:T(8,128)} %copy-done.11) | copy-start | bytes 196612
  438.5 70.7 %copy-start.14 = (f32[8,128,128]{2,1,0:T(8,128)S(1)}, f32[8,128,128]{2,1,0:T(8,128)}, u32[]{:S(2)}) copy-start(f32[8,128,128]{2,1,0:T(8,128)} %copy-done.13) | copy-start | bytes 1572868
  442.0 1.4 copy-start.16
  444.4 1.4 copy-start.17
  447.6 1.3 copy-start.18
  477.7 36.7 %copy-start.1 = (f32[1024,1024]{1,0:T(8,128)S(1)}, f32[1024,1024]{1,0:T(8,128)}, u32[]{:S(2)}) copy-start(f32[1024,1024]{1,0:T(8,128)} %copy-done) | copy-start | bytes 12582916
  519.6 17.6 %copy-start.15 = (f32[2,2,8,128]{3,1,2,0:T(2,128)S(1)}, f32[2,2,8,128]{3,1,2,0:T(2,128)}, u32[]{:S(2)}) copy-start(f32[2,2,8,128]{3,1,2,0:T(2,128)} %copy.10) | copy-start | bytes 49156

commit v10 on v9

--- a/solution.py
+++ b/solution.py
@@ -250,7 +250,7 @@
     gram, diag = lower_psum(partial_gram, n, parts)
     shift = 0.01 * jnp.trace(gram) / samples
     coeffs = cholesky_solve(gram + shift * jnp.eye(samples, dtype=jnp.float32), eps)
-    delta = jnp.dot(coeffs, centered.astype(jnp.float32), precision=lax.Precision.HIGHEST)
+    delta = jnp.sum(coeffs[:, None] * centered.astype(jnp.float32), axis=0)
     hi = lax.Precision.HIGHEST
     blocked = coeffs.reshape(diag.shape[0], diag.shape[1])
     full_c = (jnp.dot(gram, coeffs, precision=hi) + jnp.dot(coeffs, gram, precision=hi)

time: 555 us -> 527 us (0.950)
  local copies, waits for them, and re-layouts: 78.3 us -> 40.6 us
  other arithmetic: 203 us -> 212 us
    unnamed x147 -> x161, local copies, waits for them, and re-layouts: 62.1 us -> 25.4 us
    dot_general x1 -> x0, matrix products: 7.66 us -> none  [shards(): jnp.dot(coeffs, centered.astype(jnp.float32), precision=lax.Precision.HIG...]
    concatenate x7, local copies, waits for them, and re-layouts: 5.84 us -> 0.03 us  [cholesky_solve(): r = r - jnp.dot(jnp.concatenate(cs[k + 1:]), panels[k], precision=hi)]
where the time goes in v10:
time: 527 us; the launch traced here: 518 us
  other arithmetic  212 us (40%)
  Pallas kernels  195 us (37%)
  matrix products  67 us (13%)
  local copies, waits for them, and re-layouts  40.6 us (8%)
    pallas_call x1, Pallas kernels, exchange(): pl.pallas_call(functools.partial(exchange_kernel, n, width), out_shape=(j...  118 us
    another operation x24, other arithmetic, cholesky_solve(): lax.linalg.cholesky(a[lo:lo + block, lo:lo + block], symmetrize_input=False)  99.6 us
    another operation x16, other arithmetic, cholesky_solve(): inv = lax.linalg.triangular_solve(lkk, eye, left_side=True, lower=True)  84 us
    pallas_call x1, Pallas kernels, lower_psum(): pl.pallas_call(functools.partial(reduce_kernel, n, parts), out_shape=jax....  77.2 us
    unnamed x161, local copies, waits for them, and re-layouts  25.4 us
    dot_general x1, matrix products, shards(): jnp.dot(centered, centered.T, preferred_element_type=jnp.float32)  14.2 us
    dot_general x7, matrix products, cholesky_solve(): jnp.dot(panel, panel.T, precision=hi)  13.9 us

profile of v10, /device:TPU:8, one launch (start us, length us, event | category | flops | bytes accessed | tf_op | source)
XLA Modules:
  0.0 518.1 jit_solution(11770106589155780464)
XLA Ops:
  0.0 117.6 %shard_map.28 = (bf16[32,32,16,256]{3,2,1,0:T(8,128)(2,1)}, f32[32,1,32]{2,1,0:T(1,128)}) custom-call(bf16[32,16,8192]{2,1,0:T(8,128)(2,1)} %jac_ref.1, f32[1,32]{1,0:T(1,128)} %bitcast.480), custom_call_target="tpu_custom_call" | custom-call | tf_op jit(solution)/shard_map/pallas_call | solution.py:69
  117.6 4.5 convert_reduce_fusion
  122.1 8.9 %fusion.1 = bf16[32,32,16,256]{3,2,1,0:T(8,128)(2,1)} fusion(bf16[32,32,16,256]{3,2,1,0:T(8,128)(2,1)} %get-tuple-element.93, f32[16,256]{1,0:T(8,128)S(1)} %broadcast_multiply_fusion.1), kind=kLoop, calls=%fused_computation.3 | loop fusion | flops 16777216 | bytes 16793600 | tf_op jit(solution)/shard_map/convert_element_type | solution.py:246
  131.0 14.2 %fusion.4 = f32[1024,1024]{1,0:T(8,128)S(1)} fusion(bf16[1024,16,256]{2,1,0:T(8,128)(2,1)} %bitcast.461), kind=kOutput, calls=%fused_computation.12 | convolution fusion | flops 8589934592 | bytes 12582912 | tf_op jit(solution)/shard_map/dot_general | solution.py:248
  147.4 77.2 %shard_map.29 = f32[32,144,128]{2,1,0:T(8,128)} custom-call(f32[32,144,128]{2,1,0:T(8,128)} %bitcast.462), custom_call_target="tpu_custom_call" | custom-call | tf_op jit(solution)/shard_map/pallas_call | solution.py:171
  235.0 2.0 copy-done
  238.3 2.6 select_add_fusion
  240.9 1.9 copy-done.2
  242.9 11.7 %custom-call.20 = f32[128,128]{1,0:T(8,128)S(1)} custom-call(f32[128,128]{1,0:T(8,128)S(1)} %slice.784), custom_call_target="Cholesky" | custom-call | tf_op jit(solution)/shard_map/cholesky/custom-call.1 | solution.py:208
  255.9 9.8 %custom-call.21 = f32[1,128,128]{1,2,0:T(8,128)S(1)} custom-call(f32[1,128,128]{2,1,0:T(8,128)S(1)} %fusion.82), custom_call_target="InvertDiagBlocksLowerTriangular" | custom-call | tf_op jit(solution)/shard_map/triangular_solve/custom-call.0 | solution.py:209
  268.3 5.0 slice_add_fusion
  275.0 11.7 %custom-call.22 = f32[128,128]{1,0:T(8,128)S(1)} custom-call(f32[128,128]{1,0:T(8,128)S(1)} %slice.788), custom_call_target="Cholesky" | custom-call | tf_op jit(solution)/shard_map/cholesky/custom-call.1 | solution.py:208
  288.1 9.8 %custom-call.23 = f32[1,128,128]{1,2,0:T(8,128)S(1)} custom-call(f32[1,128,128]{2,1,0:T(8,128)S(1)} %fusion.83), custom_call_target="InvertDiagBlocksLowerTriangular" | custom-call | tf_op jit(solution)/shard_map/triangular_solve/custom-call.0 | solution.py:209
  300.3 3.8 slice_add_fusion.1
  304.0 11.9 %custom-call.24 = f32[128,128]{1,0:T(8,128)S(1)} custom-call(f32[128,128]{1,0:T(8,128)S(1)} %slice.793), custom_call_target="Cholesky" | custom-call | tf_op jit(solution)/shard_map/cholesky/custom-call.1 | solution.py:208
  317.3 9.8 %custom-call.25 = f32[1,128,128]{1,2,0:T(8,128)S(1)} custom-call(f32[1,128,128]{2,1,0:T(8,128)S(1)} %fusion.84), custom_call_target="InvertDiagBlocksLowerTriangular" | custom-call | tf_op jit(solution)/shard_map/triangular_solve/custom-call.0 | solution.py:209
  348.4 1.7 fusion.38
  352.8 11.7 %custom-call.26 = f32[128,128]{1,0:T(8,128)S(1)} custom-call(f32[128,128]{1,0:T(8,128)S(1)} %slice.799), custom_call_target="Cholesky" | custom-call | tf_op jit(solution)/shard_map/cholesky/custom-call.1 | solution.py:208
  365.8 10.2 %custom-call.27 = f32[1,128,128]{1,2,0:T(8,128)S(1)} custom-call(f32[1,128,128]{2,1,0:T(8,128)S(1)} %fusion.85), custom_call_target="InvertDiagBlocksLowerTriangular" | custom-call | tf_op jit(solution)/shard_map/triangular_solve/custom-call.0 | solution.py:209
  381.8 2.3 fusion.7
  384.1 11.7 %custom-call.28 = f32[128,128]{1,0:T(8,128)S(1)} custom-call(f32[128,128]{1,0:T(8,128)S(1)} %slice.806), custom_call_target="Cholesky" | custom-call | tf_op jit(solution)/shard_map/cholesky/custom-call.1 | solution.py:208
  397.2 9.8 %custom-call.29 = f32[1,128,128]{1,2,0:T(8,128)S(1)} custom-call(f32[1,128,128]{2,1,0:T(8,128)S(1)} %fusion.86), custom_call_target="InvertDiagBlocksLowerTriangular" | custom-call | tf_op jit(solution)/shard_map/triangular_solve/custom-call.0 | solution.py:209
  409.8 1.9 fusion.36
  412.4 11.9 %custom-call.30 = f32[128,128]{1,0:T(8,128)S(1)} custom-call(f32[128,128]{1,0:T(8,128)S(1)} %slice.814), custom_call_target="Cholesky" | custom-call | tf_op jit(solution)/shard_map/cholesky/custom-call.1 | solution.py:208
  425.6 9.8 %custom-call.31 = f32[1,128,128]{1,2,0:T(8,128)S(1)} custom-call(f32[1,128,128]{2,1,0:T(8,128)S(1)} %fusion.87), custom_call_target="InvertDiagBlocksLowerTriangular" | custom-call | tf_op jit(solution)/shard_map/triangular_solve/custom-call.0 | solution.py:209
  442.1 11.7 %custom-call.32 = f32[128,128]{1,0:T(8,128)S(1)} custom-call(f32[128,128]{1,0:T(8,128)S(1)} %slice.823), custom_call_target="Cholesky" | custom-call | tf_op jit(solution)/shard_map/cholesky/custom-call.1 | solution.py:208
  455.1 9.8 %custom-call.33 = f32[1,128,128]{1,2,0:T(8,128)S(1)} custom-call(f32[1,128,128]{2,1,0:T(8,128)S(1)} %fusion.88), custom_call_target="InvertDiagBlocksLowerTriangular" | custom-call | tf_op jit(solution)/shard_map/triangular_solve/custom-call.0 | solution.py:209
  470.7 11.9 %custom-call.34 = f32[128,128]{1,0:T(8,128)S(1)} custom-call(f32[128,128]{1,0:T(8,128)S(1)} %fusion.10), custom_call_target="Cholesky" | custom-call | tf_op jit(solution)/shard_map/cholesky/custom-call.1 | solution.py:208
  484.0 9.8 %custom-call.35 = f32[1,128,128]{1,2,0:T(8,128)S(1)} custom-call(f32[1,128,128]{2,1,0:T(8,128)S(1)} %fusion.89), custom_call_target="InvertDiagBlocksLowerTriangular" | custom-call | tf_op jit(solution)/shard_map/triangular_solve/custom-call.0 | solution.py:209
  500.5 4.4 fusion.129
  504.9 3.9 fusion.128
  511.8 5.5 %multiply_reduce_fusion = f32[16,256]{1,0:T(8,128)S(1)} fusion(f32[32,32]{1,0:T(8,128)S(1)} %concatenate.179, f32[16,256]{1,0:T(8,128)S(1)} %broadcast_multiply_fusion.1, bf16[32,32,16,256]{3,2,1,0:T(8,128)(2,1)} %get-tuple-element.93), kind=kLoop, calls=%fused_computation.4 | loop fusion | flops 29356032 | bytes 8425472 | tf_op jit(solution)/shard_map/reduce_sum | solution.py:253
  (299 shorter events, 84.0 us)
Async XLA Ops:
  145.9 1.4 copy-start.6
  224.6 9.9 %copy-start.3 = (f32[32,144,128]{2,1,0:T(8,128)S(1)}, f32[32,144,128]{2,1,0:T(8,128)}, u32[]{:S(2)}) copy-start(f32[32,144,128]{2,1,0:T(8,128)} %shard_map.29) | copy-start | bytes 7077892
  231.7 3.2 copy-start.13
  235.0 2.0 copy-start
  240.9 2.0 copy-start.2
  266.0 0.6 copy-start.11
  273.3 1.7 copy-start.4
  298.2 0.6 copy-start.7
  327.4 0.6 copy-start.9
  340.2 0.6 copy-start.16
  345.3 0.6 copy-start.18
  351.6 1.2 copy-start.5
  352.8 54.7 %copy-start.15 = (f32[1,128]{1,0:T(1,128)S(1)}, f32[1,128]{1,0:T(1,128)}, u32[]{:S(2)}) copy-start(f32[1,128]{1,0:T(1,128)} %fusion.126) | copy-start | bytes 1540
  352.8 54.7 %copy-start.17 = (f32[128]{0:T(128)S(1)}, f32[128]{0:T(128)}, u32[]{:S(2)}) copy-start(f32[128]{0:T(128)} %copy-done.16) | copy-start | bytes 1540
  352.8 54.8 %copy-start.19 = (f32[128]{0:T(128)S(1)}, f32[128]{0:T(128)}, u32[]{:S(2)}) copy-start(f32[128]{0:T(128)} %copy-done.18) | copy-start | bytes 1540
  352.8 56.9 %copy-start.22 = (f32[4,32]{1,0:T(4,128)S(1)}, f32[4,32]{1,0:T(4,128)}, u32[]{:S(2)}) copy-start(f32[4,32]{1,0:T(4,128)} %get-tuple-element.97) | copy-start | bytes 1540
  377.1 30.9 %copy-start.20 = (f32[128]{0:T(128)}, f32[128]{0:T(128)S(1)}, u32[]{:S(2)}) copy-start(f32[128]{0:T(128)S(1)} %convolution_bitcast_fusion.19) | copy-start | bytes 1540
  407.5 0.6 copy-start.23
  408.0 0.6 copy-start.25
  408.0 0.6 copy-start.26
  408.6 88.8 %copy-start.10 = (f32[128,128]{1,0:T(8,128)S(1)}, f32[128,128]{1,0:T(8,128)}, u32[]{:S(2)}) copy-start(f32[128,128]{1,0:T(8,128)} %copy-done.9) | copy-start | bytes 196612
  409.0 89.7 %copy-start.8 = (f32[128,128]{1,0:T(8,128)S(1)}, f32[128,128]{1,0:T(8,128)}, u32[]{:S(2)}) copy-start(f32[128,128]{1,0:T(8,128)} %copy-done.7) | copy-start | bytes 196612
  412.4 82.9 %copy-start.24 = (f32[128]{0:T(128)S(1)}, f32[128]{0:T(128)}, u32[]{:S(2)}) copy-start(f32[128]{0:T(128)} %copy-done.23) | copy-start | bytes 1540
  412.4 83.5 %copy-start.21 = (f32[128]{0:T(128)S(1)}, f32[128]{0:T(128)}, u32[]{:S(2)}) copy-start(f32[128]{0:T(128)} %copy-done.20) | copy-start | bytes 1540
  412.4 87.8 %copy-start.12 = (f32[128,128]{1,0:T(8,128)S(1)}, f32[128,128]{1,0:T(8,128)}, u32[]{:S(2)}) copy-start(f32[128,128]{1,0:T(8,128)} %copy-done.11) | copy-start | bytes 196612
  500.4 4.6 copy-start.1
  500.5 8.3 %copy-start.14 = (f32[8,128,128]{2,1,0:T(8,128)S(1)}, f32[8,128,128]{2,1,0:T(8,128)}, u32[]{:S(2)}) copy-start(f32[8,128,128]{2,1,0:T(8,128)} %copy-done.13) | copy-start | bytes 1572868

commit v11 on v10

--- a/solution.py
+++ b/solution.py
@@ -214,21 +214,17 @@
             panels.append(panel)
             a = a.at[lo + block:, lo + block:].add(-jnp.dot(panel, panel.T, precision=hi))
     ys = []
+    tail = rhs
     for k in range(nb):
-        lo = k * block
-        r = rhs[lo:lo + block]
-        if k > 0:
-            strip = jnp.concatenate(
-                [panels[j][(k - j - 1) * block:(k - j) * block] for j in range(k)], axis=1)
-            r = r - jnp.dot(strip, jnp.concatenate(ys), precision=hi)
-        ys.append(jnp.dot(inverses[k], r, precision=hi))
-    cs = [None] * nb
-    for k in reversed(range(nb)):
-        r = ys[k]
+        y = jnp.dot(inverses[k], tail[:block], precision=hi)
+        ys.append(y)
         if k < nb - 1:
-            r = r - jnp.dot(jnp.concatenate(cs[k + 1:]), panels[k], precision=hi)
-        cs[k] = jnp.dot(r, inverses[k], precision=hi)
-    return jnp.concatenate(cs)
+            tail = tail[block:] - jnp.dot(panels[k], y, precision=hi)
+    solved = jnp.dot(ys[nb - 1], inverses[nb - 1], precision=hi)
+    for k in reversed(range(nb - 1)):
+        r = ys[k] - jnp.dot(solved, panels[k], precision=hi)
+        solved = jnp.concatenate([jnp.dot(r, inverses[k], precision=hi), solved])
+    return solved
 
 
 def shards(n, jacobian, local_energy):

time: 527 us -> 495 us (0.939)
  local copies, waits for them, and re-layouts: 40.6 us -> 19.9 us
  matrix products: 67 us -> 57.3 us
    dot_general x30, matrix products: 20.9 us -> 12.2 us  [the longest x7 4.79 us: cholesky_solve(): r = ys[k] - jnp.dot(solved, panels[k], precision=hi)]
    slice x9 -> x4, local copies, waits for them, and re-layouts: 8.06 us -> 0.22 us  [the longest x2 0.11 us: cholesky_solve(): tail = tail[block:] - jnp.dot(panels[k], y, precision=hi)]
    unnamed x161 -> x139, local copies, waits for them, and re-layouts: 25.4 us -> 17.8 us
where the time goes in v11:
time: 495 us; the launch traced here: 487 us
  other arithmetic  211 us (43%)
  Pallas kernels  195 us (39%)
  matrix products  57.3 us (12%)
  local copies, waits for them, and re-layouts  19.9 us (4%)
    pallas_call x1, Pallas kernels, exchange(): pl.pallas_call(functools.partial(exchange_kernel, n, width), out_shape=(j...  118 us
    another operation x24, other arithmetic, cholesky_solve(): lax.linalg.cholesky(a[lo:lo + block, lo:lo + block], symmetrize_input=False)  99.7 us
    another operation x16, other arithmetic, cholesky_solve(): inv = lax.linalg.triangular_solve(lkk, eye, left_side=True, lower=True)  84.1 us
    pallas_call x1, Pallas kernels, lower_psum(): pl.pallas_call(functools.partial(reduce_kernel, n, parts), out_shape=jax....  77.1 us
    unnamed x139, local copies, waits for them, and re-layouts  17.8 us
    dot_general x1, matrix products, shards(): jnp.dot(centered, centered.T, preferred_element_type=jnp.float32)  14.2 us
    dot_general x7, matrix products, cholesky_solve(): jnp.dot(panel, panel.T, precision=hi)  13.7 us

profile of v11, /device:TPU:8, one launch (start us, length us, event | category | flops | bytes accessed | tf_op | source)
XLA Modules:
  0.0 486.9 jit_solution(2070858864913311487)
XLA Ops:
  0.0 117.6 %shard_map.28 = (bf16[32,32,16,256]{3,2,1,0:T(8,128)(2,1)}, f32[32,1,32]{2,1,0:T(1,128)}) custom-call(bf16[32,16,8192]{2,1,0:T(8,128)(2,1)} %jac_ref.1, f32[1,32]{1,0:T(1,128)} %bitcast.454), custom_call_target="tpu_custom_call" | custom-call | tf_op jit(solution)/shard_map/pallas_call | solution.py:69
  117.6 4.5 convert_reduce_fusion
  122.1 8.9 %fusion.1 = bf16[32,32,16,256]{3,2,1,0:T(8,128)(2,1)} fusion(bf16[32,32,16,256]{3,2,1,0:T(8,128)(2,1)} %get-tuple-element.93, f32[16,256]{1,0:T(8,128)S(1)} %broadcast_multiply_fusion.1), kind=kLoop, calls=%fused_computation.3 | loop fusion | flops 16777216 | bytes 16793600 | tf_op jit(solution)/shard_map/convert_element_type | solution.py:242
  131.0 14.2 %fusion.4 = f32[1024,1024]{1,0:T(8,128)S(1)} fusion(bf16[1024,16,256]{2,1,0:T(8,128)(2,1)} %bitcast.438), kind=kOutput, calls=%fused_computation.12 | convolution fusion | flops 8589934592 | bytes 12582912 | tf_op jit(solution)/shard_map/dot_general | solution.py:244
  147.3 77.1 %shard_map.29 = f32[32,144,128]{2,1,0:T(8,128)} custom-call(f32[32,144,128]{2,1,0:T(8,128)} %bitcast.439), custom_call_target="tpu_custom_call" | custom-call | tf_op jit(solution)/shard_map/pallas_call | solution.py:171
  234.8 2.0 copy-done
  238.2 2.6 select_add_fusion
  240.8 1.9 copy-done.2
  242.7 11.7 %custom-call.20 = f32[128,128]{1,0:T(8,128)S(1)} custom-call(f32[128,128]{1,0:T(8,128)S(1)} %slice.676), custom_call_target="Cholesky" | custom-call | tf_op jit(solution)/shard_map/cholesky/custom-call.1 | solution.py:208
  255.8 9.8 %custom-call.21 = f32[1,128,128]{1,2,0:T(8,128)S(1)} custom-call(f32[1,128,128]{2,1,0:T(8,128)S(1)} %fusion.55), custom_call_target="InvertDiagBlocksLowerTriangular" | custom-call | tf_op jit(solution)/shard_map/triangular_solve/custom-call.0 | solution.py:209
  267.5 1.6 fusion.27
  269.8 5.0 %slice_add_fusion = f32[896,896]{1,0:T(8,128)S(1)} fusion(f32[1024,1024]{1,0:T(8,128)} %copy-done.2, f32[896,128]{1,0:T(8,128)S(1)} %fusion.27), kind=kOutput, calls=%fused_computation.10 | convolution fusion | flops 1234731008 | bytes 7340032 | tf_op jit(solution)/shard_map/dot_general | solution.py:215
  274.9 1.7 copy-done.4
  276.6 11.7 %custom-call.22 = f32[128,128]{1,0:T(8,128)S(1)} custom-call(f32[128,128]{1,0:T(8,128)S(1)} %slice.680), custom_call_target="Cholesky" | custom-call | tf_op jit(solution)/shard_map/cholesky/custom-call.1 | solution.py:208
  289.6 9.8 %custom-call.23 = f32[1,128,128]{1,2,0:T(8,128)S(1)} custom-call(f32[1,128,128]{2,1,0:T(8,128)S(1)} %fusion.56), custom_call_target="InvertDiagBlocksLowerTriangular" | custom-call | tf_op jit(solution)/shard_map/triangular_solve/custom-call.0 | solution.py:209
  301.9 3.7 slice_add_fusion.1
  305.7 11.9 %custom-call.24 = f32[128,128]{1,0:T(8,128)S(1)} custom-call(f32[128,128]{1,0:T(8,128)S(1)} %slice.684), custom_call_target="Cholesky" | custom-call | tf_op jit(solution)/shard_map/cholesky/custom-call.1 | solution.py:208
  318.9 9.8 %custom-call.25 = f32[1,128,128]{1,2,0:T(8,128)S(1)} custom-call(f32[1,128,128]{2,1,0:T(8,128)S(1)} %fusion.57), custom_call_target="InvertDiagBlocksLowerTriangular" | custom-call | tf_op jit(solution)/shard_map/triangular_solve/custom-call.0 | solution.py:209
  334.1 11.7 %custom-call.26 = f32[128,128]{1,0:T(8,128)S(1)} custom-call(f32[128,128]{1,0:T(8,128)S(1)} %slice.687), custom_call_target="Cholesky" | custom-call | tf_op jit(solution)/shard_map/cholesky/custom-call.1 | solution.py:208
  347.2 10.2 %custom-call.27 = f32[1,128,128]{1,2,0:T(8,128)S(1)} custom-call(f32[1,128,128]{2,1,0:T(8,128)S(1)} %fusion.58), custom_call_target="InvertDiagBlocksLowerTriangular" | custom-call | tf_op jit(solution)/shard_map/triangular_solve/custom-call.0 | solution.py:209
  360.9 2.2 fusion.7
  363.2 11.7 %custom-call.28 = f32[128,128]{1,0:T(8,128)S(1)} custom-call(f32[128,128]{1,0:T(8,128)S(1)} %slice.690), custom_call_target="Cholesky" | custom-call | tf_op jit(solution)/shard_map/cholesky/custom-call.1 | solution.py:208
  376.3 9.8 %custom-call.29 = f32[1,128,128]{1,2,0:T(8,128)S(1)} custom-call(f32[1,128,128]{2,1,0:T(8,128)S(1)} %fusion.59), custom_call_target="InvertDiagBlocksLowerTriangular" | custom-call | tf_op jit(solution)/shard_map/triangular_solve/custom-call.0 | solution.py:209
  388.5 11.9 %custom-call.30 = f32[128,128]{1,0:T(8,128)S(1)} custom-call(f32[128,128]{1,0:T(8,128)S(1)} %slice.693), custom_call_target="Cholesky" | custom-call | tf_op jit(solution)/shard_map/cholesky/custom-call.1 | solution.py:208
  401.7 9.8 %custom-call.31 = f32[1,128,128]{1,2,0:T(8,128)S(1)} custom-call(f32[1,128,128]{2,1,0:T(8,128)S(1)} %fusion.60), custom_call_target="InvertDiagBlocksLowerTriangular" | custom-call | tf_op jit(solution)/shard_map/triangular_solve/custom-call.0 | solution.py:209
  414.4 11.7 %custom-call.32 = f32[128,128]{1,0:T(8,128)S(1)} custom-call(f32[128,128]{1,0:T(8,128)S(1)} %slice.696), custom_call_target="Cholesky" | custom-call | tf_op jit(solution)/shard_map/cholesky/custom-call.1 | solution.py:208
  427.4 9.8 %custom-call.33 = f32[1,128,128]{1,2,0:T(8,128)S(1)} custom-call(f32[1,128,128]{2,1,0:T(8,128)S(1)} %fusion.61), custom_call_target="InvertDiagBlocksLowerTriangular" | custom-call | tf_op jit(solution)/shard_map/triangular_solve/custom-call.0 | solution.py:209
  438.5 11.9 %custom-call.34 = f32[128,128]{1,0:T(8,128)S(1)} custom-call(f32[128,128]{1,0:T(8,128)S(1)} %fusion.10), custom_call_target="Cholesky" | custom-call | tf_op jit(solution)/shard_map/cholesky/custom-call.1 | solution.py:208
  451.8 9.8 %custom-call.35 = f32[1,128,128]{1,2,0:T(8,128)S(1)} custom-call(f32[1,128,128]{2,1,0:T(8,128)S(1)} %fusion.62), custom_call_target="InvertDiagBlocksLowerTriangular" | custom-call | tf_op jit(solution)/shard_map/triangular_solve/custom-call.0 | solution.py:209
  469.6 4.4 fusion.124
  474.0 3.6 fusion.123
  480.6 5.5 %multiply_reduce_fusion = f32[16,256]{1,0:T(8,128)S(1)} fusion(f32[32,32]{1,0:T(8,128)S(1)} %concatenate.137, f32[16,256]{1,0:T(8,128)S(1)} %broadcast_multiply_fusion.1, bf16[32,32,16,256]{3,2,1,0:T(8,128)(2,1)} %get-tuple-element.93), kind=kLoop, calls=%fused_computation.4 | loop fusion | flops 29356032 | bytes 8425472 | tf_op jit(solution)/shard_map/reduce_sum | solution.py:249
  (265 shorter events, 53.7 us)
Async XLA Ops:
  145.9 1.4 copy-start.6
  224.4 9.9 %copy-start.3 = (f32[32,144,128]{2,1,0:T(8,128)S(1)}, f32[32,144,128]{2,1,0:T(8,128)}, u32[]{:S(2)}) copy-start(f32[32,144,128]{2,1,0:T(8,128)} %shard_map.29) | copy-start | bytes 7077892
  231.6 3.2 copy-start.12
  234.8 2.0 copy-start
  238.2 27.7 %copy-start.14 = (f32[32,1,32]{2,1,0:T(1,128)S(1)}, f32[32,1,32]{2,1,0:T(1,128)}, u32[]{:S(2)}) copy-start(f32[32,1,32]{2,1,0:T(1,128)} %get-tuple-element.94) | copy-start | bytes 12292
  240.8 2.0 copy-start.2
  265.9 9.0 %copy-start.11 = (f32[128,128]{1,0:T(8,128)}, f32[128,128]{1,0:T(8,128)S(1)}, u32[]{:S(2)}) copy-start(f32[128,128]{1,0:T(8,128)S(1)} %fusion.49) | copy-start | bytes 196612
  267.5 1.6 copy-start.20
  274.9 1.7 copy-start.4
  299.7 2.2 copy-start.7
  299.9 5.7 %copy-start.16 = (f32[1,128]{1,0:T(1,128)}, f32[1,128]{1,0:T(1,128)S(1)}, u32[]{:S(2)}) copy-start(f32[1,128]{1,0:T(1,128)S(1)} %fusion.112) | copy-start | bytes 1540
  301.9 27.1 %copy-start.15 = (f32[768]{0:T(1024)}, f32[768]{0:T(1024)S(1)}, u32[]{:S(2)}) copy-start(f32[768]{0:T(1024)S(1)} %slice_subtract_fusion.1) | copy-start | bytes 9220
  329.0 1.1 copy-start.9
  329.2 0.9 copy-start.19
  332.9 1.2 copy-start.5
  358.5 4.7 copy-start.17
  363.2 102.8 %copy-start.10 = (f32[128,128]{1,0:T(8,128)S(1)}, f32[128,128]{1,0:T(8,128)}, u32[]{:S(2)}) copy-start(f32[128,128]{1,0:T(8,128)} %copy-done.9) | copy-start | bytes 196612
  363.2 104.0 %copy-start.8 = (f32[128,128]{1,0:T(8,128)S(1)}, f32[128,128]{1,0:T(8,128)}, u32[]{:S(2)}) copy-start(f32[128,128]{1,0:T(8,128)} %copy-done.7) | copy-start | bytes 196612
  386.6 0.7 copy-start.18
  469.4 4.6 copy-start.1
  469.6 8.1 %copy-start.13 = (f32[8,128,128]{2,1,0:T(8,128)S(1)}, f32[8,128,128]{2,1,0:T(8,128)}, u32[]{:S(2)}) copy-start(f32[8,128,128]{2,1,0:T(8,128)} %copy-done.12) | copy-start | bytes 1572868

commit v12 on v11

--- a/solution.py
+++ b/solution.py
@@ -30,8 +30,9 @@
     local_en = pltpu.make_async_copy(en_ref, en_all_ref.at[me], local_sems.at[1])
     local_en.start()
     sends = []
-    for k in range(1, n):
-        t = jnp.bitwise_xor(me, jnp.where(col == 0, k, n - k))
+    order = [i ^ (i // 2) for i in range(1, n)]
+    for i in range(n - 1):
+        t = jnp.bitwise_xor(me, jnp.where(col == 0, order[i], order[n - 2 - i]))
         dev = (t, col, slab)
         c = pltpu.make_async_remote_copy(
             src_ref=piece(t), dst_ref=cols_ref.at[me],

time: 495 us -> 488 us (0.986)
  Pallas kernels: 195 us -> 187 us
    pallas_call x1, Pallas kernels: 118 us -> 110 us  [exchange(): pl.pallas_call(functools.partial(exchange_kernel, n, width), out_shape=(j...]
where the time goes in v12:
time: 488 us; the launch traced here: 479 us
  other arithmetic  211 us (43%)
  Pallas kernels  187 us (38%)
  matrix products  57.3 us (12%)
  local copies, waits for them, and re-layouts  19.9 us (4%)
    pallas_call x1, Pallas kernels, exchange(): pl.pallas_call(functools.partial(exchange_kernel, n, width), out_shape=(j...  110 us
    another operation x24, other arithmetic, cholesky_solve(): lax.linalg.cholesky(a[lo:lo + block, lo:lo + block], symmetrize_input=False)  99.7 us
    another operation x16, other arithmetic, cholesky_solve(): inv = lax.linalg.triangular_solve(lkk, eye, left_side=True, lower=True)  84.1 us
    pallas_call x1, Pallas kernels, lower_psum(): pl.pallas_call(functools.partial(reduce_kernel, n, parts), out_shape=jax....  77.4 us
    unnamed x139, local copies, waits for them, and re-layouts  17.8 us
    dot_general x1, matrix products, shards(): jnp.dot(centered, centered.T, preferred_element_type=jnp.float32)  14.2 us
    dot_general x7, matrix products, cholesky_solve(): jnp.dot(panel, panel.T, precision=hi)  13.7 us

profile of v12, /device:TPU:8, one launch (start us, length us, event | category | flops | bytes accessed | tf_op | source)
XLA Modules:
  0.0 479.4 jit_solution(15633304286344599163)
XLA Ops:
  0.0 109.8 %shard_map.28 = (bf16[32,32,16,256]{3,2,1,0:T(8,128)(2,1)}, f32[32,1,32]{2,1,0:T(1,128)}) custom-call(bf16[32,16,8192]{2,1,0:T(8,128)(2,1)} %jac_ref.1, f32[1,32]{1,0:T(1,128)} %bitcast.454), custom_call_target="tpu_custom_call" | custom-call | tf_op jit(solution)/shard_map/pallas_call | solution.py:70
  109.8 4.5 convert_reduce_fusion
  114.3 8.9 %fusion.1 = bf16[32,32,16,256]{3,2,1,0:T(8,128)(2,1)} fusion(bf16[32,32,16,256]{3,2,1,0:T(8,128)(2,1)} %get-tuple-element.93, f32[16,256]{1,0:T(8,128)S(1)} %broadcast_multiply_fusion.1), kind=kLoop, calls=%fused_computation.3 | loop fusion | flops 16777216 | bytes 16793600 | tf_op jit(solution)/shard_map/convert_element_type | solution.py:243
  123.2 14.2 %fusion.4 = f32[1024,1024]{1,0:T(8,128)S(1)} fusion(bf16[1024,16,256]{2,1,0:T(8,128)(2,1)} %bitcast.438), kind=kOutput, calls=%fused_computation.12 | convolution fusion | flops 8589934592 | bytes 12582912 | tf_op jit(solution)/shard_map/dot_general | solution.py:245
  139.5 77.4 %shard_map.29 = f32[32,144,128]{2,1,0:T(8,128)} custom-call(f32[32,144,128]{2,1,0:T(8,128)} %bitcast.439), custom_call_target="tpu_custom_call" | custom-call | tf_op jit(solution)/shard_map/pallas_call | solution.py:172
  227.3 2.0 copy-done
  230.7 2.6 select_add_fusion
  233.3 1.9 copy-done.2
  235.2 11.7 %custom-call.20 = f32[128,128]{1,0:T(8,128)S(1)} custom-call(f32[128,128]{1,0:T(8,128)S(1)} %slice.676), custom_call_target="Cholesky" | custom-call | tf_op jit(solution)/shard_map/cholesky/custom-call.1 | solution.py:209
  248.3 9.8 %custom-call.21 = f32[1,128,128]{1,2,0:T(8,128)S(1)} custom-call(f32[1,128,128]{2,1,0:T(8,128)S(1)} %fusion.55), custom_call_target="InvertDiagBlocksLowerTriangular" | custom-call | tf_op jit(solution)/shard_map/triangular_solve/custom-call.0 | solution.py:210
  260.0 1.6 fusion.27
  262.3 5.0 %slice_add_fusion = f32[896,896]{1,0:T(8,128)S(1)} fusion(f32[1024,1024]{1,0:T(8,128)} %copy-done.2, f32[896,128]{1,0:T(8,128)S(1)} %fusion.27), kind=kOutput, calls=%fused_computation.10 | convolution fusion | flops 1234731008 | bytes 7340032 | tf_op jit(solution)/shard_map/dot_general | solution.py:216
  267.4 1.7 copy-done.4
  269.0 11.7 %custom-call.22 = f32[128,128]{1,0:T(8,128)S(1)} custom-call(f32[128,128]{1,0:T(8,128)S(1)} %slice.680), custom_call_target="Cholesky" | custom-call | tf_op jit(solution)/shard_map/cholesky/custom-call.1 | solution.py:209
  282.1 9.8 %custom-call.23 = f32[1,128,128]{1,2,0:T(8,128)S(1)} custom-call(f32[1,128,128]{2,1,0:T(8,128)S(1)} %fusion.56), custom_call_target="InvertDiagBlocksLowerTriangular" | custom-call | tf_op jit(solution)/shard_map/triangular_solve/custom-call.0 | solution.py:210
  294.4 3.7 slice_add_fusion.1
  298.1 11.9 %custom-call.24 = f32[128,128]{1,0:T(8,128)S(1)} custom-call(f32[128,128]{1,0:T(8,128)S(1)} %slice.684), custom_call_target="Cholesky" | custom-call | tf_op jit(solution)/shard_map/cholesky/custom-call.1 | solution.py:209
  311.4 9.8 %custom-call.25 = f32[1,128,128]{1,2,0:T(8,128)S(1)} custom-call(f32[1,128,128]{2,1,0:T(8,128)S(1)} %fusion.57), custom_call_target="InvertDiagBlocksLowerTriangular" | custom-call | tf_op jit(solution)/shard_map/triangular_solve/custom-call.0 | solution.py:210
  326.6 11.7 %custom-call.26 = f32[128,128]{1,0:T(8,128)S(1)} custom-call(f32[128,128]{1,0:T(8,128)S(1)} %slice.687), custom_call_target="Cholesky" | custom-call | tf_op jit(solution)/shard_map/cholesky/custom-call.1 | solution.py:209
  339.7 10.2 %custom-call.27 = f32[1,128,128]{1,2,0:T(8,128)S(1)} custom-call(f32[1,128,128]{2,1,0:T(8,128)S(1)} %fusion.58), custom_call_target="InvertDiagBlocksLowerTriangular" | custom-call | tf_op jit(solution)/shard_map/triangular_solve/custom-call.0 | solution.py:210
  353.4 2.2 fusion.7
  355.7 11.7 %custom-call.28 = f32[128,128]{1,0:T(8,128)S(1)} custom-call(f32[128,128]{1,0:T(8,128)S(1)} %slice.690), custom_call_target="Cholesky" | custom-call | tf_op jit(solution)/shard_map/cholesky/custom-call.1 | solution.py:209
  368.8 9.8 %custom-call.29 = f32[1,128,128]{1,2,0:T(8,128)S(1)} custom-call(f32[1,128,128]{2,1,0:T(8,128)S(1)} %fusion.59), custom_call_target="InvertDiagBlocksLowerTriangular" | custom-call | tf_op jit(solution)/shard_map/triangular_solve/custom-call.0 | solution.py:210
  381.0 11.9 %custom-call.30 = f32[128,128]{1,0:T(8,128)S(1)} custom-call(f32[128,128]{1,0:T(8,128)S(1)} %slice.693), custom_call_target="Cholesky" | custom-call | tf_op jit(solution)/shard_map/cholesky/custom-call.1 | solution.py:209
  394.2 9.8 %custom-call.31 = f32[1,128,128]{1,2,0:T(8,128)S(1)} custom-call(f32[1,128,128]{2,1,0:T(8,128)S(1)} %fusion.60), custom_call_target="InvertDiagBlocksLowerTriangular" | custom-call | tf_op jit(solution)/shard_map/triangular_solve/custom-call.0 | solution.py:210
  406.8 11.7 %custom-call.32 = f32[128,128]{1,0:T(8,128)S(1)} custom-call(f32[128,128]{1,0:T(8,128)S(1)} %slice.696), custom_call_target="Cholesky" | custom-call | tf_op jit(solution)/shard_map/cholesky/custom-call.1 | solution.py:209
  419.9 9.8 %custom-call.33 = f32[1,128,128]{1,2,0:T(8,128)S(1)} custom-call(f32[1,128,128]{2,1,0:T(8,128)S(1)} %fusion.61), custom_call_target="InvertDiagBlocksLowerTriangular" | custom-call | tf_op jit(solution)/shard_map/triangular_solve/custom-call.0 | solution.py:210
  431.0 11.9 %custom-call.34 = f32[128,128]{1,0:T(8,128)S(1)} custom-call(f32[128,128]{1,0:T(8,128)S(1)} %fusion.10), custom_call_target="Cholesky" | custom-call | tf_op jit(solution)/shard_map/cholesky/custom-call.1 | solution.py:209
  444.2 9.8 %custom-call.35 = f32[1,128,128]{1,2,0:T(8,128)S(1)} custom-call(f32[1,128,128]{2,1,0:T(8,128)S(1)} %fusion.62), custom_call_target="InvertDiagBlocksLowerTriangular" | custom-call | tf_op jit(solution)/shard_map/triangular_solve/custom-call.0 | solution.py:210
  462.1 4.4 fusion.124
  466.5 3.6 fusion.123
  473.1 5.5 %multiply_reduce_fusion = f32[16,256]{1,0:T(8,128)S(1)} fusion(f32[32,32]{1,0:T(8,128)S(1)} %concatenate.137, f32[16,256]{1,0:T(8,128)S(1)} %broadcast_multiply_fusion.1, bf16[32,32,16,256]{3,2,1,0:T(8,128)(2,1)} %get-tuple-element.93), kind=kLoop, calls=%fused_computation.4 | loop fusion | flops 29356032 | bytes 8425472 | tf_op jit(solution)/shard_map/reduce_sum | solution.py:250
  (265 shorter events, 53.7 us)
Async XLA Ops:
  138.1 1.4 copy-start.6
  216.9 9.9 %copy-start.3 = (f32[32,144,128]{2,1,0:T(8,128)S(1)}, f32[32,144,128]{2,1,0:T(8,128)}, u32[]{:S(2)}) copy-start(f32[32,144,128]{2,1,0:T(8,128)} %shard_map.29) | copy-start | bytes 7077892
  224.1 3.2 copy-start.12
  227.3 2.0 copy-start
  230.7 27.7 %copy-start.14 = (f32[32,1,32]{2,1,0:T(1,128)S(1)}, f32[32,1,32]{2,1,0:T(1,128)}, u32[]{:S(2)}) copy-start(f32[32,1,32]{2,1,0:T(1,128)} %get-tuple-element.94) | copy-start | bytes 12292
  233.2 2.0 copy-start.2
  258.4 9.0 %copy-start.11 = (f32[128,128]{1,0:T(8,128)}, f32[128,128]{1,0:T(8,128)S(1)}, u32[]{:S(2)}) copy-start(f32[128,128]{1,0:T(8,128)S(1)} %fusion.49) | copy-start | bytes 196612
  260.0 1.6 copy-start.20
  267.3 1.7 copy-start.4
  292.2 2.2 copy-start.7
  292.4 5.7 %copy-start.16 = (f32[1,128]{1,0:T(1,128)}, f32[1,128]{1,0:T(1,128)S(1)}, u32[]{:S(2)}) copy-start(f32[1,128]{1,0:T(1,128)S(1)} %fusion.112) | copy-start | bytes 1540
  294.4 27.1 %copy-start.15 = (f32[768]{0:T(1024)}, f32[768]{0:T(1024)S(1)}, u32[]{:S(2)}) copy-start(f32[768]{0:T(1024)S(1)} %slice_subtract_fusion.1) | copy-start | bytes 9220
  321.5 1.1 copy-start.9
  321.7 0.9 copy-start.19
  325.4 1.2 copy-start.5
  351.0 4.7 copy-start.17
  355.7 102.8 %copy-start.10 = (f32[128,128]{1,0:T(8,128)S(1)}, f32[128,128]{1,0:T(8,128)}, u32[]{:S(2)}) copy-start(f32[128,128]{1,0:T(8,128)} %copy-done.9) | copy-start | bytes 196612
  355.7 104.0 %copy-start.8 = (f32[128,128]{1,0:T(8,128)S(1)}, f32[128,128]{1,0:T(8,128)}, u32[]{:S(2)}) copy-start(f32[128,128]{1,0:T(8,128)} %copy-done.7) | copy-start | bytes 196612
  379.0 0.7 copy-start.18
  461.9 4.6 copy-start.1
  462.1 8.1 %copy-start.13 = (f32[8,128,128]{2,1,0:T(8,128)S(1)}, f32[8,128,128]{2,1,0:T(8,128)}, u32[]{:S(2)}) copy-start(f32[8,128,128]{2,1,0:T(8,128)} %copy-done.12) | copy-start | bytes 1572868

commit v13 on v12

--- a/solution.py
+++ b/solution.py
@@ -94,8 +94,10 @@
     cs = col * 2 + slab
     mesh_id = pl.DeviceIdType.MESH
 
+    order = [i ^ (i // 2) for i in range(1, n)]
+
     def peer(k):
-        return jnp.bitwise_xor(me, jnp.where(col == 0, k, n - k))
+        return jnp.bitwise_xor(me, jnp.where(col == 0, order[k - 1], order[n - 1 - k]))
 
     barrier = pltpu.get_barrier_semaphore()
     for k in range(1, n):

time: 488 us -> 491 us (level)
  the two profiles are of different devices: /device:TPU:8 before, /device:TPU:65 now
where the time goes in v13:
time: 491 us; the launch traced here: 484 us
  other arithmetic  211 us (43%)
  Pallas kernels  191 us (39%)
  matrix products  57.3 us (12%)
  local copies, waits for them, and re-layouts  19.9 us (4%)
    pallas_call x1, Pallas kernels, exchange(): pl.pallas_call(functools.partial(exchange_kernel, n, width), out_shape=(j...  109 us
    another operation x24, other arithmetic, cholesky_solve(): lax.linalg.cholesky(a[lo:lo + block, lo:lo + block], symmetrize_input=False)  99.7 us
    another operation x16, other arithmetic, cholesky_solve(): inv = lax.linalg.triangular_solve(lkk, eye, left_side=True, lower=True)  84.1 us
    pallas_call x1, Pallas kernels, lower_psum(): pl.pallas_call(functools.partial(reduce_kernel, n, parts), out_shape=jax....  82.7 us
    unnamed x139, local copies, waits for them, and re-layouts  17.8 us
    dot_general x1, matrix products, shards(): jnp.dot(centered, centered.T, preferred_element_type=jnp.float32)  14.2 us
    dot_general x7, matrix products, cholesky_solve(): jnp.dot(panel, panel.T, precision=hi)  13.7 us

profile of v13, /device:TPU:65, one launch (start us, length us, event | category | flops | bytes accessed | tf_op | source)
XLA Modules:
  0.0 483.6 jit_solution(10925866888812372834)
XLA Ops:
  0.0 108.7 %shard_map.28 = (bf16[32,32,16,256]{3,2,1,0:T(8,128)(2,1)}, f32[32,1,32]{2,1,0:T(1,128)}) custom-call(bf16[32,16,8192]{2,1,0:T(8,128)(2,1)} %jac_ref.1, f32[1,32]{1,0:T(1,128)} %bitcast.454), custom_call_target="tpu_custom_call" | custom-call | tf_op jit(solution)/shard_map/pallas_call | solution.py:70
  108.7 4.5 convert_reduce_fusion
  113.2 8.9 %fusion.1 = bf16[32,32,16,256]{3,2,1,0:T(8,128)(2,1)} fusion(bf16[32,32,16,256]{3,2,1,0:T(8,128)(2,1)} %get-tuple-element.93, f32[16,256]{1,0:T(8,128)S(1)} %broadcast_multiply_fusion.1), kind=kLoop, calls=%fused_computation.3 | loop fusion | flops 16777216 | bytes 16793600 | tf_op jit(solution)/shard_map/convert_element_type | solution.py:245
  122.1 14.2 %fusion.4 = f32[1024,1024]{1,0:T(8,128)S(1)} fusion(bf16[1024,16,256]{2,1,0:T(8,128)(2,1)} %bitcast.438), kind=kOutput, calls=%fused_computation.12 | convolution fusion | flops 8589934592 | bytes 12582912 | tf_op jit(solution)/shard_map/dot_general | solution.py:247
  138.4 82.7 %shard_map.29 = f32[32,144,128]{2,1,0:T(8,128)} custom-call(f32[32,144,128]{2,1,0:T(8,128)} %bitcast.439), custom_call_target="tpu_custom_call" | custom-call | tf_op jit(solution)/shard_map/pallas_call | solution.py:174
  231.5 2.0 copy-done
  234.8 2.6 select_add_fusion
  237.4 1.9 copy-done.2
  239.4 11.7 %custom-call.20 = f32[128,128]{1,0:T(8,128)S(1)} custom-call(f32[128,128]{1,0:T(8,128)S(1)} %slice.676), custom_call_target="Cholesky" | custom-call | tf_op jit(solution)/shard_map/cholesky/custom-call.1 | solution.py:211
  252.4 9.8 %custom-call.21 = f32[1,128,128]{1,2,0:T(8,128)S(1)} custom-call(f32[1,128,128]{2,1,0:T(8,128)S(1)} %fusion.55), custom_call_target="InvertDiagBlocksLowerTriangular" | custom-call | tf_op jit(solution)/shard_map/triangular_solve/custom-call.0 | solution.py:212
  264.2 1.6 fusion.27
  266.5 5.0 %slice_add_fusion = f32[896,896]{1,0:T(8,128)S(1)} fusion(f32[1024,1024]{1,0:T(8,128)} %copy-done.2, f32[896,128]{1,0:T(8,128)S(1)} %fusion.27), kind=kOutput, calls=%fused_computation.10 | convolution fusion | flops 1234731008 | bytes 7340032 | tf_op jit(solution)/shard_map/dot_general | solution.py:218
  271.5 1.7 copy-done.4
  273.2 11.7 %custom-call.22 = f32[128,128]{1,0:T(8,128)S(1)} custom-call(f32[128,128]{1,0:T(8,128)S(1)} %slice.680), custom_call_target="Cholesky" | custom-call | tf_op jit(solution)/shard_map/cholesky/custom-call.1 | solution.py:211
  286.3 9.8 %custom-call.23 = f32[1,128,128]{1,2,0:T(8,128)S(1)} custom-call(f32[1,128,128]{2,1,0:T(8,128)S(1)} %fusion.56), custom_call_target="InvertDiagBlocksLowerTriangular" | custom-call | tf_op jit(solution)/shard_map/triangular_solve/custom-call.0 | solution.py:212
  298.6 3.7 slice_add_fusion.1
  302.3 11.9 %custom-call.24 = f32[128,128]{1,0:T(8,128)S(1)} custom-call(f32[128,128]{1,0:T(8,128)S(1)} %slice.684), custom_call_target="Cholesky" | custom-call | tf_op jit(solution)/shard_map/cholesky/custom-call.1 | solution.py:211
  315.6 9.8 %custom-call.25 = f32[1,128,128]{1,2,0:T(8,128)S(1)} custom-call(f32[1,128,128]{2,1,0:T(8,128)S(1)} %fusion.57), custom_call_target="InvertDiagBlocksLowerTriangular" | custom-call | tf_op jit(solution)/shard_map/triangular_solve/custom-call.0 | solution.py:212
  330.8 11.7 %custom-call.26 = f32[128,128]{1,0:T(8,128)S(1)} custom-call(f32[128,128]{1,0:T(8,128)S(1)} %slice.687), custom_call_target="Cholesky" | custom-call | tf_op jit(solution)/shard_map/cholesky/custom-call.1 | solution.py:211
  343.8 10.2 %custom-call.27 = f32[1,128,128]{1,2,0:T(8,128)S(1)} custom-call(f32[1,128,128]{2,1,0:T(8,128)S(1)} %fusion.58), custom_call_target="InvertDiagBlocksLowerTriangular" | custom-call | tf_op jit(solution)/shard_map/triangular_solve/custom-call.0 | solution.py:212
  357.6 2.2 fusion.7
  359.9 11.7 %custom-call.28 = f32[128,128]{1,0:T(8,128)S(1)} custom-call(f32[128,128]{1,0:T(8,128)S(1)} %slice.690), custom_call_target="Cholesky" | custom-call | tf_op jit(solution)/shard_map/cholesky/custom-call.1 | solution.py:211
  372.9 9.8 %custom-call.29 = f32[1,128,128]{1,2,0:T(8,128)S(1)} custom-call(f32[1,128,128]{2,1,0:T(8,128)S(1)} %fusion.59), custom_call_target="InvertDiagBlocksLowerTriangular" | custom-call | tf_op jit(solution)/shard_map/triangular_solve/custom-call.0 | solution.py:212
  385.2 11.9 %custom-call.30 = f32[128,128]{1,0:T(8,128)S(1)} custom-call(f32[128,128]{1,0:T(8,128)S(1)} %slice.693), custom_call_target="Cholesky" | custom-call | tf_op jit(solution)/shard_map/cholesky/custom-call.1 | solution.py:211
  398.4 9.8 %custom-call.31 = f32[1,128,128]{1,2,0:T(8,128)S(1)} custom-call(f32[1,128,128]{2,1,0:T(8,128)S(1)} %fusion.60), custom_call_target="InvertDiagBlocksLowerTriangular" | custom-call | tf_op jit(solution)/shard_map/triangular_solve/custom-call.0 | solution.py:212
  411.0 11.7 %custom-call.32 = f32[128,128]{1,0:T(8,128)S(1)} custom-call(f32[128,128]{1,0:T(8,128)S(1)} %slice.696), custom_call_target="Cholesky" | custom-call | tf_op jit(solution)/shard_map/cholesky/custom-call.1 | solution.py:211
  424.1 9.8 %custom-call.33 = f32[1,128,128]{1,2,0:T(8,128)S(1)} custom-call(f32[1,128,128]{2,1,0:T(8,128)S(1)} %fusion.61), custom_call_target="InvertDiagBlocksLowerTriangular" | custom-call | tf_op jit(solution)/shard_map/triangular_solve/custom-call.0 | solution.py:212
  435.1 11.9 %custom-call.34 = f32[128,128]{1,0:T(8,128)S(1)} custom-call(f32[128,128]{1,0:T(8,128)S(1)} %fusion.10), custom_call_target="Cholesky" | custom-call | tf_op jit(solution)/shard_map/cholesky/custom-call.1 | solution.py:211
  448.4 9.8 %custom-call.35 = f32[1,128,128]{1,2,0:T(8,128)S(1)} custom-call(f32[1,128,128]{2,1,0:T(8,128)S(1)} %fusion.62), custom_call_target="InvertDiagBlocksLowerTriangular" | custom-call | tf_op jit(solution)/shard_map/triangular_solve/custom-call.0 | solution.py:212
  466.2 4.4 fusion.124
  470.6 3.6 fusion.123
  477.3 5.5 %multiply_reduce_fusion = f32[16,256]{1,0:T(8,128)S(1)} fusion(f32[32,32]{1,0:T(8,128)S(1)} %concatenate.137, f32[16,256]{1,0:T(8,128)S(1)} %broadcast_multiply_fusion.1, bf16[32,32,16,256]{3,2,1,0:T(8,128)(2,1)} %get-tuple-element.93), kind=kLoop, calls=%fused_computation.4 | loop fusion | flops 29356032 | bytes 8425472 | tf_op jit(solution)/shard_map/reduce_sum | solution.py:252
  (265 shorter events, 53.7 us)
Async XLA Ops:
  136.9 1.4 copy-start.6
  221.1 9.9 %copy-start.3 = (f32[32,144,128]{2,1,0:T(8,128)S(1)}, f32[32,144,128]{2,1,0:T(8,128)}, u32[]{:S(2)}) copy-start(f32[32,144,128]{2,1,0:T(8,128)} %shard_map.29) | copy-start | bytes 7077892
  228.2 3.2 copy-start.12
  231.5 2.0 copy-start
  234.8 27.7 %copy-start.14 = (f32[32,1,32]{2,1,0:T(1,128)S(1)}, f32[32,1,32]{2,1,0:T(1,128)}, u32[]{:S(2)}) copy-start(f32[32,1,32]{2,1,0:T(1,128)} %get-tuple-element.94) | copy-start | bytes 12292
  237.4 2.0 copy-start.2
  262.5 9.0 %copy-start.11 = (f32[128,128]{1,0:T(8,128)}, f32[128,128]{1,0:T(8,128)S(1)}, u32[]{:S(2)}) copy-start(f32[128,128]{1,0:T(8,128)S(1)} %fusion.49) | copy-start | bytes 196612
  264.2 1.6 copy-start.20
  271.5 1.7 copy-start.4
  296.4 2.2 copy-start.7
  296.5 5.7 %copy-start.16 = (f32[1,128]{1,0:T(1,128)}, f32[1,128]{1,0:T(1,128)S(1)}, u32[]{:S(2)}) copy-start(f32[1,128]{1,0:T(1,128)S(1)} %fusion.112) | copy-start | bytes 1540
  298.6 27.1 %copy-start.15 = (f32[768]{0:T(1024)}, f32[768]{0:T(1024)S(1)}, u32[]{:S(2)}) copy-start(f32[768]{0:T(1024)S(1)} %slice_subtract_fusion.1) | copy-start | bytes 9220
  325.7 1.1 copy-start.9
  325.9 0.9 copy-start.19
  329.5 1.2 copy-start.5
  355.2 4.7 copy-start.17
  359.8 102.8 %copy-start.10 = (f32[128,128]{1,0:T(8,128)S(1)}, f32[128,128]{1,0:T(8,128)}, u32[]{:S(2)}) copy-start(f32[128,128]{1,0:T(8,128)} %copy-done.9) | copy-start | bytes 196612
  359.8 104.0 %copy-start.8 = (f32[128,128]{1,0:T(8,128)S(1)}, f32[128,128]{1,0:T(8,128)}, u32[]{:S(2)}) copy-start(f32[128,128]{1,0:T(8,128)} %copy-done.7) | copy-start | bytes 196612
  383.2 0.7 copy-start.18
  466.1 4.6 copy-start.1
  466.2 8.1 %copy-start.13 = (f32[8,128,128]{2,1,0:T(8,128)S(1)}, f32[8,128,128]{2,1,0:T(8,128)}, u32[]{:S(2)}) copy-start(f32[8,128,128]{2,1,0:T(8,128)} %copy-done.12) | copy-start | bytes 1572868

commit v14 on v12

--- a/solution.py
+++ b/solution.py
@@ -198,7 +198,7 @@
     return lower, diag
 
 
-def cholesky_solve(a, rhs, block=128):
+def cholesky_solve(a, rhs, shift, block=128):
     n = a.shape[0]
     nb = n // block
     hi = lax.Precision.HIGHEST
@@ -206,7 +206,8 @@
     inverses, panels, factors = [], [], []
     for k in range(nb):
         lo = k * block
-        lkk = lax.linalg.cholesky(a[lo:lo + block, lo:lo + block], symmetrize_input=False)
+        lkk = lax.linalg.cholesky(a[lo:lo + block, lo:lo + block] + shift * eye,
+                                  symmetrize_input=False)
         inv = lax.linalg.triangular_solve(lkk, eye, left_side=True, lower=True)
         factors.append(lkk)
         inverses.append(inv)
@@ -245,8 +246,8 @@
     partial_gram = jnp.dot(centered, centered.T, preferred_element_type=jnp.float32)
     parts = lax.psum(1, ("col", "slab"))
     gram, diag = lower_psum(partial_gram, n, parts)
-    shift = 0.01 * jnp.trace(gram) / samples
-    coeffs = cholesky_solve(gram + shift * jnp.eye(samples, dtype=jnp.float32), eps)
+    shift = 0.01 * jnp.sum(jnp.trace(diag, axis1=1, axis2=2)) / samples
+    coeffs = cholesky_solve(gram, eps, shift)
     delta = jnp.sum(coeffs[:, None] * centered.astype(jnp.float32), axis=0)
     hi = lax.Precision.HIGHEST
     blocked = coeffs.reshape(diag.shape[0], diag.shape[1])

time: 488 us -> 525 us (1.076)
  local copies, waits for them, and re-layouts: 19.9 us -> 55.8 us
    unnamed x139 -> x163, local copies, waits for them, and re-layouts: 17.8 us -> 52.1 us
    another operation x24 -> x25, other arithmetic: 99.7 us -> 99.7 us  [cholesky_solve(): lax.linalg.cholesky(a[lo:lo + block, lo:lo + block] + shift * eye, symmet...]
where the time goes in v14:
time: 525 us; the launch traced here: 517 us
  other arithmetic  212 us (40%)
  Pallas kernels  187 us (36%)
  matrix products  58.6 us (11%)
  local copies, waits for them, and re-layouts  55.8 us (11%)
    pallas_call x1, Pallas kernels, exchange(): pl.pallas_call(functools.partial(exchange_kernel, n, width), out_shape=(j...  110 us
    another operation x25, other arithmetic, cholesky_solve(): lax.linalg.cholesky(a[lo:lo + block, lo:lo + block] + shift * eye, symmet...  99.7 us
    another operation x16, other arithmetic, cholesky_solve(): inv = lax.linalg.triangular_solve(lkk, eye, left_side=True, lower=True)  84.1 us
    pallas_call x1, Pallas kernels, lower_psum(): pl.pallas_call(functools.partial(reduce_kernel, n, parts), out_shape=jax....  77.5 us
    unnamed x163, local copies, waits for them, and re-layouts  52.1 us
    dot_general x1, matrix products, shards(): jnp.dot(centered, centered.T, preferred_element_type=jnp.float32)  14.2 us
    dot_general x7, matrix products, cholesky_solve(): jnp.dot(panel, panel.T, precision=hi)  13.7 us

profile of v14, /device:TPU:8, one launch (start us, length us, event | category | flops | bytes accessed | tf_op | source)
XLA Modules:
  0.0 517.0 jit_solution(13881095299717458022)
XLA Ops:
  0.0 109.9 %shard_map.28 = (bf16[32,32,16,256]{3,2,1,0:T(8,128)(2,1)}, f32[32,1,32]{2,1,0:T(1,128)}) custom-call(bf16[32,16,8192]{2,1,0:T(8,128)(2,1)} %jac_ref.1, f32[1,32]{1,0:T(1,128)} %bitcast.537), custom_call_target="tpu_custom_call" | custom-call | tf_op jit(solution)/shard_map/pallas_call | solution.py:70
  109.9 4.5 convert_reduce_fusion
  114.4 8.9 %fusion.1 = bf16[32,32,16,256]{3,2,1,0:T(8,128)(2,1)} fusion(bf16[32,32,16,256]{3,2,1,0:T(8,128)(2,1)} %get-tuple-element.93, f32[16,256]{1,0:T(8,128)S(1)} %broadcast_multiply_fusion.1), kind=kLoop, calls=%fused_computation.3 | loop fusion | flops 16777216 | bytes 16793600 | tf_op jit(solution)/shard_map/convert_element_type | solution.py:244
  123.3 14.2 %fusion.4 = f32[1024,1024]{1,0:T(8,128)S(1)} fusion(bf16[1024,16,256]{2,1,0:T(8,128)(2,1)} %bitcast.521), kind=kOutput, calls=%fused_computation.9 | convolution fusion | flops 8589934592 | bytes 12582912 | tf_op jit(solution)/shard_map/dot_general | solution.py:246
  138.1 1.5 copy-done.3
  139.6 77.5 %shard_map.29 = f32[32,144,128]{2,1,0:T(8,128)} custom-call(f32[32,144,128]{2,1,0:T(8,128)} %bitcast.522), custom_call_target="tpu_custom_call" | custom-call | tf_op jit(solution)/shard_map/pallas_call | solution.py:172
  251.8 11.7 %custom-call.20 = f32[128,128]{1,0:T(8,128)S(1)} custom-call(f32[128,128]{1,0:T(8,128)S(1)} %get-tuple-element.96), custom_call_target="Cholesky" | custom-call | tf_op jit(solution)/shard_map/cholesky/custom-call.1 | solution.py:209
  264.9 9.8 %custom-call.21 = f32[1,128,128]{1,2,0:T(8,128)S(1)} custom-call(f32[1,128,128]{2,1,0:T(8,128)S(1)} %fusion.60), custom_call_target="InvertDiagBlocksLowerTriangular" | custom-call | tf_op jit(solution)/shard_map/triangular_solve/custom-call.0 | solution.py:211
  296.2 1.5 fusion.32
  298.4 5.0 slice_add_fusion
  303.5 1.7 copy-done.1
  305.2 11.7 %custom-call.22 = f32[128,128]{1,0:T(8,128)S(1)} custom-call(f32[128,128]{1,0:T(8,128)S(1)} %select_add_fusion.5), custom_call_target="Cholesky" | custom-call | tf_op jit(solution)/shard_map/cholesky/custom-call.1 | solution.py:209
  318.2 9.8 %custom-call.23 = f32[1,128,128]{1,2,0:T(8,128)S(1)} custom-call(f32[1,128,128]{2,1,0:T(8,128)S(1)} %fusion.61), custom_call_target="InvertDiagBlocksLowerTriangular" | custom-call | tf_op jit(solution)/shard_map/triangular_solve/custom-call.0 | solution.py:211
  328.5 1.5 fusion.34
  330.5 3.7 slice_add_fusion.1
  334.3 11.9 %custom-call.24 = f32[128,128]{1,0:T(8,128)S(1)} custom-call(f32[128,128]{1,0:T(8,128)S(1)} %select_add_fusion.4), custom_call_target="Cholesky" | custom-call | tf_op jit(solution)/shard_map/cholesky/custom-call.1 | solution.py:209
  347.5 9.8 %custom-call.25 = f32[1,128,128]{1,2,0:T(8,128)S(1)} custom-call(f32[1,128,128]{2,1,0:T(8,128)S(1)} %fusion.62), custom_call_target="InvertDiagBlocksLowerTriangular" | custom-call | tf_op jit(solution)/shard_map/triangular_solve/custom-call.0 | solution.py:211
  360.1 1.4 slice_add_fusion.2
  362.8 11.7 %custom-call.26 = f32[128,128]{1,0:T(8,128)S(1)} custom-call(f32[128,128]{1,0:T(8,128)S(1)} %select_add_fusion.3), custom_call_target="Cholesky" | custom-call | tf_op jit(solution)/shard_map/cholesky/custom-call.1 | solution.py:209
  375.8 10.2 %custom-call.27 = f32[1,128,128]{1,2,0:T(8,128)S(1)} custom-call(f32[1,128,128]{2,1,0:T(8,128)S(1)} %fusion.63), custom_call_target="InvertDiagBlocksLowerTriangular" | custom-call | tf_op jit(solution)/shard_map/triangular_solve/custom-call.0 | solution.py:211
  389.6 2.2 fusion.7
  391.8 11.7 %custom-call.28 = f32[128,128]{1,0:T(8,128)S(1)} custom-call(f32[128,128]{1,0:T(8,128)S(1)} %select_add_fusion.2), custom_call_target="Cholesky" | custom-call | tf_op jit(solution)/shard_map/cholesky/custom-call.1 | solution.py:209
  404.9 9.8 %custom-call.29 = f32[1,128,128]{1,2,0:T(8,128)S(1)} custom-call(f32[1,128,128]{2,1,0:T(8,128)S(1)} %fusion.64), custom_call_target="InvertDiagBlocksLowerTriangular" | custom-call | tf_op jit(solution)/shard_map/triangular_solve/custom-call.0 | solution.py:211
  417.2 11.9 %custom-call.30 = f32[128,128]{1,0:T(8,128)S(1)} custom-call(f32[128,128]{1,0:T(8,128)S(1)} %select_add_fusion.1), custom_call_target="Cholesky" | custom-call | tf_op jit(solution)/shard_map/cholesky/custom-call.1 | solution.py:209
  430.4 9.8 %custom-call.31 = f32[1,128,128]{1,2,0:T(8,128)S(1)} custom-call(f32[1,128,128]{2,1,0:T(8,128)S(1)} %fusion.65), custom_call_target="InvertDiagBlocksLowerTriangular" | custom-call | tf_op jit(solution)/shard_map/triangular_solve/custom-call.0 | solution.py:211
  443.0 11.7 %custom-call.32 = f32[128,128]{1,0:T(8,128)S(1)} custom-call(f32[128,128]{1,0:T(8,128)S(1)} %select_add_fusion), custom_call_target="Cholesky" | custom-call | tf_op jit(solution)/shard_map/cholesky/custom-call.1 | solution.py:209
  456.1 9.8 %custom-call.33 = f32[1,128,128]{1,2,0:T(8,128)S(1)} custom-call(f32[1,128,128]{2,1,0:T(8,128)S(1)} %fusion.66), custom_call_target="InvertDiagBlocksLowerTriangular" | custom-call | tf_op jit(solution)/shard_map/triangular_solve/custom-call.0 | solution.py:211
  467.2 11.9 %custom-call.34 = f32[128,128]{1,0:T(8,128)S(1)} custom-call(f32[128,128]{1,0:T(8,128)S(1)} %fusion.11), custom_call_target="Cholesky" | custom-call | tf_op jit(solution)/shard_map/cholesky/custom-call.1 | solution.py:209
  480.4 9.8 %custom-call.35 = f32[1,128,128]{1,2,0:T(8,128)S(1)} custom-call(f32[1,128,128]{2,1,0:T(8,128)S(1)} %fusion.67), custom_call_target="InvertDiagBlocksLowerTriangular" | custom-call | tf_op jit(solution)/shard_map/triangular_solve/custom-call.0 | solution.py:211
  497.6 4.3 fusion.149
  501.9 5.8 %fusion.148 = f32[1,1024]{1,0:T(1,128)S(1)} fusion(f32[1024,1024]{1,0:T(8,128)} %get-tuple-element.95, f32[1024,1]{0,1:T(1,128)S(1)} %bitcast.524), kind=kOutput, calls=%fused_computation.355 | convolution fusion | flops 12582912 | bytes 4202496 | tf_op jit(solution)/shard_map/dot_general | solution.py:254
  510.6 5.5 %multiply_reduce_fusion = f32[16,256]{1,0:T(8,128)S(1)} fusion(f32[32,32]{1,0:T(8,128)S(1)} %concatenate.142, f32[16,256]{1,0:T(8,128)S(1)} %broadcast_multiply_fusion.1, bf16[32,32,16,256]{3,2,1,0:T(8,128)(2,1)} %get-tuple-element.93), kind=kLoop, calls=%fused_computation.4 | loop fusion | flops 29356032 | bytes 8425472 | tf_op jit(solution)/shard_map/reduce_sum | solution.py:251
  (290 shorter events, 91.4 us)
Async XLA Ops:
  138.1 1.5 copy-start.3
  217.1 12.5 %copy-start = (f32[32,144,128]{2,1,0:T(8,128)S(1)}, f32[32,144,128]{2,1,0:T(8,128)}, u32[]{:S(2)}) copy-start(f32[32,144,128]{2,1,0:T(8,128)} %shard_map.29) | copy-start | bytes 7077892
  224.2 0.8 copy-start.4
  228.4 46.6 %copy-start.11 = (f32[32,1,32]{2,1,0:T(1,128)S(1)}, f32[32,1,32]{2,1,0:T(1,128)}, u32[]{:S(2)}) copy-start(f32[32,1,32]{2,1,0:T(1,128)} %get-tuple-element.94) | copy-start | bytes 12292
  275.0 28.5 %copy-start.10 = (f32[128,128]{1,0:T(8,128)}, f32[128,128]{1,0:T(8,128)S(1)}, u32[]{:S(2)}) copy-start(f32[128,128]{1,0:T(8,128)S(1)} %fusion.54) | copy-start | bytes 196612
  276.6 21.2 %copy-start.18 = (f32[1,128]{1,0:T(1,128)}, f32[1,128]{1,0:T(1,128)S(1)}, u32[]{:S(2)}) copy-start(f32[1,128]{1,0:T(1,128)S(1)} %fusion.146) | copy-start | bytes 1540
  303.5 1.7 copy-start.1
  328.3 2.2 copy-start.6
  328.5 2.0 copy-start.13
  330.5 27.1 %copy-start.12 = (f32[768]{0:T(1024)}, f32[768]{0:T(1024)S(1)}, u32[]{:S(2)}) copy-start(f32[768]{0:T(1024)S(1)} %slice_subtract_fusion.1) | copy-start | bytes 9220
  357.7 1.1 copy-start.8
  357.8 0.9 copy-start.17
  361.5 1.2 copy-start.2
  387.2 4.6 copy-start.14
  391.8 102.2 %copy-start.9 = (f32[128,128]{1,0:T(8,128)S(1)}, f32[128,128]{1,0:T(8,128)}, u32[]{:S(2)}) copy-start(f32[128,128]{1,0:T(8,128)} %copy-done.8) | copy-start | bytes 196612
  415.2 0.7 copy-start.16
  415.2 80.0 %copy-start.7 = (f32[128,128]{1,0:T(8,128)S(1)}, f32[128,128]{1,0:T(8,128)}, u32[]{:S(2)}) copy-start(f32[128,128]{1,0:T(8,128)} %copy-done.6) | copy-start | bytes 196612
  417.1 75.5 %copy-start.15 = (f32[1,128]{1,0:T(1,128)S(1)}, f32[1,128]{1,0:T(1,128)}, u32[]{:S(2)}) copy-start(f32[1,128]{1,0:T(1,128)} %copy-done.14) | copy-start | bytes 1540
  497.6 10.1 %copy-start.5 = (f32[8,128,128]{2,1,0:T(8,128)S(1)}, f32[8,128,128]{2,1,0:T(8,128)}, u32[]{:S(2)}) copy-start(f32[8,128,128]{2,1,0:T(8,128)} %copy-done.4) | copy-start | bytes 1572868

commit v15 on v12

--- a/solution.py
+++ b/solution.py
@@ -162,11 +162,11 @@
 
 
 def lower_psum(partial, n, parts, block=128):
-    size = partial.shape[0]
+    size = partial[-1].shape[1]
     nb = size // block
     pairs = [(i, j) for i in range(nb) for j in range(i + 1)]
     packed = jnp.concatenate(
-        [partial[i * block:(i + 1) * block, j * block:(j + 1) * block] for i, j in pairs], axis=0)
+        [partial[i][:, j * block:(j + 1) * block] for i, j in pairs], axis=0)
     rows = packed.shape[0] // n
     packed = packed.reshape(n, rows, block)
     reduced = pl.pallas_call(
@@ -242,9 +242,10 @@
     centered = (
         ((values - mean_row) / root_count).astype(jnp.bfloat16).reshape(samples, slab_count * width)
     )
-    partial_gram = jnp.dot(centered, centered.T, preferred_element_type=jnp.float32)
+    strips = [jnp.dot(centered[i * 128:(i + 1) * 128], centered[:(i + 1) * 128].T,
+                      preferred_element_type=jnp.float32) for i in range(samples // 128)]
     parts = lax.psum(1, ("col", "slab"))
-    gram, diag = lower_psum(partial_gram, n, parts)
+    gram, diag = lower_psum(strips, n, parts)
     shift = 0.01 * jnp.trace(gram) / samples
     coeffs = cholesky_solve(gram + shift * jnp.eye(samples, dtype=jnp.float32), eps)
     delta = jnp.sum(coeffs[:, None] * centered.astype(jnp.float32), axis=0)

time: 488 us -> 497 us (1.018)
  other arithmetic: 211 us -> 224 us
    convert_element_type x0 -> x1, other arithmetic: none -> 11.5 us  [shards(): values = columns.astype(jnp.float32)]
    dot_general x1 -> x8, matrix products: 14.2 us -> 12.6 us  [shards(): jnp.dot(centered[i * 128:(i + 1) * 128], centered[:(i + 1) * 128].T, pref...]
where the time goes in v15:
time: 497 us; the launch traced here: 491 us
  other arithmetic  224 us (45%)
  Pallas kernels  187 us (38%)
  matrix products  55.9 us (11%)
  local copies, waits for them, and re-layouts  19.7 us (4%)
    pallas_call x1, Pallas kernels, exchange(): pl.pallas_call(functools.partial(exchange_kernel, n, width), out_shape=(j...  110 us
    another operation x24, other arithmetic, cholesky_solve(): lax.linalg.cholesky(a[lo:lo + block, lo:lo + block], symmetrize_input=False)  100 us
    another operation x16, other arithmetic, cholesky_solve(): inv = lax.linalg.triangular_solve(lkk, eye, left_side=True, lower=True)  84.2 us
    pallas_call x1, Pallas kernels, lower_psum(): pl.pallas_call(functools.partial(reduce_kernel, n, parts), out_shape=jax....  77.5 us
    unnamed x139, local copies, waits for them, and re-layouts  17.6 us
    dot_general x7, matrix products, cholesky_solve(): jnp.dot(panel, panel.T, precision=hi)  13.7 us
    dot_general x8, matrix products, shards(): jnp.dot(centered[i * 128:(i + 1) * 128], centered[:(i + 1) * 128].T, pref...  12.6 us
    convert_element_type x1, other arithmetic, shards(): values = columns.astype(jnp.float32)  11.5 us

profile of v15, /device:TPU:8, one launch (start us, length us, event | category | flops | bytes accessed | tf_op | source)
XLA Modules:
  0.0 490.9 jit_solution(14571101843923905883)
XLA Ops:
  0.0 109.8 %shard_map.28 = (bf16[32,32,16,256]{3,2,1,0:T(8,128)(2,1)}, f32[32,1,32]{2,1,0:T(1,128)}) custom-call(bf16[32,16,8192]{2,1,0:T(8,128)(2,1)} %jac_ref.1, f32[1,32]{1,0:T(1,128)} %bitcast.472), custom_call_target="tpu_custom_call" | custom-call | tf_op jit(solution)/shard_map/pallas_call | solution.py:70
  109.8 4.5 convert_reduce_fusion
  114.3 11.5 %bitcast_convert_fusion = f32[1024,16,256]{2,1,0:T(8,128)} fusion(bf16[32,32,16,256]{3,2,1,0:T(8,128)(2,1)} %get-tuple-element.93), kind=kLoop, calls=%fused_computation.336 | loop fusion | flops 4194304 | bytes 25165824 | tf_op jit(solution)/shard_map/convert_element_type | solution.py:240
  125.9 9.9 %fusion.1 = bf16[1024,16,256]{2,0,1:T(8,128)(2,1)S(1)} fusion(f32[1024,16,256]{2,1,0:T(8,128)} %bitcast_convert_fusion, f32[16,256]{1,0:T(8,128)S(1)} %broadcast_multiply_fusion.1), kind=kLoop, calls=%fused_computation.2 | loop fusion | flops 12582912 | bytes 25182208 | tf_op jit(solution)/shard_map/convert_element_type | solution.py:243
  141.4 2.1 fusion.19
  143.6 2.4 fusion.16
  146.1 2.8 convolution_bitcast_fusion
  150.4 77.5 %shard_map.29 = f32[32,144,128]{2,1,0:T(8,128)} custom-call(f32[32,144,128]{2,1,0:T(8,128)} %bitcast.457), custom_call_target="tpu_custom_call" | custom-call | tf_op jit(solution)/shard_map/pallas_call | solution.py:172
  241.7 2.6 select_add_fusion
  244.3 2.0 copy-done.2
  246.2 11.9 %custom-call.20 = f32[128,128]{1,0:T(8,128)S(1)} custom-call(f32[128,128]{1,0:T(8,128)S(1)} %slice.759), custom_call_target="Cholesky" | custom-call | tf_op jit(solution)/shard_map/cholesky/custom-call.1 | solution.py:209
  259.5 9.8 %custom-call.21 = f32[1,128,128]{1,2,0:T(8,128)S(1)} custom-call(f32[1,128,128]{2,1,0:T(8,128)S(1)} %fusion.89), custom_call_target="InvertDiagBlocksLowerTriangular" | custom-call | tf_op jit(solution)/shard_map/triangular_solve/custom-call.0 | solution.py:210
  273.5 4.8 slice_add_fusion
  280.1 11.7 %custom-call.22 = f32[128,128]{1,0:T(8,128)S(1)} custom-call(f32[128,128]{1,0:T(8,128)S(1)} %slice.763), custom_call_target="Cholesky" | custom-call | tf_op jit(solution)/shard_map/cholesky/custom-call.1 | solution.py:209
  293.1 10.2 %custom-call.23 = f32[1,128,128]{1,2,0:T(8,128)S(1)} custom-call(f32[1,128,128]{2,1,0:T(8,128)S(1)} %fusion.90), custom_call_target="InvertDiagBlocksLowerTriangular" | custom-call | tf_op jit(solution)/shard_map/triangular_solve/custom-call.0 | solution.py:210
  305.8 3.7 slice_add_fusion.1
  309.5 11.7 %custom-call.24 = f32[128,128]{1,0:T(8,128)S(1)} custom-call(f32[128,128]{1,0:T(8,128)S(1)} %slice.767), custom_call_target="Cholesky" | custom-call | tf_op jit(solution)/shard_map/cholesky/custom-call.1 | solution.py:209
  322.7 9.8 %custom-call.25 = f32[1,128,128]{1,2,0:T(8,128)S(1)} custom-call(f32[1,128,128]{2,1,0:T(8,128)S(1)} %fusion.91), custom_call_target="InvertDiagBlocksLowerTriangular" | custom-call | tf_op jit(solution)/shard_map/triangular_solve/custom-call.0 | solution.py:210
  338.1 11.7 %custom-call.26 = f32[128,128]{1,0:T(8,128)S(1)} custom-call(f32[128,128]{1,0:T(8,128)S(1)} %slice.770), custom_call_target="Cholesky" | custom-call | tf_op jit(solution)/shard_map/cholesky/custom-call.1 | solution.py:209
  351.1 9.8 %custom-call.27 = f32[1,128,128]{1,2,0:T(8,128)S(1)} custom-call(f32[1,128,128]{2,1,0:T(8,128)S(1)} %fusion.92), custom_call_target="InvertDiagBlocksLowerTriangular" | custom-call | tf_op jit(solution)/shard_map/triangular_solve/custom-call.0 | solution.py:210
  364.5 2.2 fusion.14
  366.8 11.9 %custom-call.28 = f32[128,128]{1,0:T(8,128)S(1)} custom-call(f32[128,128]{1,0:T(8,128)S(1)} %slice.773), custom_call_target="Cholesky" | custom-call | tf_op jit(solution)/shard_map/cholesky/custom-call.1 | solution.py:209
  380.0 9.8 %custom-call.29 = f32[1,128,128]{1,2,0:T(8,128)S(1)} custom-call(f32[1,128,128]{2,1,0:T(8,128)S(1)} %fusion.93), custom_call_target="InvertDiagBlocksLowerTriangular" | custom-call | tf_op jit(solution)/shard_map/triangular_solve/custom-call.0 | solution.py:210
  392.3 11.7 %custom-call.30 = f32[128,128]{1,0:T(8,128)S(1)} custom-call(f32[128,128]{1,0:T(8,128)S(1)} %slice.776), custom_call_target="Cholesky" | custom-call | tf_op jit(solution)/shard_map/cholesky/custom-call.1 | solution.py:209
  405.4 9.8 %custom-call.31 = f32[1,128,128]{1,2,0:T(8,128)S(1)} custom-call(f32[1,128,128]{2,1,0:T(8,128)S(1)} %fusion.94), custom_call_target="InvertDiagBlocksLowerTriangular" | custom-call | tf_op jit(solution)/shard_map/triangular_solve/custom-call.0 | solution.py:210
  418.0 12.1 %custom-call.32 = f32[128,128]{1,0:T(8,128)S(1)} custom-call(f32[128,128]{1,0:T(8,128)S(1)} %slice.779), custom_call_target="Cholesky" | custom-call | tf_op jit(solution)/shard_map/cholesky/custom-call.1 | solution.py:209
  431.5 9.8 %custom-call.33 = f32[1,128,128]{1,2,0:T(8,128)S(1)} custom-call(f32[1,128,128]{2,1,0:T(8,128)S(1)} %fusion.95), custom_call_target="InvertDiagBlocksLowerTriangular" | custom-call | tf_op jit(solution)/shard_map/triangular_solve/custom-call.0 | solution.py:210
  442.6 11.7 %custom-call.34 = f32[128,128]{1,0:T(8,128)S(1)} custom-call(f32[128,128]{1,0:T(8,128)S(1)} %fusion.35), custom_call_target="Cholesky" | custom-call | tf_op jit(solution)/shard_map/cholesky/custom-call.1 | solution.py:209
  455.6 9.8 %custom-call.35 = f32[1,128,128]{1,2,0:T(8,128)S(1)} custom-call(f32[1,128,128]{2,1,0:T(8,128)S(1)} %fusion.96), custom_call_target="InvertDiagBlocksLowerTriangular" | custom-call | tf_op jit(solution)/shard_map/triangular_solve/custom-call.0 | solution.py:210
  473.6 4.4 fusion.158
  478.0 3.6 fusion.157
  484.6 5.5 %multiply_reduce_fusion = f32[16,256]{1,0:T(8,128)S(1)} fusion(bf16[32,32,16,256]{3,2,1,0:T(8,128)(2,1)} %get-tuple-element.93, f32[16,256]{1,0:T(8,128)S(1)} %broadcast_multiply_fusion.1, f32[32,32]{1,0:T(8,128)S(1)} %concatenate.136), kind=kLoop, calls=%fused_computation.3 | loop fusion | flops 29356032 | bytes 8425472 | tf_op jit(solution)/shard_map/reduce_sum | solution.py:251
  (273 shorter events, 64.6 us)
Async XLA Ops:
  149.0 1.4 copy-start.6
  228.0 9.9 %copy-start.3 = (f32[32,144,128]{2,1,0:T(8,128)S(1)}, f32[32,144,128]{2,1,0:T(8,128)}, u32[]{:S(2)}) copy-start(f32[32,144,128]{2,1,0:T(8,128)} %shard_map.29) | copy-start | bytes 7077892
  235.1 3.2 copy-start.12
  238.4 1.9 copy-start
  241.7 27.9 %copy-start.14 = (f32[32,1,32]{2,1,0:T(1,128)S(1)}, f32[32,1,32]{2,1,0:T(1,128)}, u32[]{:S(2)}) copy-start(f32[32,1,32]{2,1,0:T(1,128)} %get-tuple-element.94) | copy-start | bytes 12292
  244.3 2.0 copy-start.2
  269.6 8.8 %copy-start.11 = (f32[128,128]{1,0:T(8,128)}, f32[128,128]{1,0:T(8,128)S(1)}, u32[]{:S(2)}) copy-start(f32[128,128]{1,0:T(8,128)S(1)} %fusion.83) | copy-start | bytes 196612
  271.2 1.6 copy-start.20
  278.4 1.7 copy-start.4
  303.6 2.2 copy-start.7
  303.8 5.7 %copy-start.16 = (f32[1,128]{1,0:T(1,128)}, f32[1,128]{1,0:T(1,128)S(1)}, u32[]{:S(2)}) copy-start(f32[1,128]{1,0:T(1,128)S(1)} %fusion.146) | copy-start | bytes 1540
  305.8 27.0 %copy-start.15 = (f32[768]{0:T(1024)}, f32[768]{0:T(1024)S(1)}, u32[]{:S(2)}) copy-start(f32[768]{0:T(1024)S(1)} %slice_subtract_fusion.1) | copy-start | bytes 9220
  332.8 1.1 copy-start.9
  333.0 0.9 copy-start.19
  336.9 1.2 copy-start.5
  362.1 4.6 copy-start.17
  366.7 103.2 %copy-start.10 = (f32[128,128]{1,0:T(8,128)S(1)}, f32[128,128]{1,0:T(8,128)}, u32[]{:S(2)}) copy-start(f32[128,128]{1,0:T(8,128)} %copy-done.9) | copy-start | bytes 196612
  366.7 104.4 %copy-start.8 = (f32[128,128]{1,0:T(8,128)S(1)}, f32[128,128]{1,0:T(8,128)}, u32[]{:S(2)}) copy-start(f32[128,128]{1,0:T(8,128)} %copy-done.7) | copy-start | bytes 196612
  390.3 0.7 copy-start.18
  473.4 4.6 copy-start.1
  473.6 8.1 %copy-start.13 = (f32[8,128,128]{2,1,0:T(8,128)S(1)}, f32[8,128,128]{2,1,0:T(8,128)}, u32[]{:S(2)}) copy-start(f32[8,128,128]{2,1,0:T(8,128)} %copy-done.12) | copy-start | bytes 1572868

commit v16 on v12

--- a/solution.py
+++ b/solution.py
@@ -43,8 +43,9 @@
             src_ref=en_ref, dst_ref=en_all_ref.at[me],
             send_sem=en_send.at[t], recv_sem=en_recv.at[me],
             device_id=dev, device_id_type=pl.DeviceIdType.MESH)
+        sends.append((c, e))
+    for c, e in sends:
         e.start()
-        sends.append((c, e))
     for k in range(1, n):
         s = jnp.bitwise_xor(me, k)
         dev = (s, col, slab)

time: 488 us -> 489 us (level)
  no operation moved by 1% of the time
where the time goes in v16:
time: 489 us; the launch traced here: 481 us
  other arithmetic  211 us (43%)
  Pallas kernels  189 us (39%)
  matrix products  57.3 us (12%)
  local copies, waits for them, and re-layouts  19.9 us (4%)
    pallas_call x1, Pallas kernels, exchange(): pl.pallas_call(functools.partial(exchange_kernel, n, width), out_shape=(j...  112 us
    another operation x24, other arithmetic, cholesky_solve(): lax.linalg.cholesky(a[lo:lo + block, lo:lo + block], symmetrize_input=False)  99.7 us
    another operation x16, other arithmetic, cholesky_solve(): inv = lax.linalg.triangular_solve(lkk, eye, left_side=True, lower=True)  84.1 us
    pallas_call x1, Pallas kernels, lower_psum(): pl.pallas_call(functools.partial(reduce_kernel, n, parts), out_shape=jax....  76.8 us
    unnamed x139, local copies, waits for them, and re-layouts  17.8 us
    dot_general x1, matrix products, shards(): jnp.dot(centered, centered.T, preferred_element_type=jnp.float32)  14.2 us
    dot_general x7, matrix products, cholesky_solve(): jnp.dot(panel, panel.T, precision=hi)  13.7 us

profile of v16, /device:TPU:8, one launch (start us, length us, event | category | flops | bytes accessed | tf_op | source)
XLA Modules:
  0.0 480.8 jit_solution(15947765379692867605)
XLA Ops:
  0.0 111.8 %shard_map.28 = (bf16[32,32,16,256]{3,2,1,0:T(8,128)(2,1)}, f32[32,1,32]{2,1,0:T(1,128)}) custom-call(bf16[32,16,8192]{2,1,0:T(8,128)(2,1)} %jac_ref.1, f32[1,32]{1,0:T(1,128)} %bitcast.454), custom_call_target="tpu_custom_call" | custom-call | tf_op jit(solution)/shard_map/pallas_call | solution.py:71
  111.8 4.5 convert_reduce_fusion
  116.3 8.9 %fusion.1 = bf16[32,32,16,256]{3,2,1,0:T(8,128)(2,1)} fusion(bf16[32,32,16,256]{3,2,1,0:T(8,128)(2,1)} %get-tuple-element.93, f32[16,256]{1,0:T(8,128)S(1)} %broadcast_multiply_fusion.1), kind=kLoop, calls=%fused_computation.3 | loop fusion | flops 16777216 | bytes 16793600 | tf_op jit(solution)/shard_map/convert_element_type | solution.py:244
  125.2 14.2 %fusion.4 = f32[1024,1024]{1,0:T(8,128)S(1)} fusion(bf16[1024,16,256]{2,1,0:T(8,128)(2,1)} %bitcast.438), kind=kOutput, calls=%fused_computation.12 | convolution fusion | flops 8589934592 | bytes 12582912 | tf_op jit(solution)/shard_map/dot_general | solution.py:246
  141.5 76.8 %shard_map.29 = f32[32,144,128]{2,1,0:T(8,128)} custom-call(f32[32,144,128]{2,1,0:T(8,128)} %bitcast.439), custom_call_target="tpu_custom_call" | custom-call | tf_op jit(solution)/shard_map/pallas_call | solution.py:173
  228.7 2.0 copy-done
  232.1 2.6 select_add_fusion
  234.6 1.9 copy-done.2
  236.6 11.7 %custom-call.20 = f32[128,128]{1,0:T(8,128)S(1)} custom-call(f32[128,128]{1,0:T(8,128)S(1)} %slice.676), custom_call_target="Cholesky" | custom-call | tf_op jit(solution)/shard_map/cholesky/custom-call.1 | solution.py:210
  249.7 9.8 %custom-call.21 = f32[1,128,128]{1,2,0:T(8,128)S(1)} custom-call(f32[1,128,128]{2,1,0:T(8,128)S(1)} %fusion.55), custom_call_target="InvertDiagBlocksLowerTriangular" | custom-call | tf_op jit(solution)/shard_map/triangular_solve/custom-call.0 | solution.py:211
  261.4 1.6 fusion.27
  263.7 5.0 %slice_add_fusion = f32[896,896]{1,0:T(8,128)S(1)} fusion(f32[1024,1024]{1,0:T(8,128)} %copy-done.2, f32[896,128]{1,0:T(8,128)S(1)} %fusion.27), kind=kOutput, calls=%fused_computation.10 | convolution fusion | flops 1234731008 | bytes 7340032 | tf_op jit(solution)/shard_map/dot_general | solution.py:217
  268.7 1.7 copy-done.4
  270.4 11.7 %custom-call.22 = f32[128,128]{1,0:T(8,128)S(1)} custom-call(f32[128,128]{1,0:T(8,128)S(1)} %slice.680), custom_call_target="Cholesky" | custom-call | tf_op jit(solution)/shard_map/cholesky/custom-call.1 | solution.py:210
  283.5 9.8 %custom-call.23 = f32[1,128,128]{1,2,0:T(8,128)S(1)} custom-call(f32[1,128,128]{2,1,0:T(8,128)S(1)} %fusion.56), custom_call_target="InvertDiagBlocksLowerTriangular" | custom-call | tf_op jit(solution)/shard_map/triangular_solve/custom-call.0 | solution.py:211
  295.8 3.7 slice_add_fusion.1
  299.5 11.9 %custom-call.24 = f32[128,128]{1,0:T(8,128)S(1)} custom-call(f32[128,128]{1,0:T(8,128)S(1)} %slice.684), custom_call_target="Cholesky" | custom-call | tf_op jit(solution)/shard_map/cholesky/custom-call.1 | solution.py:210
  312.8 9.8 %custom-call.25 = f32[1,128,128]{1,2,0:T(8,128)S(1)} custom-call(f32[1,128,128]{2,1,0:T(8,128)S(1)} %fusion.57), custom_call_target="InvertDiagBlocksLowerTriangular" | custom-call | tf_op jit(solution)/shard_map/triangular_solve/custom-call.0 | solution.py:211
  328.0 11.7 %custom-call.26 = f32[128,128]{1,0:T(8,128)S(1)} custom-call(f32[128,128]{1,0:T(8,128)S(1)} %slice.687), custom_call_target="Cholesky" | custom-call | tf_op jit(solution)/shard_map/cholesky/custom-call.1 | solution.py:210
  341.1 10.2 %custom-call.27 = f32[1,128,128]{1,2,0:T(8,128)S(1)} custom-call(f32[1,128,128]{2,1,0:T(8,128)S(1)} %fusion.58), custom_call_target="InvertDiagBlocksLowerTriangular" | custom-call | tf_op jit(solution)/shard_map/triangular_solve/custom-call.0 | solution.py:211
  354.8 2.2 fusion.7
  357.1 11.7 %custom-call.28 = f32[128,128]{1,0:T(8,128)S(1)} custom-call(f32[128,128]{1,0:T(8,128)S(1)} %slice.690), custom_call_target="Cholesky" | custom-call | tf_op jit(solution)/shard_map/cholesky/custom-call.1 | solution.py:210
  370.1 9.8 %custom-call.29 = f32[1,128,128]{1,2,0:T(8,128)S(1)} custom-call(f32[1,128,128]{2,1,0:T(8,128)S(1)} %fusion.59), custom_call_target="InvertDiagBlocksLowerTriangular" | custom-call | tf_op jit(solution)/shard_map/triangular_solve/custom-call.0 | solution.py:211
  382.4 11.9 %custom-call.30 = f32[128,128]{1,0:T(8,128)S(1)} custom-call(f32[128,128]{1,0:T(8,128)S(1)} %slice.693), custom_call_target="Cholesky" | custom-call | tf_op jit(solution)/shard_map/cholesky/custom-call.1 | solution.py:210
  395.6 9.8 %custom-call.31 = f32[1,128,128]{1,2,0:T(8,128)S(1)} custom-call(f32[1,128,128]{2,1,0:T(8,128)S(1)} %fusion.60), custom_call_target="InvertDiagBlocksLowerTriangular" | custom-call | tf_op jit(solution)/shard_map/triangular_solve/custom-call.0 | solution.py:211
  408.2 11.7 %custom-call.32 = f32[128,128]{1,0:T(8,128)S(1)} custom-call(f32[128,128]{1,0:T(8,128)S(1)} %slice.696), custom_call_target="Cholesky" | custom-call | tf_op jit(solution)/shard_map/cholesky/custom-call.1 | solution.py:210
  421.3 9.8 %custom-call.33 = f32[1,128,128]{1,2,0:T(8,128)S(1)} custom-call(f32[1,128,128]{2,1,0:T(8,128)S(1)} %fusion.61), custom_call_target="InvertDiagBlocksLowerTriangular" | custom-call | tf_op jit(solution)/shard_map/triangular_solve/custom-call.0 | solution.py:211
  432.4 11.9 %custom-call.34 = f32[128,128]{1,0:T(8,128)S(1)} custom-call(f32[128,128]{1,0:T(8,128)S(1)} %fusion.10), custom_call_target="Cholesky" | custom-call | tf_op jit(solution)/shard_map/cholesky/custom-call.1 | solution.py:210
  445.6 9.8 %custom-call.35 = f32[1,128,128]{1,2,0:T(8,128)S(1)} custom-call(f32[1,128,128]{2,1,0:T(8,128)S(1)} %fusion.62), custom_call_target="InvertDiagBlocksLowerTriangular" | custom-call | tf_op jit(solution)/shard_map/triangular_solve/custom-call.0 | solution.py:211
  463.4 4.4 fusion.124
  467.9 3.6 fusion.123
  474.5 5.5 %multiply_reduce_fusion = f32[16,256]{1,0:T(8,128)S(1)} fusion(f32[32,32]{1,0:T(8,128)S(1)} %concatenate.137, f32[16,256]{1,0:T(8,128)S(1)} %broadcast_multiply_fusion.1, bf16[32,32,16,256]{3,2,1,0:T(8,128)(2,1)} %get-tuple-element.93), kind=kLoop, calls=%fused_computation.4 | loop fusion | flops 29356032 | bytes 8425472 | tf_op jit(solution)/shard_map/reduce_sum | solution.py:251
  (265 shorter events, 53.7 us)
Async XLA Ops:
  140.0 1.4 copy-start.6
  218.3 9.9 %copy-start.3 = (f32[32,144,128]{2,1,0:T(8,128)S(1)}, f32[32,144,128]{2,1,0:T(8,128)}, u32[]{:S(2)}) copy-start(f32[32,144,128]{2,1,0:T(8,128)} %shard_map.29) | copy-start | bytes 7077892
  225.4 3.2 copy-start.12
  228.7 2.0 copy-start
  232.1 27.7 %copy-start.14 = (f32[32,1,32]{2,1,0:T(1,128)S(1)}, f32[32,1,32]{2,1,0:T(1,128)}, u32[]{:S(2)}) copy-start(f32[32,1,32]{2,1,0:T(1,128)} %get-tuple-element.94) | copy-start | bytes 12292
  234.6 2.0 copy-start.2
  259.8 9.0 %copy-start.11 = (f32[128,128]{1,0:T(8,128)}, f32[128,128]{1,0:T(8,128)S(1)}, u32[]{:S(2)}) copy-start(f32[128,128]{1,0:T(8,128)S(1)} %fusion.49) | copy-start | bytes 196612
  261.4 1.6 copy-start.20
  268.7 1.7 copy-start.4
  293.6 2.2 copy-start.7
  293.8 5.7 %copy-start.16 = (f32[1,128]{1,0:T(1,128)}, f32[1,128]{1,0:T(1,128)S(1)}, u32[]{:S(2)}) copy-start(f32[1,128]{1,0:T(1,128)S(1)} %fusion.112) | copy-start | bytes 1540
  295.8 27.1 %copy-start.15 = (f32[768]{0:T(1024)}, f32[768]{0:T(1024)S(1)}, u32[]{:S(2)}) copy-start(f32[768]{0:T(1024)S(1)} %slice_subtract_fusion.1) | copy-start | bytes 9220
  322.9 1.1 copy-start.9
  323.1 0.9 copy-start.19
  326.8 1.2 copy-start.5
  352.4 4.7 copy-start.17
  357.0 102.8 %copy-start.10 = (f32[128,128]{1,0:T(8,128)S(1)}, f32[128,128]{1,0:T(8,128)}, u32[]{:S(2)}) copy-start(f32[128,128]{1,0:T(8,128)} %copy-done.9) | copy-start | bytes 196612
  357.1 104.0 %copy-start.8 = (f32[128,128]{1,0:T(8,128)S(1)}, f32[128,128]{1,0:T(8,128)}, u32[]{:S(2)}) copy-start(f32[128,128]{1,0:T(8,128)} %copy-done.7) | copy-start | bytes 196612
  380.4 0.7 copy-start.18
  463.3 4.6 copy-start.1
  463.4 8.1 %copy-start.13 = (f32[8,128,128]{2,1,0:T(8,128)S(1)}, f32[8,128,128]{2,1,0:T(8,128)}, u32[]{:S(2)}) copy-start(f32[8,128,128]{2,1,0:T(8,128)} %copy-done.12) | copy-start | bytes 1572868

commit v17 on v12

--- a/solution.py
+++ b/solution.py
@@ -26,9 +26,7 @@
                             device_id_type=pl.DeviceIdType.MESH)
     pl.semaphore_wait(barrier, n - 1)
     local = pltpu.make_async_copy(piece(me), cols_ref.at[me], local_sems.at[0])
-    local.start()
     local_en = pltpu.make_async_copy(en_ref, en_all_ref.at[me], local_sems.at[1])
-    local_en.start()
     sends = []
     order = [i ^ (i // 2) for i in range(1, n)]
     for i in range(n - 1):
@@ -45,6 +43,8 @@
             device_id=dev, device_id_type=pl.DeviceIdType.MESH)
         e.start()
         sends.append((c, e))
+    local.start()
+    local_en.start()
     for k in range(1, n):
         s = jnp.bitwise_xor(me, k)
         dev = (s, col, slab)

time: 488 us -> 488 us (level)
  no operation moved by 1% of the time
where the time goes in v17:
time: 488 us; the launch traced here: 479 us
  other arithmetic  211 us (43%)
  Pallas kernels  187 us (38%)
  matrix products  57.3 us (12%)
  local copies, waits for them, and re-layouts  19.9 us (4%)
    pallas_call x1, Pallas kernels, exchange(): pl.pallas_call(functools.partial(exchange_kernel, n, width), out_shape=(j...  110 us
    another operation x24, other arithmetic, cholesky_solve(): lax.linalg.cholesky(a[lo:lo + block, lo:lo + block], symmetrize_input=False)  99.7 us
    another operation x16, other arithmetic, cholesky_solve(): inv = lax.linalg.triangular_solve(lkk, eye, left_side=True, lower=True)  84.1 us
    pallas_call x1, Pallas kernels, lower_psum(): pl.pallas_call(functools.partial(reduce_kernel, n, parts), out_shape=jax....  77.5 us
    unnamed x139, local copies, waits for them, and re-layouts  17.8 us
    dot_general x1, matrix products, shards(): jnp.dot(centered, centered.T, preferred_element_type=jnp.float32)  14.2 us
    dot_general x7, matrix products, cholesky_solve(): jnp.dot(panel, panel.T, precision=hi)  13.7 us

profile of v17, /device:TPU:8, one launch (start us, length us, event | category | flops | bytes accessed | tf_op | source)
XLA Modules:
  0.0 479.4 jit_solution(11413355865291017609)
XLA Ops:
  0.0 109.7 %shard_map.28 = (bf16[32,32,16,256]{3,2,1,0:T(8,128)(2,1)}, f32[32,1,32]{2,1,0:T(1,128)}) custom-call(bf16[32,16,8192]{2,1,0:T(8,128)(2,1)} %jac_ref.1, f32[1,32]{1,0:T(1,128)} %bitcast.454), custom_call_target="tpu_custom_call" | custom-call | tf_op jit(solution)/shard_map/pallas_call | solution.py:70
  109.7 4.5 convert_reduce_fusion
  114.2 8.9 %fusion.1 = bf16[32,32,16,256]{3,2,1,0:T(8,128)(2,1)} fusion(bf16[32,32,16,256]{3,2,1,0:T(8,128)(2,1)} %get-tuple-element.93, f32[16,256]{1,0:T(8,128)S(1)} %broadcast_multiply_fusion.1), kind=kLoop, calls=%fused_computation.3 | loop fusion | flops 16777216 | bytes 16793600 | tf_op jit(solution)/shard_map/convert_element_type | solution.py:243
  123.1 14.2 %fusion.4 = f32[1024,1024]{1,0:T(8,128)S(1)} fusion(bf16[1024,16,256]{2,1,0:T(8,128)(2,1)} %bitcast.438), kind=kOutput, calls=%fused_computation.12 | convolution fusion | flops 8589934592 | bytes 12582912 | tf_op jit(solution)/shard_map/dot_general | solution.py:245
  139.4 77.5 %shard_map.29 = f32[32,144,128]{2,1,0:T(8,128)} custom-call(f32[32,144,128]{2,1,0:T(8,128)} %bitcast.439), custom_call_target="tpu_custom_call" | custom-call | tf_op jit(solution)/shard_map/pallas_call | solution.py:172
  227.3 2.0 copy-done
  230.6 2.6 select_add_fusion
  233.2 1.9 copy-done.2
  235.2 11.7 %custom-call.20 = f32[128,128]{1,0:T(8,128)S(1)} custom-call(f32[128,128]{1,0:T(8,128)S(1)} %slice.676), custom_call_target="Cholesky" | custom-call | tf_op jit(solution)/shard_map/cholesky/custom-call.1 | solution.py:209
  248.2 9.8 %custom-call.21 = f32[1,128,128]{1,2,0:T(8,128)S(1)} custom-call(f32[1,128,128]{2,1,0:T(8,128)S(1)} %fusion.55), custom_call_target="InvertDiagBlocksLowerTriangular" | custom-call | tf_op jit(solution)/shard_map/triangular_solve/custom-call.0 | solution.py:210
  260.0 1.6 fusion.27
  262.3 5.0 %slice_add_fusion = f32[896,896]{1,0:T(8,128)S(1)} fusion(f32[1024,1024]{1,0:T(8,128)} %copy-done.2, f32[896,128]{1,0:T(8,128)S(1)} %fusion.27), kind=kOutput, calls=%fused_computation.10 | convolution fusion | flops 1234731008 | bytes 7340032 | tf_op jit(solution)/shard_map/dot_general | solution.py:216
  267.3 1.7 copy-done.4
  269.0 11.7 %custom-call.22 = f32[128,128]{1,0:T(8,128)S(1)} custom-call(f32[128,128]{1,0:T(8,128)S(1)} %slice.680), custom_call_target="Cholesky" | custom-call | tf_op jit(solution)/shard_map/cholesky/custom-call.1 | solution.py:209
  282.0 9.8 %custom-call.23 = f32[1,128,128]{1,2,0:T(8,128)S(1)} custom-call(f32[1,128,128]{2,1,0:T(8,128)S(1)} %fusion.56), custom_call_target="InvertDiagBlocksLowerTriangular" | custom-call | tf_op jit(solution)/shard_map/triangular_solve/custom-call.0 | solution.py:210
  294.4 3.7 slice_add_fusion.1
  298.1 11.9 %custom-call.24 = f32[128,128]{1,0:T(8,128)S(1)} custom-call(f32[128,128]{1,0:T(8,128)S(1)} %slice.684), custom_call_target="Cholesky" | custom-call | tf_op jit(solution)/shard_map/cholesky/custom-call.1 | solution.py:209
  311.3 9.8 %custom-call.25 = f32[1,128,128]{1,2,0:T(8,128)S(1)} custom-call(f32[1,128,128]{2,1,0:T(8,128)S(1)} %fusion.57), custom_call_target="InvertDiagBlocksLowerTriangular" | custom-call | tf_op jit(solution)/shard_map/triangular_solve/custom-call.0 | solution.py:210
  326.6 11.7 %custom-call.26 = f32[128,128]{1,0:T(8,128)S(1)} custom-call(f32[128,128]{1,0:T(8,128)S(1)} %slice.687), custom_call_target="Cholesky" | custom-call | tf_op jit(solution)/shard_map/cholesky/custom-call.1 | solution.py:209
  339.6 10.2 %custom-call.27 = f32[1,128,128]{1,2,0:T(8,128)S(1)} custom-call(f32[1,128,128]{2,1,0:T(8,128)S(1)} %fusion.58), custom_call_target="InvertDiagBlocksLowerTriangular" | custom-call | tf_op jit(solution)/shard_map/triangular_solve/custom-call.0 | solution.py:210
  353.4 2.2 fusion.7
  355.6 11.7 %custom-call.28 = f32[128,128]{1,0:T(8,128)S(1)} custom-call(f32[128,128]{1,0:T(8,128)S(1)} %slice.690), custom_call_target="Cholesky" | custom-call | tf_op jit(solution)/shard_map/cholesky/custom-call.1 | solution.py:209
  368.7 9.8 %custom-call.29 = f32[1,128,128]{1,2,0:T(8,128)S(1)} custom-call(f32[1,128,128]{2,1,0:T(8,128)S(1)} %fusion.59), custom_call_target="InvertDiagBlocksLowerTriangular" | custom-call | tf_op jit(solution)/shard_map/triangular_solve/custom-call.0 | solution.py:210
  381.0 11.9 %custom-call.30 = f32[128,128]{1,0:T(8,128)S(1)} custom-call(f32[128,128]{1,0:T(8,128)S(1)} %slice.693), custom_call_target="Cholesky" | custom-call | tf_op jit(solution)/shard_map/cholesky/custom-call.1 | solution.py:209
  394.2 9.8 %custom-call.31 = f32[1,128,128]{1,2,0:T(8,128)S(1)} custom-call(f32[1,128,128]{2,1,0:T(8,128)S(1)} %fusion.60), custom_call_target="InvertDiagBlocksLowerTriangular" | custom-call | tf_op jit(solution)/shard_map/triangular_solve/custom-call.0 | solution.py:210
  406.8 11.7 %custom-call.32 = f32[128,128]{1,0:T(8,128)S(1)} custom-call(f32[128,128]{1,0:T(8,128)S(1)} %slice.696), custom_call_target="Cholesky" | custom-call | tf_op jit(solution)/shard_map/cholesky/custom-call.1 | solution.py:209
  419.8 9.8 %custom-call.33 = f32[1,128,128]{1,2,0:T(8,128)S(1)} custom-call(f32[1,128,128]{2,1,0:T(8,128)S(1)} %fusion.61), custom_call_target="InvertDiagBlocksLowerTriangular" | custom-call | tf_op jit(solution)/shard_map/triangular_solve/custom-call.0 | solution.py:210
  430.9 11.9 %custom-call.34 = f32[128,128]{1,0:T(8,128)S(1)} custom-call(f32[128,128]{1,0:T(8,128)S(1)} %fusion.10), custom_call_target="Cholesky" | custom-call | tf_op jit(solution)/shard_map/cholesky/custom-call.1 | solution.py:209
  444.2 9.8 %custom-call.35 = f32[1,128,128]{1,2,0:T(8,128)S(1)} custom-call(f32[1,128,128]{2,1,0:T(8,128)S(1)} %fusion.62), custom_call_target="InvertDiagBlocksLowerTriangular" | custom-call | tf_op jit(solution)/shard_map/triangular_solve/custom-call.0 | solution.py:210
  462.0 4.4 fusion.124
  466.4 3.6 fusion.123
  473.1 5.5 %multiply_reduce_fusion = f32[16,256]{1,0:T(8,128)S(1)} fusion(f32[32,32]{1,0:T(8,128)S(1)} %concatenate.137, f32[16,256]{1,0:T(8,128)S(1)} %broadcast_multiply_fusion.1, bf16[32,32,16,256]{3,2,1,0:T(8,128)(2,1)} %get-tuple-element.93), kind=kLoop, calls=%fused_computation.4 | loop fusion | flops 29356032 | bytes 8425472 | tf_op jit(solution)/shard_map/reduce_sum | solution.py:250
  (265 shorter events, 53.7 us)
Async XLA Ops:
  137.9 1.4 copy-start.6
  216.9 9.9 %copy-start.3 = (f32[32,144,128]{2,1,0:T(8,128)S(1)}, f32[32,144,128]{2,1,0:T(8,128)}, u32[]{:S(2)}) copy-start(f32[32,144,128]{2,1,0:T(8,128)} %shard_map.29) | copy-start | bytes 7077892
  224.0 3.2 copy-start.12
  227.3 2.0 copy-start
  230.6 27.7 %copy-start.14 = (f32[32,1,32]{2,1,0:T(1,128)S(1)}, f32[32,1,32]{2,1,0:T(1,128)}, u32[]{:S(2)}) copy-start(f32[32,1,32]{2,1,0:T(1,128)} %get-tuple-element.94) | copy-start | bytes 12292
  233.2 2.0 copy-start.2
  258.3 9.0 %copy-start.11 = (f32[128,128]{1,0:T(8,128)}, f32[128,128]{1,0:T(8,128)S(1)}, u32[]{:S(2)}) copy-start(f32[128,128]{1,0:T(8,128)S(1)} %fusion.49) | copy-start | bytes 196612
  260.0 1.6 copy-start.20
  267.3 1.7 copy-start.4
  292.2 2.2 copy-start.7
  292.3 5.7 %copy-start.16 = (f32[1,128]{1,0:T(1,128)}, f32[1,128]{1,0:T(1,128)S(1)}, u32[]{:S(2)}) copy-start(f32[1,128]{1,0:T(1,128)S(1)} %fusion.112) | copy-start | bytes 1540
  294.4 27.1 %copy-start.15 = (f32[768]{0:T(1024)}, f32[768]{0:T(1024)S(1)}, u32[]{:S(2)}) copy-start(f32[768]{0:T(1024)S(1)} %slice_subtract_fusion.1) | copy-start | bytes 9220
  321.5 1.1 copy-start.9
  321.6 0.9 copy-start.19
  325.3 1.2 copy-start.5
  350.9 4.7 copy-start.17
  355.6 102.8 %copy-start.10 = (f32[128,128]{1,0:T(8,128)S(1)}, f32[128,128]{1,0:T(8,128)}, u32[]{:S(2)}) copy-start(f32[128,128]{1,0:T(8,128)} %copy-done.9) | copy-start | bytes 196612
  355.6 104.0 %copy-start.8 = (f32[128,128]{1,0:T(8,128)S(1)}, f32[128,128]{1,0:T(8,128)}, u32[]{:S(2)}) copy-start(f32[128,128]{1,0:T(8,128)} %copy-done.7) | copy-start | bytes 196612
  379.0 0.7 copy-start.18
  461.9 4.6 copy-start.1
  462.0 8.1 %copy-start.13 = (f32[8,128,128]{2,1,0:T(8,128)S(1)}, f32[8,128,128]{2,1,0:T(8,128)}, u32[]{:S(2)}) copy-start(f32[8,128,128]{2,1,0:T(8,128)} %copy-done.12) | copy-start | bytes 1572868

commit v18 on v12

--- a/solution.py
+++ b/solution.py
@@ -115,12 +115,14 @@
             recv_sem=rs_recv.at[me], device_id=(t, col, slab), device_id_type=mesh_id)
         c.start()
         sends.append(c)
-    rs_buf[pl.ds(me, 1)] = p_ref[pl.ds(me, 1)]
+    own = pltpu.make_async_copy(p_ref.at[me], rs_buf.at[me], local_sem.at[1])
+    own.start()
     for k in range(1, n):
         s = jnp.bitwise_xor(me, k)
         pltpu.make_async_remote_copy(
             src_ref=p_ref.at[s], dst_ref=rs_buf.at[s], send_sem=rs_send.at[s],
             recv_sem=rs_recv.at[s], device_id=(s, col, slab), device_id_type=mesh_id).wait_recv()
+    own.wait()
     total = rs_buf[0]
     for s in range(1, n):
         total = total + rs_buf[s]
@@ -172,7 +174,7 @@
     reduced = pl.pallas_call(
         functools.partial(reduce_kernel, n, parts),
         out_shape=jax.ShapeDtypeStruct((n, rows, block), jnp.float32),
-        in_specs=[pl.BlockSpec(memory_space=pltpu.VMEM)],
+        in_specs=[pl.BlockSpec(memory_space=pl.ANY)],
         out_specs=pl.BlockSpec(memory_space=pl.ANY),
         scratch_shapes=[
             pltpu.VMEM((n, rows, block), jnp.float32),
@@ -184,7 +186,7 @@
             pltpu.SemaphoreType.DMA((parts,)),
             pltpu.SemaphoreType.DMA((n,)),
             pltpu.SemaphoreType.DMA((n,)),
-            pltpu.SemaphoreType.DMA((1,)),
+            pltpu.SemaphoreType.DMA((2,)),
         ],
         compiler_params=pltpu.CompilerParams(collective_id=1, has_side_effects=True),
     )(packed)

time: 488 us -> 486 us (level)
  no operation moved by 1% of the time
where the time goes in v18:
time: 486 us; the launch traced here: 478 us
  other arithmetic  211 us (43%)
  Pallas kernels  186 us (38%)
  matrix products  57.1 us (12%)
  local copies, waits for them, and re-layouts  19.9 us (4%)
    pallas_call x1, Pallas kernels, exchange(): pl.pallas_call(functools.partial(exchange_kernel, n, width), out_shape=(j...  110 us
    another operation x24, other arithmetic, cholesky_solve(): lax.linalg.cholesky(a[lo:lo + block, lo:lo + block], symmetrize_input=False)  100 us
    another operation x16, other arithmetic, cholesky_solve(): inv = lax.linalg.triangular_solve(lkk, eye, left_side=True, lower=True)  83.8 us
    pallas_call x1, Pallas kernels, lower_psum(): pl.pallas_call(functools.partial(reduce_kernel, n, parts), out_shape=jax....  76.1 us
    unnamed x139, local copies, waits for them, and re-layouts  17.8 us
    dot_general x1, matrix products, shards(): jnp.dot(centered, centered.T, preferred_element_type=jnp.float32)  13.9 us
    dot_general x7, matrix products, cholesky_solve(): jnp.dot(panel, panel.T, precision=hi)  13.8 us

profile of v18, /device:TPU:8, one launch (start us, length us, event | category | flops | bytes accessed | tf_op | source)
XLA Modules:
  0.0 477.9 jit_solution(14700519578461834253)
XLA Ops:
  0.0 109.8 %shard_map.28 = (bf16[32,32,16,256]{3,2,1,0:T(8,128)(2,1)}, f32[32,1,32]{2,1,0:T(1,128)}) custom-call(bf16[32,16,8192]{2,1,0:T(8,128)(2,1)} %jac_ref.1, f32[1,32]{1,0:T(1,128)} %bitcast.454), custom_call_target="tpu_custom_call" | custom-call | tf_op jit(solution)/shard_map/pallas_call | solution.py:70
  109.8 4.5 convert_reduce_fusion
  114.3 8.9 %fusion.1 = bf16[32,32,16,256]{3,2,1,0:T(8,128)(2,1)} fusion(bf16[32,32,16,256]{3,2,1,0:T(8,128)(2,1)} %get-tuple-element.93, f32[16,256]{1,0:T(8,128)S(1)} %broadcast_multiply_fusion.1), kind=kLoop, calls=%fused_computation.3 | loop fusion | flops 16777216 | bytes 16793600 | tf_op jit(solution)/shard_map/convert_element_type | solution.py:245
  123.2 13.9 %fusion.4 = f32[1024,1024]{1,0:T(8,128)S(1)} fusion(bf16[1024,16,256]{2,1,0:T(8,128)(2,1)} %bitcast.438), kind=kOutput, calls=%fused_computation.12 | convolution fusion | flops 8589934592 | bytes 12582912 | tf_op jit(solution)/shard_map/dot_general | solution.py:247
  139.2 76.1 %shard_map.29 = f32[32,144,128]{2,1,0:T(8,128)} custom-call(f32[32,144,128]{2,1,0:T(8,128)} %bitcast.439), custom_call_target="tpu_custom_call" | custom-call | tf_op jit(solution)/shard_map/pallas_call | solution.py:174
  225.7 2.0 copy-done
  229.0 2.6 select_add_fusion
  231.6 1.9 copy-done.2
  233.6 11.7 %custom-call.20 = f32[128,128]{1,0:T(8,128)S(1)} custom-call(f32[128,128]{1,0:T(8,128)S(1)} %slice.676), custom_call_target="Cholesky" | custom-call | tf_op jit(solution)/shard_map/cholesky/custom-call.1 | solution.py:211
  246.6 9.8 %custom-call.21 = f32[1,128,128]{1,2,0:T(8,128)S(1)} custom-call(f32[1,128,128]{2,1,0:T(8,128)S(1)} %fusion.55), custom_call_target="InvertDiagBlocksLowerTriangular" | custom-call | tf_op jit(solution)/shard_map/triangular_solve/custom-call.0 | solution.py:212
  258.4 1.6 fusion.27
  260.7 5.1 %slice_add_fusion = f32[896,896]{1,0:T(8,128)S(1)} fusion(f32[1024,1024]{1,0:T(8,128)} %copy-done.2, f32[896,128]{1,0:T(8,128)S(1)} %fusion.27), kind=kOutput, calls=%fused_computation.10 | convolution fusion | flops 1234731008 | bytes 7340032 | tf_op jit(solution)/shard_map/dot_general | solution.py:218
  265.8 1.7 copy-done.4
  267.4 11.7 %custom-call.22 = f32[128,128]{1,0:T(8,128)S(1)} custom-call(f32[128,128]{1,0:T(8,128)S(1)} %slice.680), custom_call_target="Cholesky" | custom-call | tf_op jit(solution)/shard_map/cholesky/custom-call.1 | solution.py:211
  280.5 9.8 %custom-call.23 = f32[1,128,128]{1,2,0:T(8,128)S(1)} custom-call(f32[1,128,128]{2,1,0:T(8,128)S(1)} %fusion.56), custom_call_target="InvertDiagBlocksLowerTriangular" | custom-call | tf_op jit(solution)/shard_map/triangular_solve/custom-call.0 | solution.py:212
  292.8 3.7 slice_add_fusion.1
  296.5 12.1 %custom-call.24 = f32[128,128]{1,0:T(8,128)S(1)} custom-call(f32[128,128]{1,0:T(8,128)S(1)} %slice.684), custom_call_target="Cholesky" | custom-call | tf_op jit(solution)/shard_map/cholesky/custom-call.1 | solution.py:211
  310.0 9.8 %custom-call.25 = f32[1,128,128]{1,2,0:T(8,128)S(1)} custom-call(f32[1,128,128]{2,1,0:T(8,128)S(1)} %fusion.57), custom_call_target="InvertDiagBlocksLowerTriangular" | custom-call | tf_op jit(solution)/shard_map/triangular_solve/custom-call.0 | solution.py:212
  325.2 11.7 %custom-call.26 = f32[128,128]{1,0:T(8,128)S(1)} custom-call(f32[128,128]{1,0:T(8,128)S(1)} %slice.687), custom_call_target="Cholesky" | custom-call | tf_op jit(solution)/shard_map/cholesky/custom-call.1 | solution.py:211
  338.3 9.9 %custom-call.27 = f32[1,128,128]{1,2,0:T(8,128)S(1)} custom-call(f32[1,128,128]{2,1,0:T(8,128)S(1)} %fusion.58), custom_call_target="InvertDiagBlocksLowerTriangular" | custom-call | tf_op jit(solution)/shard_map/triangular_solve/custom-call.0 | solution.py:212
  351.8 2.2 fusion.7
  354.0 11.7 %custom-call.28 = f32[128,128]{1,0:T(8,128)S(1)} custom-call(f32[128,128]{1,0:T(8,128)S(1)} %slice.690), custom_call_target="Cholesky" | custom-call | tf_op jit(solution)/shard_map/cholesky/custom-call.1 | solution.py:211
  367.1 9.8 %custom-call.29 = f32[1,128,128]{1,2,0:T(8,128)S(1)} custom-call(f32[1,128,128]{2,1,0:T(8,128)S(1)} %fusion.59), custom_call_target="InvertDiagBlocksLowerTriangular" | custom-call | tf_op jit(solution)/shard_map/triangular_solve/custom-call.0 | solution.py:212
  379.4 12.1 %custom-call.30 = f32[128,128]{1,0:T(8,128)S(1)} custom-call(f32[128,128]{1,0:T(8,128)S(1)} %slice.693), custom_call_target="Cholesky" | custom-call | tf_op jit(solution)/shard_map/cholesky/custom-call.1 | solution.py:211
  392.8 9.8 %custom-call.31 = f32[1,128,128]{1,2,0:T(8,128)S(1)} custom-call(f32[1,128,128]{2,1,0:T(8,128)S(1)} %fusion.60), custom_call_target="InvertDiagBlocksLowerTriangular" | custom-call | tf_op jit(solution)/shard_map/triangular_solve/custom-call.0 | solution.py:212
  405.4 11.7 %custom-call.32 = f32[128,128]{1,0:T(8,128)S(1)} custom-call(f32[128,128]{1,0:T(8,128)S(1)} %slice.696), custom_call_target="Cholesky" | custom-call | tf_op jit(solution)/shard_map/cholesky/custom-call.1 | solution.py:211
  418.5 9.8 %custom-call.33 = f32[1,128,128]{1,2,0:T(8,128)S(1)} custom-call(f32[1,128,128]{2,1,0:T(8,128)S(1)} %fusion.61), custom_call_target="InvertDiagBlocksLowerTriangular" | custom-call | tf_op jit(solution)/shard_map/triangular_solve/custom-call.0 | solution.py:212
  429.6 11.9 %custom-call.34 = f32[128,128]{1,0:T(8,128)S(1)} custom-call(f32[128,128]{1,0:T(8,128)S(1)} %fusion.10), custom_call_target="Cholesky" | custom-call | tf_op jit(solution)/shard_map/cholesky/custom-call.1 | solution.py:211
  442.8 9.8 %custom-call.35 = f32[1,128,128]{1,2,0:T(8,128)S(1)} custom-call(f32[1,128,128]{2,1,0:T(8,128)S(1)} %fusion.62), custom_call_target="InvertDiagBlocksLowerTriangular" | custom-call | tf_op jit(solution)/shard_map/triangular_solve/custom-call.0 | solution.py:212
  460.6 4.4 fusion.124
  465.0 3.6 fusion.123
  471.6 5.5 %multiply_reduce_fusion = f32[16,256]{1,0:T(8,128)S(1)} fusion(f32[32,32]{1,0:T(8,128)S(1)} %concatenate.137, f32[16,256]{1,0:T(8,128)S(1)} %broadcast_multiply_fusion.1, bf16[32,32,16,256]{3,2,1,0:T(8,128)(2,1)} %get-tuple-element.93), kind=kLoop, calls=%fused_computation.4 | loop fusion | flops 29356032 | bytes 8425472 | tf_op jit(solution)/shard_map/reduce_sum | solution.py:252
  (265 shorter events, 53.7 us)
Async XLA Ops:
  137.8 1.4 copy-start.6
  215.3 9.9 %copy-start.3 = (f32[32,144,128]{2,1,0:T(8,128)S(1)}, f32[32,144,128]{2,1,0:T(8,128)}, u32[]{:S(2)}) copy-start(f32[32,144,128]{2,1,0:T(8,128)} %shard_map.29) | copy-start | bytes 7077892
  222.4 3.2 copy-start.12
  225.7 2.0 copy-start
  229.0 27.7 %copy-start.14 = (f32[32,1,32]{2,1,0:T(1,128)S(1)}, f32[32,1,32]{2,1,0:T(1,128)}, u32[]{:S(2)}) copy-start(f32[32,1,32]{2,1,0:T(1,128)} %get-tuple-element.94) | copy-start | bytes 12292
  231.6 2.0 copy-start.2
  256.7 9.0 %copy-start.11 = (f32[128,128]{1,0:T(8,128)}, f32[128,128]{1,0:T(8,128)S(1)}, u32[]{:S(2)}) copy-start(f32[128,128]{1,0:T(8,128)S(1)} %fusion.49) | copy-start | bytes 196612
  258.4 1.6 copy-start.20
  265.7 1.7 copy-start.4
  290.6 2.2 copy-start.7
  290.8 5.7 %copy-start.16 = (f32[1,128]{1,0:T(1,128)}, f32[1,128]{1,0:T(1,128)S(1)}, u32[]{:S(2)}) copy-start(f32[1,128]{1,0:T(1,128)S(1)} %fusion.112) | copy-start | bytes 1540
  292.8 27.3 %copy-start.15 = (f32[768]{0:T(1024)}, f32[768]{0:T(1024)S(1)}, u32[]{:S(2)}) copy-start(f32[768]{0:T(1024)S(1)} %slice_subtract_fusion.1) | copy-start | bytes 9220
  320.1 1.1 copy-start.9
  320.3 0.9 copy-start.19
  324.0 1.2 copy-start.5
  349.3 4.7 copy-start.17
  354.0 103.0 %copy-start.10 = (f32[128,128]{1,0:T(8,128)S(1)}, f32[128,128]{1,0:T(8,128)}, u32[]{:S(2)}) copy-start(f32[128,128]{1,0:T(8,128)} %copy-done.9) | copy-start | bytes 196612
  354.0 104.1 %copy-start.8 = (f32[128,128]{1,0:T(8,128)S(1)}, f32[128,128]{1,0:T(8,128)}, u32[]{:S(2)}) copy-start(f32[128,128]{1,0:T(8,128)} %copy-done.7) | copy-start | bytes 196612
  377.4 0.7 copy-start.18
  460.5 4.6 copy-start.1
  460.6 8.1 %copy-start.13 = (f32[8,128,128]{2,1,0:T(8,128)S(1)}, f32[8,128,128]{2,1,0:T(8,128)}, u32[]{:S(2)}) copy-start(f32[8,128,128]{2,1,0:T(8,128)} %copy-done.12) | copy-start | bytes 1572868
